TPU v7x, 128 devices: a whole 4x4x4 slice. The times are simulated.
128 devices in a mesh: dp: 4 (over z_hi, core), tm: 32 (over z_lo, x, y).
Axes of the slice: x: 4, y: 4, z: 4 (z_hi: 2, z_lo: 2; z = z_hi * 2 + z_lo), core: 2. Of those that a mesh axis runs over, the one named last changes fastest.
Arguments:
- tokens: bfloat16 [4, 32, 512, 768], P('dp', 'tm'), may hold values from -60 to 60
- qkv_weight: bfloat16 [768, 2304], replicated, may hold values from -0.21875 to 0.21875
- pool_kernel: float32 [2, 27, 64], replicated, may hold values from -1.25 to 1.25
- norm_gain: float32 [2, 64], replicated, may hold values from 0.1 to 1.9
- out_weight: bfloat16 [768, 768], replicated, may hold values from -0.21875 to 0.21875
- out_cotangent: bfloat16 [4, 32, 512, 768], P('dp', 'tm'), may hold values from -6 to 6
Outputs:
- block_out: bfloat16 [4, 32, 512, 768], P('dp', 'tm')
- grad_tokens: bfloat16 [4, 32, 512, 768], P('dp', 'tm')
- grad_qkv_weight: float32 [768, 2304], P('tm')
- grad_out_weight: float32 [768, 768], P('tm')
- grad_kernel: float32 [2, 27, 64], replicated
- grad_gain: float32 [2, 64], replicated
All inputs are finite; a program needn't handle non-finite values.
Results may differ from a plain program's by a relative error of at most 0.0055.
The roundings to bfloat16 on the way count: a program that leaves them out, or rounds other values in their place, can miss the bound.
Values may be sent and summed in bfloat16 or wider, within the bound.
No kernel may reach another device: no remote copies, remote signals or barrier semaphores. Data moves between devices by JAX's collectives and lax.ppermute only.
A program may use at most 128 MiB of HBM per device.

v0:
```python
from functools import partial

import jax
import jax.numpy as jnp
from jax import lax
from jax.sharding import Mesh
from jax.sharding import PartitionSpec as P

HEADS = 12
GRID_H = 32
TM = ("tm_0", "tm_1", "tm_2")
DP = ("dp_0", "dp_1")
DP_TM = ("dp_0", "dp_1", "tm_0", "tm_1", "tm_2")


EPSILON = 1e-05
pair_heads = 2


def shifted_2(value, axis, steps):
    count = lax.axis_size(axis)
    first, last = (max(0, -steps), min(count, count - steps))
    return lax.ppermute(value, axis, [(source, source + steps) for source in range(first, last)])


def extended(array, sides, width):
    for axis, dim in sides:
        size, length = (lax.axis_size(axis), array.shape[dim])
        up = [(i, (i + 1) % size) for i in range(size - 1)]
        down = [(j, i) for i, j in up]
        last = lax.slice_in_dim(array, length - width, length, axis=dim)
        first = lax.slice_in_dim(array, 0, width, axis=dim)
        before = lax.ppermute(last, axis, up)
        after = lax.ppermute(first, axis, down)
        array = jnp.concatenate([before, array, after], axis=dim)
    return array


def in_one_piece(arrays, axis, dim, along):
    widths = [a.shape[along] for a in arrays]
    both = jnp.concatenate(arrays, axis=along)
    filled = lax.psum_scatter(both, axis, scatter_dimension=dim, tiled=True)
    return tuple(jnp.split(filled, [sum(widths[:k]) for k in range(1, len(widths))], axis=along))


def from_everyone(array, axis):
    copies = jnp.broadcast_to(array, (lax.axis_size(axis), *array.shape))
    return lax.all_to_all(copies, axis, split_axis=0, concat_axis=0, tiled=True)


def taken_together(array, axis):
    return from_everyone(array, axis).sum(axis=0)


def together(arrays, axis):
    line, at, outs = (jnp.concatenate([a.reshape(-1) for a in arrays]), 0, [])
    total = taken_together(line, axis)
    for a in arrays:
        outs.append(total[at : at + a.size].reshape(a.shape))
        at += a.size
    return tuple(outs)


def by_axis(array, axes):
    for axis in axes:
        array = lax.psum(array, axis)
    return array


def tap_table(kernel, head_count):
    tiled = jnp.tile(kernel, (1, 1, head_count))
    return jnp.transpose(tiled, (1, 0, 2)).reshape(3, 3, 3, -1)


def cut_blocks(volume):
    lead_dims = volume.ndim - 3
    extent = volume.shape
    padded = jnp.pad(volume, [(0, 0)] * lead_dims + [(1, 3), (1, 3), (0, 0)])
    pooled_h = extent[-3] // 4
    pooled_w = extent[-2] // 4
    tiled_view = padded.reshape(extent[:-3] + (pooled_h + 1, 4, pooled_w + 1, 4, extent[-1]))
    return tiled_view[..., :pooled_h, :3, :pooled_w, :3, :]


def spatial_sums(blocks, kernel_taps):
    widened = blocks.astype(jnp.float32)
    results = []
    for offset_t in range(3):
        running = None
        for offset_h in range(3):
            for offset_w in range(3):
                product_term = (
                    widened[..., offset_h, :, offset_w, :]
                    * kernel_taps[offset_t, offset_h, offset_w]
                )
                running = product_term if running is None else running + product_term
        results.append(running)
    return results


def spread_taps(shifted, kernel_taps, height, breadth):
    running = None
    for offset_t in range(3):
        product_term = (
            shifted[offset_t][..., :, None, :, None, :] * kernel_taps[offset_t][:, None, :, :]
        )
        running = product_term if running is None else running + product_term
    lead_dims = running.ndim - 5
    padded = jnp.pad(running, [(0, 0)] * lead_dims + [(0, 1)] * 4 + [(0, 0)])
    extent = padded.shape
    volume = padded.reshape(
        extent[:lead_dims] + (extent[lead_dims] * 4, extent[lead_dims + 2] * 4, extent[-1])
    )
    return volume[..., 1 : height + 1, 1 : breadth + 1, :]


def tap_grads(shifted, blocks, head_count):
    widened = blocks.astype(jnp.float32)
    per_offset = [
        jnp.einsum(
            "cfijd,cfibjed->bed", shifted[offset_t], widened, precision=lax.Precision.HIGHEST
        )
        for offset_t in range(3)
    ]
    stacked = jnp.stack(per_offset).reshape(27, 2, head_count, -1)
    return jnp.transpose(jnp.sum(stacked, axis=2), (1, 0, 2))


def pooled_norm(summed, gain, head_count):
    grouped_view = summed.reshape(summed.shape[:-1] + (2, head_count, -1))
    centred = grouped_view - jnp.mean(grouped_view, axis=-1, keepdims=True)
    inv_std = lax.rsqrt(jnp.mean(centred * centred, axis=-1, keepdims=True) + EPSILON)
    normed = centred * inv_std
    pooled = (normed * gain[:, None, :]).reshape(summed.shape).astype(jnp.bfloat16)
    return (pooled, normed, inv_std)


def split_heads(tensor):
    extent = tensor.shape
    paired = tensor.reshape(extent[:2] + (extent[2] // pair_heads, pair_heads) + extent[3:])
    return jnp.moveaxis(paired, 2, 0)


def join_heads(tensor):
    moved = jnp.moveaxis(tensor, 0, 2)
    extent = moved.shape
    return moved.reshape(extent[:2] + (extent[2] * extent[3],) + extent[4:])


def by_pairs(function, tensors):
    results = lax.map(
        lambda members: function(*members), tuple((split_heads(element) for element in tensors))
    )
    return tuple((join_heads(element) for element in results))


def group_forward(queries, keys_part, values_part, softmax_scale):
    scores = (
        jnp.einsum("crgd,ckgd->crgk", queries, keys_part, preferred_element_type=jnp.float32)
        * softmax_scale
    )
    row_max = jnp.max(scores, axis=-1)
    weights = jnp.exp(scores - row_max[..., None])
    row_total = jnp.sum(weights, axis=-1)
    weighted = jnp.einsum(
        "crgk,ckgd->crgd",
        weights.astype(jnp.bfloat16),
        values_part,
        preferred_element_type=jnp.float32,
    )
    return (row_max, row_total, weighted)


def group_backward(
    queries, keys_part, values_part, row_max, row_total, attended, d_mixed, softmax_scale
):
    scores = (
        jnp.einsum("crgd,ckgd->crgk", queries, keys_part, preferred_element_type=jnp.float32)
        * softmax_scale
    )
    weights = jnp.exp(scores - row_max[..., None])
    probability = weights / row_total[..., None]
    d_widened = d_mixed.astype(jnp.float32)
    scaled_grad = (d_widened / row_total[..., None]).astype(jnp.bfloat16)
    d_values = jnp.einsum(
        "crgk,crgd->ckgd",
        weights.astype(jnp.bfloat16),
        scaled_grad,
        preferred_element_type=jnp.float32,
    )
    d_probs = jnp.einsum(
        "crgd,ckgd->crgk", d_mixed, values_part, preferred_element_type=jnp.float32
    )
    row_delta = jnp.sum(d_widened * attended, axis=-1)
    d_scores = (probability * (d_probs - row_delta[..., None])).astype(jnp.bfloat16)
    d_queries = (
        jnp.einsum("crgk,ckgd->crgd", d_scores, keys_part, preferred_element_type=jnp.float32)
        * softmax_scale
        + d_widened
    )
    d_keys = (
        jnp.einsum("crgk,crgd->ckgd", d_scores, queries, preferred_element_type=jnp.float32)
        * softmax_scale
    )
    return (d_queries, d_keys, d_values)


def shards(tokens, qkv_weight, pool_kernel, norm_gain, out_weight, out_cotangent):
    clip_count, frame_count, cell_count, model_width = tokens.shape
    head_count = HEADS
    head_size = model_width // head_count
    softmax_scale = head_size ** (-0.5)
    query_rows = frame_count * cell_count
    breadth = cell_count // GRID_H
    token_rows = tokens.reshape(-1, model_width)
    projected = jnp.dot(token_rows, qkv_weight, preferred_element_type=jnp.float32).astype(
        jnp.bfloat16
    )
    projected = projected.reshape(clip_count, frame_count, cell_count, 3 * model_width)
    queries = projected[..., :model_width].reshape(clip_count, query_rows, head_count, head_size)
    volume = projected[..., model_width:].reshape(
        clip_count, frame_count, GRID_H, breadth, 2 * model_width
    )
    kernel_taps = tap_table(pool_kernel, head_count)
    own_blocks = cut_blocks(volume)
    partials = spatial_sums(own_blocks, kernel_taps)
    from_lower = shifted_2(partials[0], TM, 1)
    from_upper = shifted_2(partials[2], TM, -1)
    pooled_sum = (
        jnp.concatenate([from_lower, partials[0][:, : frame_count - 1]], axis=1)
        + partials[1]
        + jnp.concatenate([partials[2][:, 1:], from_upper], axis=1)
    )
    pooled, normed, inv_std = pooled_norm(pooled_sum, norm_gain, head_count)
    pooled = pooled.reshape(clip_count, -1, 2 * model_width)
    gathered = lax.all_gather(pooled, TM, axis=1, tiled=True)
    keys_part = gathered[..., :model_width].reshape(clip_count, -1, head_count, head_size)
    values_part = gathered[..., model_width:].reshape(clip_count, -1, head_count, head_size)
    row_max, row_total, weighted = by_pairs(
        partial(group_forward, softmax_scale=softmax_scale), (queries, keys_part, values_part)
    )
    attended = weighted / row_total[..., None]
    mixed = (attended + queries.astype(jnp.float32)).astype(jnp.bfloat16)
    mixed_rows = mixed.reshape(-1, model_width)
    block_out = (
        jnp.dot(mixed_rows, out_weight, preferred_element_type=jnp.float32)
        .astype(jnp.bfloat16)
        .reshape(tokens.shape)
    )
    cotangent_rows = out_cotangent.reshape(-1, model_width)
    d_mixed = jnp.einsum(
        "re,de->rd", cotangent_rows, out_weight, preferred_element_type=jnp.float32
    ).astype(jnp.bfloat16)
    d_mixed = d_mixed.reshape(clip_count, query_rows, head_count, head_size)
    out_local = jnp.einsum(
        "rd,re->de", mixed_rows, cotangent_rows, preferred_element_type=jnp.float32
    )
    keys_all = gathered[..., :model_width].reshape(clip_count, -1, head_count, head_size)
    values_all = gathered[..., model_width:].reshape(clip_count, -1, head_count, head_size)
    d_queries, d_keys, d_values = by_pairs(
        partial(group_backward, softmax_scale=softmax_scale),
        (queries, keys_all, values_all, row_max, row_total, attended, d_mixed),
    )
    d_pooled_all = jnp.concatenate(
        [
            d_keys.reshape(clip_count, -1, model_width),
            d_values.reshape(clip_count, -1, model_width),
        ],
        axis=-1,
    )
    d_pooled = lax.psum_scatter(d_pooled_all, TM, scatter_dimension=1, tiled=True)
    d_grouped = d_pooled.reshape(normed.shape)
    sum_axes = tuple(range(normed.ndim - 3)) + (normed.ndim - 2,)
    gain_local = jnp.sum(d_grouped * normed, axis=sum_axes)
    d_normed = d_grouped * norm_gain[:, None, :]
    d_summed = inv_std * (
        d_normed
        - jnp.mean(d_normed, axis=-1, keepdims=True)
        - normed * jnp.mean(d_normed * normed, axis=-1, keepdims=True)
    )
    d_summed = d_summed.reshape(pooled_sum.shape)
    rims = extended(d_summed, ((TM, 1),), 1)
    shifted = [rims[:, 2:], rims[:, 1 : frame_count + 1], rims[:, :frame_count]]
    d_volume = spread_taps(shifted, kernel_taps, GRID_H, breadth)
    kernel_local = tap_grads(shifted, own_blocks, head_count)
    d_projected = jnp.concatenate(
        [
            d_queries.reshape(clip_count, frame_count, cell_count, model_width),
            d_volume.reshape(clip_count, frame_count, cell_count, 2 * model_width),
        ],
        axis=-1,
    )
    d_projected = d_projected.astype(jnp.bfloat16).reshape(-1, 3 * model_width)
    grad_tokens = (
        jnp.einsum("re,de->rd", d_projected, qkv_weight, preferred_element_type=jnp.float32)
        .astype(jnp.bfloat16)
        .reshape(tokens.shape)
    )
    qkv_local = jnp.einsum("rd,re->de", token_rows, d_projected, preferred_element_type=jnp.float32)
    norm_scale = float(
        clip_count * frame_count * cell_count * lax.axis_size(DP) * lax.axis_size(TM)
    ) ** (-0.5)
    partial_qkv, partial_out = in_one_piece((qkv_local, out_local), TM, 0, 1)
    shard_qkv, shard_out = together((partial_qkv, partial_out), DP)
    kernel_total, gain_total = (by_axis(kernel_local, DP_TM), by_axis(gain_local, DP_TM))
    return (
        block_out,
        grad_tokens,
        shard_qkv * norm_scale,
        shard_out * norm_scale,
        kernel_total * norm_scale,
        gain_total * norm_scale,
    )


def solution(mesh):
    torus = Mesh(mesh.devices.reshape(2, 2, 2, 4, 4), ("dp_0", "dp_1", "tm_0", "tm_1", "tm_2"))
    placed = (P(DP, TM, None, None), P(), P(), P(), P(), P(DP, TM, None, None))
    return jax.shard_map(
        shards,
        mesh=torus,
        in_specs=placed,
        out_specs=(
            P(DP, TM, None, None),
            P(DP, TM, None, None),
            P(TM, None),
            P(TM, None),
            P(),
            P(),
        ),
        check_vma=False,
    )
```

profile of v0, /device:TPU:1, one launch (start us, length us, event | category | flops | bytes accessed | tf_op | source)
XLA Modules:
  0.0 1005.3 jit_solution(17187182631220196640)
XLA Ops:
  9.2 3.1 fusion.88
  16.5 4.2 reshape.1066
  31.6 2.3 multiply_add_fusion
  37.1 5.3 collective-permute-start
  45.3 2.5 add_add_fusion
  69.4 2.3 copy.367
  71.7 3.2 convolution_convert_fusion.1
  74.9 2.3 copy.375
  78.2 130.4 %all-gather.2.cloned.1.call-done = bf16[1,1024,1536]{2,1,0:T(8,128)(2,1)} async-done(((bf16[1,32,1536]{2,1,0:T(8,128)(2,1)}), bf16[1,1024,1536]{2,1,0:T(8,128)(2,1)}) %all-gather.2.cloned.1.call-update) | async-done | bytes 3145744 | tf_op jit(solution)/shard_map/all_gather | solution.py:236
  208.6 3.8 fusion.122
  212.3 2.6 copy.366
  214.9 2.6 copy.368
  217.5 33.2 %while.30 = (s32[]{:T(128)}, f32[6,1,512,2]{2,3,1,0:T(2,128)}, f32[6,1,512,2]{2,3,1,0:T(2,128)}, f32[6,1,512,2,64]{2,4,3,1,0:T(8,128)}, bf16[6,1,1024,2,64]{2,4,...) while((s32[]{:T(128)}, f32[6,1,512,2]{2,3,1,0:T(2,128)}, ...), condition=%wide.region_5.6_spmd.clone, body=%wide.region_2.5_spmd.sunk.clone | while | flops 276822016 | bytes 13535321 | solution.py:151
  220.6 2.5 fusion.170
  226.1 2.5 fusion.170
  231.6 2.5 fusion.170
  237.2 2.5 fusion.170
  242.7 2.5 fusion.170
  248.2 2.5 fusion.170
  250.7 2.8 broadcast_divide_fusion
  253.5 72.1 %while.31 = (s32[]{:T(128)}, bf16[6,1,512,2,64]{2,4,3,1,0:T(8,128)(2,1)}, f32[6,1,1024,2,64]{2,4,3,1,0:T(8,128)}, f32[6,1,1024,2,64]{2,4,3,1,0:T(8,128)}, bf16[6...) while((s32[]{:T(128)}, ...), condition=%wide.region_8.9_spmd.clone, body=%wide.region_6.8_spmd.sunk.clone | while | flops 681245696 | bytes 25212056 | solution.py:151
  257.0 2.2 fusion.182
  259.2 2.1 fusion.183
  261.3 2.5 fusion.184
  269.0 2.2 fusion.182
  271.2 2.1 fusion.183
  273.3 2.5 fusion.184
  281.0 2.2 fusion.182
  283.2 2.1 fusion.183
  285.3 2.4 fusion.184
  293.0 2.2 fusion.182
  295.2 2.1 fusion.183
  297.3 2.5 fusion.184
  305.0 2.2 fusion.182
  307.2 2.1 fusion.183
  309.3 2.5 fusion.184
  317.0 2.2 fusion.182
  321.4 2.5 fusion.184
  325.6 6.6 pad_maximum_fusion.1
  332.2 16.0 %copy.383 = f32[1,1024,1536]{2,0,1:T(1,128)} copy(f32[1,1024,1536]{1,2,0:T(8,128)} %pad_maximum_fusion.1) | data formatting | bytes 12582912 | tf_op jit(solution)/shard_map/concatenate | solution.py:264
  364.0 2.3 copy.393
  368.3 2.3 fusion.101
  370.6 313.2 %all-reduce.10.cloned.1.call-done = f32[1,1024,1536]{2,0,1:T(1,128)} async-done(((f32[1,1024,1536]{2,0,1:T(1,128)}), f32[1,1024,1536]{2,0,1:T(1,128)}) %all-reduce.10.cloned.1.call-update) | async-done | bytes 6291472
  683.8 2.5 fusion.121
  704.1 2.1 collective-permute-start.3
  709.3 3.3 collective-permute-done.2
  716.4 4.1 reshape.1078
  724.5 5.0 convolution_bitcast_fusion
  729.5 8.0 pad_maximum_fusion
  737.5 9.6 copy.426
  752.6 3.1 copy.373
  759.2 3.0 copy.374
  762.2 4.2 fusion.98
  768.5 2.2 fusion.89
  775.0 10.8 %all-reduce.7 = (f32[2,27,64]{2,0,1:T(2,128)}, f32[2,64]{1,0:T(2,128)S(1)}) all-reduce(f32[2,27,64]{2,0,1:T(2,128)} %bitcast.517, f32[2,64]{1,0:T(2,128)S(1)} %copy-done.21), channel_id=1, replica_groups=mesh['dp_0'=2,'dp_1'=2,'tm_0'=2,'tm_1'=4,'tm_2'=4] {'dp_0'}, use_global_device_ids=true, to_apply=%region_15.16 | all-reduce | flops 3584 | bytes 28672 | tf_op jit(solution)/shard_map/psum | solution.py:66
  785.8 30.2 %all-reduce.6 = (f32[2,27,64]{2,0,1:T(2,128)}, f32[2,64]{1,0:T(2,128)S(1)}) all-reduce(f32[2,27,64]{2,0,1:T(2,128)} %get-tuple-element.312, f32[2,64]{1,0:T(2,128)S(1)} %get-tuple-element.313), channel_id=1, replica_groups=mesh['dp_0'=2,'dp_1'=2,'tm_0'=2,'tm_1'=4,'tm_2'=4] {'dp_1'}, use_global_device_ids=true, to_apply=%region_16.17 | all-reduce | flops 3584 | bytes 28672 | tf_op jit(solution)/shard_map/psum | solution.py:66
  816.0 10.5 %all-reduce.5 = (f32[2,27,64]{2,0,1:T(2,128)}, f32[2,64]{1,0:T(2,128)S(1)}) all-reduce(f32[2,27,64]{2,0,1:T(2,128)} %get-tuple-element.310, f32[2,64]{1,0:T(2,128)S(1)} %get-tuple-element.311), channel_id=1, replica_groups=mesh['dp_0'=2,'dp_1'=2,'tm_0'=2,'tm_1'=4,'tm_2'=4] {'tm_0'}, use_global_device_ids=true, to_apply=%region_17.18 | all-reduce | flops 3584 | bytes 28672 | tf_op jit(solution)/shard_map/psum | solution.py:66
  826.5 13.3 %all-reduce.4 = (f32[2,27,64]{2,0,1:T(2,128)}, f32[2,64]{1,0:T(2,128)S(1)}) all-reduce(f32[2,27,64]{2,0,1:T(2,128)} %get-tuple-element.308, f32[2,64]{1,0:T(2,128)S(1)} %get-tuple-element.309), channel_id=1, replica_groups=mesh['dp_0'=2,'dp_1'=2,'tm_0'=2,'tm_1'=4,'tm_2'=4] {'tm_1'}, use_global_device_ids=true, to_apply=%region_18.19 | all-reduce | flops 3584 | bytes 28672 | tf_op jit(solution)/shard_map/psum | solution.py:66
  839.8 20.7 %all-reduce.3 = (f32[2,27,64]{2,0,1:T(2,128)}, f32[2,64]{1,0:T(2,128)S(1)}) all-reduce(f32[2,27,64]{2,0,1:T(2,128)} %get-tuple-element.306, f32[2,64]{1,0:T(2,128)S(1)} %get-tuple-element.307), channel_id=1, replica_groups=mesh['dp_0'=2,'dp_1'=2,'tm_0'=2,'tm_1'=4,'tm_2'=4] {'tm_2'}, use_global_device_ids=true, to_apply=%region_19.20 | all-reduce | flops 3584 | bytes 28672 | tf_op jit(solution)/shard_map/psum | solution.py:66
  860.6 74.5 %reduce-scatter.4.cloned.1.call-done = f32[24,3072]{1,0:T(8,128)} async-done(((f32[768,3072]{1,0:T(8,128)}), f32[24,3072]{1,0:T(8,128)}) %reduce-scatter.4.cloned.1.call-update) | async-done | bytes 294928
  944.0 28.5 %all-to-all-start = ((f32[4,1,73728]{2,1,0:T(1,128)}), f32[4,1,73728]{2,1,0:T(1,128)}, u32[]{:S(2)}, u32[]{:S(2)}) async-start(f32[4,1,73728]{2,1,0:T(1,128)} %broadcast_in_dim.35), calls=%async_computation | async-start | bytes 2359296 | tf_op jit(solution)/shard_map/all_to_all | solution.py:48
  974.4 4.5 fusion.97
  978.9 10.0 all-to-all-done
  988.9 3.1 reduce_sum.92
  (201 shorter events, 175.2 us)
Async XLA Ops:
  7.2 2.0 copy-start
  7.2 201.4 %all-gather.2.cloned.1.call-start = ((), (), s32[]{:S(2)}) async-start(), calls=%async_computation.2 | async-start | bytes 3244032 | tf_op jit(solution)/shard_map/all_gather | solution.py:236
  12.3 1.4 copy-start.4
  20.7 4.4 copy-start.20
  22.6 1.0 copy-start.2
  27.8 14.6 %copy-start.22 = (f32[2,64]{1,0:T(2,128)S(1)}, f32[2,64]{1,0:T(2,128)}, u32[]{:S(2)}) copy-start(f32[2,64]{1,0:T(2,128)} %param.13) | copy-start | bytes 1540
  29.6 6.7 copy-start.1
  34.0 9.9 collective-permute-start.1
  37.1 8.2 collective-permute-start
  54.3 0.6 copy-start.15
  56.4 0.6 copy-start.19
  67.1 616.7 %all-reduce.10.cloned.1.call-start = ((), (), s32[]{:S(2)}) async-start(), calls=%async_computation.4 | async-start | bytes 12582912
  253.5 1.8 copy-start.3
  265.5 1.8 copy-start.3
  277.5 1.8 copy-start.3
  289.5 1.8 copy-start.3
  301.5 1.8 copy-start.3
  313.5 1.8 copy-start.3
  348.2 10.8 %copy-start.25 = (u32[128]{0:T(128)S(1)}, u32[128]{0:T(128)}, u32[]{:S(2)}) copy-start(u32[128]{0:T(128)} %constant.80) | copy-start | bytes 1540
  348.2 586.8 %reduce-scatter.4.cloned.1.call-start = ((), (), s32[]{:S(2)}) async-start(), calls=%async_computation.3 | async-start | bytes 9732096
  366.3 2.0 copy-start.11
  368.3 319.9 %copy-start.23 = (f32[2,64]{1,0:T(2,128)S(1)}, f32[2,64]{1,0:T(2,128)}, u32[]{:S(2)}) copy-start(f32[2,64]{1,0:T(2,128)} %param.13) | copy-start | bytes 1540
  702.5 10.8 %copy-start.16 = (f32[3,3,1536]{2,0,1:T(4,128)S(1)}, f32[3,3,1536]{2,0,1:T(4,128)}, u32[]{:S(2)}) copy-start(f32[3,3,1536]{2,0,1:T(4,128)} %copy.391) | copy-start | bytes 165892
  702.5 10.8 %copy-start.17 = (f32[3,3,1536]{2,0,1:T(4,128)S(1)}, f32[3,3,1536]{2,0,1:T(4,128)}, u32[]{:S(2)}) copy-start(f32[3,3,1536]{2,0,1:T(4,128)} %copy.390) | copy-start | bytes 165892
  702.5 10.8 %copy-start.18 = (f32[3,3,1536]{2,0,1:T(4,128)S(1)}, f32[3,3,1536]{2,0,1:T(4,128)}, u32[]{:S(2)}) copy-start(f32[3,3,1536]{2,0,1:T(4,128)} %copy.386) | copy-start | bytes 165892
  704.1 8.6 copy-start.12
  704.1 5.2 collective-permute-start.3
  706.3 6.4 collective-permute-start.2
  709.3 3.3 copy-start.13
  712.7 0.7 copy-start.14
  722.4 2.0 copy-start.7
  722.5 2.0 copy-start.24
  723.3 1.2 copy-start.6
  762.2 4.2 copy-start.5
  762.2 4.2 copy-start.8
  762.2 4.2 copy-start.9
  762.2 4.2 copy-start.10
  768.5 6.6 copy-start.21
  944.0 45.0 %all-to-all-start = ((f32[4,1,73728]{2,1,0:T(1,128)}), f32[4,1,73728]{2,1,0:T(1,128)}, u32[]{:S(2)}, u32[]{:S(2)}) async-start(f32[4,1,73728]{2,1,0:T(1,128)} %broadcast_in_dim.35), calls=%async_computation | async-start | bytes 2359296 | tf_op jit(solution)/shard_map/all_to_all | solution.py:48
Sparse Core Ops, SparseCore 0:
  67.2 141.2 all-gather.1
  348.3 335.4 all-reduce.9
  747.3 187.7 reduce-scatter.3
where the time goes:
time: 1020 us; the launch traced here: 1010 us
  waiting for transfers between devices  533 us (52%)
  local copies, waits for them, and re-layouts  158 us (15%)
  matrix products  109 us (11%)
  blocking collectives  85.5 us (8%)
  other arithmetic  64.7 us (6%)
  starting transfers between devices  39 us (4%)
  between operations  15.2 us (1%)
    unnamed x5, waiting for transfers between devices  388 us
    all_gather x1, waiting for transfers between devices, shards(): gathered = lax.all_gather(pooled, TM, axis=1, tiled=True)  130 us
    psum x5, blocking collectives, by_axis(): array = lax.psum(array, axis)  85.5 us
    all_to_all x1, starting transfers between devices, from_everyone(): return lax.all_to_all(copies, axis, split_axis=0, concat_axis=0, tiled=True)  28.5 us
  transfers between devices with their start and end apart: 8, of which 6 were waited for; matrix products, arithmetic and copies ran while one was open for 7% of the time, Pallas kernels for 0%

commit v1 on v0

v1 whole, which is shorter than its diff:
```python
import jax
import jax.numpy as jnp
from jax import lax
from jax.experimental import pallas as pl
from jax.experimental.pallas import tpu as pltpu
from jax.sharding import Mesh
from jax.sharding import PartitionSpec as P

HEADS = 12
GROUPS = 4
GROUP_HEADS = 3
HEAD = 64
WIDTH = 768
SPAN = GROUP_HEADS * HEAD
HW = 512
TAPS = 288
POS = 32
EPSILON = 1e-05
TM = ("tm_0", "tm_1", "tm_2")
DP = ("dp_0", "dp_1")
BF = jnp.bfloat16
F32 = jnp.float32


def dot(a, b, ca, cb):
    return lax.dot_general(a, b, (((ca,), (cb,)), ((), ())), preferred_element_type=F32)


def params(*semantics):
    return pltpu.CompilerParams(
        dimension_semantics=semantics or None, vmem_limit_bytes=56 * 1024 * 1024
    )


def tap_token(row):
    tap = row >> 5
    i = (row & 31) >> 2
    u = row & 3
    b = jnp.where(tap >= 3, 1, 0) + jnp.where(tap >= 6, 1, 0)
    e = tap - 3 * b
    y = 4 * i + b - 1
    x = 4 * u + e - 1
    return jnp.where((y >= 0) & (x >= 0), y * 16 + x, -1)


def gather_matrix():
    row = lax.broadcasted_iota(jnp.int32, (TAPS, 1), 0)
    token = lax.broadcasted_iota(jnp.int32, (TAPS, HW), 1)
    return jnp.where(token == tap_token(row), 1.0, 0.0).astype(BF)


def scatter_matrix():
    row = lax.broadcasted_iota(jnp.int32, (1, TAPS), 1)
    token = lax.broadcasted_iota(jnp.int32, (HW, TAPS), 0)
    return jnp.where(token == tap_token(row), 1.0, 0.0).astype(BF)


def over_heads(row):
    pair = jnp.concatenate([row, row], axis=-1)
    return jnp.concatenate([pair] * (HEADS // 2), axis=-1)


def head_mean(x):
    rows = x.shape[0]
    chunks = x.shape[1] // 128
    tall = jnp.concatenate([x[:, 128 * k : 128 * k + 128] for k in range(chunks)], axis=0)
    i = lax.broadcasted_iota(jnp.int32, (128, 128), 0) >> 6
    j = lax.broadcasted_iota(jnp.int32, (128, 128), 1) >> 6
    block = jnp.where(i == j, 1.0 / 64.0, 0.0).astype(F32)
    mean = jnp.dot(tall, block, preferred_element_type=F32, precision=lax.Precision.HIGHEST)
    return jnp.concatenate([mean[rows * k : rows * k + rows] for k in range(chunks)], axis=1)


def tap_sums_kernel(tok_ref, w_ref, pk_ref, taps_ref, tt_ref, p0_ref, p1_ref, p2_ref):
    @pl.when(pl.program_id(0) == 0)
    def _():
        tt_ref[...] = dot(gather_matrix(), tok_ref[...], 1, 0).astype(BF)

    taps = dot(tt_ref[...], w_ref[...], 1, 0).astype(BF)
    taps_ref[...] = taps
    wide = taps.astype(F32)
    kernel = over_heads(pk_ref[0])
    for a, p_ref in enumerate((p0_ref, p1_ref, p2_ref)):
        total = None
        for be in range(9):
            term = wide[32 * be : 32 * be + 32] * kernel[9 * a + be : 9 * a + be + 1]
            total = term if total is None else total + term
        p_ref[...] = total


def tap_sums(tokens, qkv_weight, pool_kernel):
    part = jax.ShapeDtypeStruct((POS, 2 * WIDTH), F32)
    part_spec = pl.BlockSpec((POS, WIDTH), lambda s: (0, s))
    return pl.pallas_call(
        tap_sums_kernel,
        grid=(2,),
        in_specs=[
            pl.BlockSpec((HW, WIDTH), lambda s: (0, 0)),
            pl.BlockSpec((WIDTH, WIDTH), lambda s: (0, s + 1)),
            pl.BlockSpec((1, 27, HEAD), lambda s: (s, 0, 0)),
        ],
        out_specs=[
            pl.BlockSpec((TAPS, WIDTH), lambda s: (0, s)),
            pl.BlockSpec((TAPS, WIDTH), lambda s: (0, 0)),
            part_spec,
            part_spec,
            part_spec,
        ],
        out_shape=[
            jax.ShapeDtypeStruct((TAPS, 2 * WIDTH), BF),
            jax.ShapeDtypeStruct((TAPS, WIDTH), BF),
            part,
            part,
            part,
        ],
        compiler_params=params("arbitrary"),
        name="tap_sums",
    )(tokens, qkv_weight, pool_kernel)


def query_kernel(tok_ref, w_ref, cot_ref, ow_ref, qd_ref):
    q = dot(tok_ref[...], w_ref[...], 1, 0).astype(BF)
    dm = dot(cot_ref[...], ow_ref[...], 1, 1).astype(BF)
    for g in range(GROUPS):
        lanes = slice(SPAN * g, SPAN * g + SPAN)
        qd_ref[g] = jnp.concatenate([q[:, lanes], dm[:, lanes]], axis=-1)


def query_side(tokens, qkv_weight, cotangent, out_weight):
    full = pl.BlockSpec((HW, WIDTH), lambda i: (0, 0))
    square = pl.BlockSpec((WIDTH, WIDTH), lambda i: (0, 0))
    return pl.pallas_call(
        query_kernel,
        grid=(1,),
        in_specs=[full, square, full, square],
        out_specs=pl.BlockSpec((GROUPS, HW, 2 * SPAN), lambda i: (0, 0, 0)),
        out_shape=jax.ShapeDtypeStruct((GROUPS, HW, 2 * SPAN), BF),
        compiler_params=params("arbitrary"),
        name="query_side",
    )(tokens, qkv_weight, cotangent, out_weight)


def gain_row(gain_ref):
    return jnp.concatenate([over_heads(gain_ref[0:1, :]), over_heads(gain_ref[1:2, :])], axis=-1)


def norm_kernel(low_ref, own_ref, up_ref, gain_ref, kv_ref, normed_ref, inv_ref):
    x = low_ref[...] + own_ref[...] + up_ref[...]
    centred = x - head_mean(x)
    inv = lax.rsqrt(head_mean(centred * centred) + EPSILON)
    normed = centred * inv
    normed_ref[...] = normed
    inv_ref[...] = inv
    pooled = normed * gain_row(gain_ref)
    for g in range(GROUPS):
        k = pooled[:, SPAN * g : SPAN * g + SPAN]
        v = pooled[:, WIDTH + SPAN * g : WIDTH + SPAN * g + SPAN]
        block = jnp.concatenate([k, v], axis=-1).astype(BF)
        for z in range(2):
            for y in range(4):
                kv_ref[z, g, y] = block


def norm_side(low, own, up, gain):
    flat = jax.ShapeDtypeStruct((POS, 2 * WIDTH), F32)
    return pl.pallas_call(
        norm_kernel,
        out_shape=[jax.ShapeDtypeStruct((2, GROUPS, 4, POS, 2 * SPAN), BF), flat, flat],
        compiler_params=params(),
        name="norm_side",
    )(low, own, up, gain)


def attention_kernel(qd_ref, kv_ref, md_ref, dkv_ref, acc_ref):
    step = pl.program_id(0)

    @pl.when(step == 0)
    def _():
        acc_ref[...] = jnp.zeros_like(acc_ref)

    mixed, d_query = [], []
    for h in range(GROUP_HEADS):
        lo = slice(HEAD * h, HEAD * h + HEAD)
        hi = slice(SPAN + HEAD * h, SPAN + HEAD * h + HEAD)
        q = qd_ref[0, :, lo]
        dm = qd_ref[0, :, hi]
        k = kv_ref[:, lo]
        v = kv_ref[:, hi]
        scores = dot(q * jnp.asarray(0.125, BF), k, 1, 1)
        weights = jnp.exp(scores - jnp.max(scores, axis=-1, keepdims=True))
        inverse = 1.0 / jnp.sum(weights, axis=-1, keepdims=True)
        rounded = weights.astype(BF)
        attended = dot(rounded, v, 1, 0) * inverse
        mixed.append((attended + q.astype(F32)).astype(BF))
        wide = dm.astype(F32)
        delta = jnp.sum(wide * attended, axis=-1, keepdims=True)
        acc_ref[hi, :] += dot((wide * inverse).astype(BF), rounded, 0, 0)
        d_scores = ((weights * inverse) * (dot(dm, v, 1, 1) - delta)).astype(BF)
        d_query.append((dot(d_scores, k, 1, 0) * 0.125 + wide).astype(BF))
        acc_ref[lo, :] += dot(q, d_scores, 0, 0) * 0.125
    md_ref[0] = jnp.concatenate(mixed + d_query, axis=-1)

    @pl.when(step == pl.num_programs(0) - 1)
    def _():
        dkv_ref[...] = jnp.transpose(acc_ref[...]).astype(BF)


def attention(qd, kv):
    frames, rows, lanes = qd.shape
    keys = kv.shape[0]
    return pl.pallas_call(
        attention_kernel,
        grid=(frames,),
        in_specs=[
            pl.BlockSpec((1, rows, lanes), lambda f: (f, 0, 0)),
            pl.BlockSpec((keys, lanes), lambda f: (0, 0)),
        ],
        out_specs=[
            pl.BlockSpec((1, rows, lanes), lambda f: (f, 0, 0)),
            pl.BlockSpec((keys, lanes), lambda f: (0, 0)),
        ],
        out_shape=[
            jax.ShapeDtypeStruct(qd.shape, BF),
            jax.ShapeDtypeStruct(kv.shape, BF),
        ],
        scratch_shapes=[pltpu.VMEM((lanes, keys), F32)],
        compiler_params=params("arbitrary"),
        name="attention",
    )(qd, kv)


def norm_back_kernel(parts_ref, normed_ref, inv_ref, gain_ref, d_ref, gsum_ref):
    keys, values = [], []
    for g in range(GROUPS):
        total = None
        for z in range(2):
            for y in range(4):
                term = parts_ref[z, g, y].astype(F32)
                total = term if total is None else total + term
        keys.append(total[:, :SPAN])
        values.append(total[:, SPAN:])
    d_pooled = jnp.concatenate(keys + values, axis=-1)
    normed = normed_ref[...]
    gsum_ref[...] = jnp.sum(d_pooled * normed, axis=0, keepdims=True)
    dn = d_pooled * gain_row(gain_ref)
    d_ref[...] = inv_ref[...] * (dn - head_mean(dn) - normed * head_mean(dn * normed))


def norm_back(parts, normed, inv, gain):
    return pl.pallas_call(
        norm_back_kernel,
        out_shape=[
            jax.ShapeDtypeStruct((POS, 2 * WIDTH), F32),
            jax.ShapeDtypeStruct((1, 2 * WIDTH), F32),
        ],
        compiler_params=params(),
        name="norm_back",
    )(parts, normed, inv, gain)


def head_sum(x):
    out = []
    for s in range(2):
        pair = x[:, WIDTH * s : WIDTH * s + 128]
        for k in range(1, HEADS // 2):
            pair = pair + x[:, WIDTH * s + 128 * k : WIDTH * s + 128 * k + 128]
        out.append(pair[:, :HEAD] + pair[:, HEAD:])
    return jnp.concatenate(out, axis=-1)


def pool_back_kernel(up_ref, own_ref, low_ref, taps_ref, tt_ref, pk_ref, gsum_ref, dv_ref, pay_ref):
    kernel = jnp.concatenate([over_heads(pk_ref[0]), over_heads(pk_ref[1])], axis=-1)
    sources = (up_ref[...], own_ref[...], low_ref[...])
    tap_rows = []
    for a in range(3):
        for be in range(9):
            tap = taps_ref[32 * be : 32 * be + 32, :].astype(F32)
            tap_rows.append(jnp.sum(sources[a] * tap, axis=0, keepdims=True))
    for be in range(9):
        total = None
        for a in range(3):
            term = sources[a] * kernel[9 * a + be : 9 * a + be + 1]
            total = term if total is None else total + term
        dv_ref[32 * be : 32 * be + 32, :] = total.astype(BF)
    small = head_sum(jnp.concatenate(tap_rows + [gsum_ref[...]], axis=0))
    first = small[0:24]
    second = jnp.concatenate([small[24:28], jnp.zeros((20, 128), F32)], axis=0)
    extra = jnp.concatenate([first, second], axis=-1).astype(BF)
    grads = dot(tt_ref[...], dv_ref[...], 0, 0)
    for f in range(32):
        pay_ref[f, :, : 2 * WIDTH] = grads[24 * f : 24 * f + 24].astype(BF)
        pay_ref[f, :, 2 * WIDTH :] = extra


def pool_back(up, own, low, taps, tap_tokens, pool_kernel, gain_sum):
    return pl.pallas_call(
        pool_back_kernel,
        out_shape=[
            jax.ShapeDtypeStruct((TAPS, 2 * WIDTH), BF),
            jax.ShapeDtypeStruct((32, 24, 2 * WIDTH + 256), BF),
        ],
        compiler_params=params(),
        name="pool_back",
    )(up, own, low, taps, tap_tokens, pool_kernel, gain_sum)


def output_kernel(md_ref, tok_ref, cot_ref, ow_ref, out_ref, dq_ref, pay_ref):
    mixed = jnp.concatenate([md_ref[g, :, :SPAN] for g in range(GROUPS)], axis=-1)
    dq = jnp.concatenate([md_ref[g, :, SPAN:] for g in range(GROUPS)], axis=-1)
    dq_ref[...] = dq
    out_ref[...] = dot(mixed, ow_ref[...], 1, 0).astype(BF)
    q_grad = dot(tok_ref[...], dq, 0, 0)
    o_grad = dot(mixed, cot_ref[...], 0, 0)
    for f in range(32):
        rows = slice(24 * f, 24 * f + 24)
        pay_ref[f, :, :WIDTH] = q_grad[rows].astype(BF)
        pay_ref[f, :, WIDTH:] = o_grad[rows].astype(BF)


def output_side(md, tokens, cotangent, out_weight):
    return pl.pallas_call(
        output_kernel,
        out_shape=[
            jax.ShapeDtypeStruct((HW, WIDTH), BF),
            jax.ShapeDtypeStruct((HW, WIDTH), BF),
            jax.ShapeDtypeStruct((32, 24, 2 * WIDTH), BF),
        ],
        compiler_params=params(),
        name="output_side",
    )(md, tokens, cotangent, out_weight)


def token_grad_kernel(dq_ref, dv_ref, w_ref, out_ref):
    spread = dot(scatter_matrix(), dv_ref[...], 1, 0).astype(BF)
    total = dot(dq_ref[...], w_ref[:, :WIDTH], 1, 1) + dot(spread, w_ref[:, WIDTH:], 1, 1)
    out_ref[...] = total.astype(BF)


def token_grad(dq, dv, qkv_weight):
    return pl.pallas_call(
        token_grad_kernel,
        out_shape=jax.ShapeDtypeStruct((HW, WIDTH), BF),
        compiler_params=params(),
        name="token_grad",
    )(dq, dv, qkv_weight)


def fold_kernel(parts_ref, out_ref):
    total = parts_ref[0].astype(F32)
    for f in range(1, 32):
        total = total + parts_ref[f].astype(F32)
    for c in range(4):
        out_ref[c] = total


def fold(parts):
    return pl.pallas_call(
        fold_kernel,
        out_shape=jax.ShapeDtypeStruct((4,) + parts.shape[1:], F32),
        compiler_params=params(),
        name="fold",
    )(parts)


def finish_kernel(scale, a_ref, b_ref, qkv_ref, out_ref, kernel_ref, gain_ref):
    a = (a_ref[0] + a_ref[1] + a_ref[2] + a_ref[3]) * scale
    b = (b_ref[0] + b_ref[1] + b_ref[2] + b_ref[3]) * scale
    qkv_ref[:, :WIDTH] = a[:, :WIDTH]
    qkv_ref[:, WIDTH:] = b[:, : 2 * WIDTH]
    out_ref[...] = a[:, WIDTH:]
    first = b[:, 2 * WIDTH : 2 * WIDTH + 128]
    second = b[:, 2 * WIDTH + 128 :]
    for s in range(2):
        lanes = slice(HEAD * s, HEAD * s + HEAD)
        kernel_ref[s, 0:24, :] = first[:, lanes]
        kernel_ref[s, 24:27, :] = second[0:3, lanes]
        gain_ref[s : s + 1, :] = second[3:4, lanes]


def finish(a, b, scale):
    return pl.pallas_call(
        lambda *refs: finish_kernel(scale, *refs),
        out_shape=[
            jax.ShapeDtypeStruct((24, 3 * WIDTH), F32),
            jax.ShapeDtypeStruct((24, WIDTH), F32),
            jax.ShapeDtypeStruct((2, 27, HEAD), F32),
            jax.ShapeDtypeStruct((2, HEAD), F32),
        ],
        compiler_params=params(),
        name="finish",
    )(a, b)


def exchange(array, axis):
    return lax.all_to_all(array, axis, split_axis=0, concat_axis=0, tiled=True)


def to_next(array):
    return lax.ppermute(array, TM, [(i, i + 1) for i in range(lax.axis_size(TM) - 1)])


def to_previous(array):
    return lax.ppermute(array, TM, [(i + 1, i) for i in range(lax.axis_size(TM) - 1)])


def shards(tokens, qkv_weight, pool_kernel, norm_gain, out_weight, out_cotangent):
    shape = tokens.shape
    token_rows = tokens.reshape(HW, WIDTH)
    cotangent_rows = out_cotangent.reshape(HW, WIDTH)
    taps, tap_tokens, part0, part1, part2 = tap_sums(token_rows, qkv_weight, pool_kernel)
    low = to_next(part0)
    up = to_previous(part2)
    qd = query_side(token_rows, qkv_weight, cotangent_rows, out_weight)
    qd = exchange(qd, "tm_1")
    kv, normed, inv = norm_side(low, part1, up, norm_gain)
    kv = exchange(kv.reshape(32, POS, 2 * SPAN), TM)
    md, dkv = attention(qd, kv.reshape(32 * POS, 2 * SPAN))
    parts = exchange(dkv.reshape(32, POS, 2 * SPAN), TM)
    md = exchange(md, "tm_1")
    d_summed, gain_sum = norm_back(
        parts.reshape(2, GROUPS, 4, POS, 2 * SPAN), normed, inv, norm_gain
    )
    d_low = to_next(d_summed)
    d_up = to_previous(d_summed)
    block_out, dq, pay_a = output_side(md, token_rows, cotangent_rows, out_weight)
    pay_a = fold(exchange(pay_a, TM))
    pay_a = exchange(pay_a, DP)
    dv, pay_b = pool_back(d_up, d_summed, d_low, taps, tap_tokens, pool_kernel, gain_sum)
    pay_b = fold(exchange(pay_b, TM))
    grad_tokens = token_grad(dq, dv, qkv_weight)
    pay_b = exchange(pay_b, DP)
    scale = float(HW * lax.axis_size(DP) * lax.axis_size(TM)) ** (-0.5)
    grads = finish(pay_a, pay_b, scale)
    return (block_out.reshape(shape), grad_tokens.reshape(shape), *grads)


def solution(mesh):
    torus = Mesh(mesh.devices.reshape(2, 2, 2, 4, 4), DP + TM)
    placed = (P(DP, TM, None, None), P(), P(), P(), P(), P(DP, TM, None, None))
    return jax.shard_map(
        shards,
        mesh=torus,
        in_specs=placed,
        out_specs=(
            P(DP, TM, None, None),
            P(DP, TM, None, None),
            P(TM, None),
            P(TM, None),
            P(),
            P(),
        ),
        check_vma=False,
    )
```

time: 1020 us -> 260 us (0.25); the launches traced: 1010 us -> 259 us
  waiting for transfers between devices: 533 us -> 84 us
  local copies, waits for them, and re-layouts: 158 us -> 7.33 us
  matrix products: 109 us -> 0 us
  Pallas kernels: 0 us -> 71.7 us
  other arithmetic: 64.7 us -> 0 us
  blocking collectives: 85.5 us -> 42.6 us
  between operations: 15.2 us -> 0.72 us
  starting transfers between devices: 39 us -> 52.3 us
    unnamed x5 -> x0, waiting for transfers between devices: 388 us -> none
    all_gather x1 -> x0, waiting for transfers between devices: 130 us -> none  [shards(): gathered = lax.all_gather(pooled, TM, axis=1, tiled=True)]
    dot_general x48 -> x0, matrix products: 109 us -> none  [the longest x6 14.9 us: group_backward(): jnp.einsum('crgk,crgd->ckgd', d_scores, queries, preferred_element_type=j...]
    psum x5 -> x0, blocking collectives: 85.5 us -> none  [by_axis(): array = lax.psum(array, axis)]
    pallas_call x0 -> x11, Pallas kernels: none -> 71.7 us  [the longest x1 31.9 us: attention(): pl.pallas_call(attention_kernel, grid=(frames,), in_specs=[pl.BlockSpec((...]
    all_to_all x1 -> x6, waiting for transfers between devices: 10 us -> 53.2 us  [exchange(): return lax.all_to_all(array, axis, split_axis=0, concat_axis=0, tiled=True)]
    all_to_all x0 -> x2, blocking collectives: none -> 42.6 us  [exchange(): return lax.all_to_all(array, axis, split_axis=0, concat_axis=0, tiled=True)]
    reshape x13 -> x0, local copies, waits for them, and re-layouts: 28 us -> none  [the longest x1 4.24 us: cut_blocks(): padded.reshape(extent[:-3] + (pooled_h + 1, 4, pooled_w + 1, 4, extent[-1]))]
  transfers between devices with their start and end apart: 8 -> 10, of which waited for: 6 -> 9; matrix products, arithmetic and copies ran while one was open for 7% -> 0% of each run, Pallas kernels for 0% -> 12%
where the time goes in v1:
time: 260 us; the launch traced here: 259 us
  waiting for transfers between devices  84 us (32%)
  Pallas kernels  71.7 us (28%)
  starting transfers between devices  52.3 us (20%)
  blocking collectives  42.6 us (16%)
  local copies, waits for them, and re-layouts  7.33 us (3%)
    all_to_all x6, waiting for transfers between devices, exchange(): return lax.all_to_all(array, axis, split_axis=0, concat_axis=0, tiled=True)  53.2 us
    all_to_all x6, starting transfers between devices, exchange(): return lax.all_to_all(array, axis, split_axis=0, concat_axis=0, tiled=True)  42.7 us
    all_to_all x2, blocking collectives, exchange(): return lax.all_to_all(array, axis, split_axis=0, concat_axis=0, tiled=True)  42.6 us
    pallas_call x1, Pallas kernels, attention(): pl.pallas_call(attention_kernel, grid=(frames,), in_specs=[pl.BlockSpec((...  31.9 us
    ppermute x2, waiting for transfers between devices, to_next(): lax.ppermute(array, TM, [(i, i + 1) for i in range(lax.axis_size(TM) - 1)])  18.8 us
    ppermute x2, waiting for transfers between devices, to_previous(): lax.ppermute(array, TM, [(i + 1, i) for i in range(lax.axis_size(TM) - 1)])  12 us
    unnamed x22, local copies, waits for them, and re-layouts  7.33 us
    ppermute x2, starting transfers between devices, to_next(): lax.ppermute(array, TM, [(i, i + 1) for i in range(lax.axis_size(TM) - 1)])  7.04 us
  transfers between devices with their start and end apart: 10, of which 9 were waited for; matrix products, arithmetic and copies ran while one was open for 0% of the time, Pallas kernels for 12%

profile of v1, /device:TPU:1, one launch (start us, length us, event | category | flops | bytes accessed | tf_op | source)
XLA Modules:
  0.0 258.7 jit_solution(16406597427477135668)
XLA Ops:
  0.6 1.4 copy.12.pk_ref
  2.0 4.1 %tap_sums.1 = (bf16[288,1536]{1,0:T(8,128)(2,1)}, bf16[288,768]{1,0:T(8,128)(2,1)}, f32[32,1536]{1,0:T(8,128)}, f32[32,1536]{1,0:T(8,128)}, f32[32,1536]{1,0:T(8,128)}) custom-call(bf16[512,768]{1,0:T(8,128)(2,1)} %bitcast.8, bf16[768,2304]{1,0:T(8,128)(2,1)} %w_ref.5, f32[2,27,64]{2,1,0:T(8,128)} %copy.12.pk_ref), custom_call_target="tpu_custom_call" | custom-call | tf_op jit(solution)/shard_map/tap_sums/pallas_call | solution.py:94
  6.1 4.0 %collective-permute-start = (f32[32,1536]{1,0:T(8,128)}, f32[32,1536]{1,0:T(8,128)S(1)}, u32[]{:S(2)}, u32[]{:S(2)}) collective-permute-start(f32[32,1536]{1,0:T(8,128)} %get-tuple-element.27), channel_id=1, source_target_pairs={{0,1},{1,2},{2,3},{3,4},{4,5},{5,6},{6,7},{7,8},{8,9},{9,10},{10,1... | collective-permute-start | bytes 589832 | tf_op jit(solution)/shard_map/ppermute | solution.py:399
  10.1 1.3 collective-permute-start.1
  11.4 2.6 collective-permute-done.low_ref
  14.0 0.0 copy-start.8
  14.0 3.7 %collective-permute-done.1.up_ref = f32[32,1536]{1,0:T(8,128)S(1)} collective-permute-done((f32[32,1536]{1,0:T(8,128)}, f32[32,1536]{1,0:T(8,128)S(1)}, u32[]{:S(2)}, u32[]{:S(2)}) %collective-permute-start.1) | collective-permute-done | bytes 196640 | tf_op jit(solution)/shard_map/ppermute | solution.py:403
  17.7 0.0 copy-start.9
  17.7 0.0 copy-done.8
  17.7 0.7 copy-done.9
  18.4 3.0 %norm_side.1 = (bf16[2,4,4,32,384]{4,3,2,1,0:T(8,128)(2,1)}, f32[32,1536]{1,0:T(8,128)}, f32[32,1536]{1,0:T(8,128)}) custom-call(f32[32,1536]{1,0:T(8,128)} %copy-done.8, f32[32,1536]{1,0:T(8,128)} %get-tuple-element.28.own_ref, f32[32,1536]{1,0:T(8,128)} %copy-done.9, f32[2,64]{1,0:T(2,128)} %gain_ref.3), custom_call_target="tpu_custom_call" | custom-call | tf_op jit(solution)/shard_map/norm_side/pallas_call | solution.py:166
  21.3 10.7 %all-to-all-start.1 = ((bf16[32,32,384]{2,1,0:T(8,128)(2,1)}), bf16[32,32,384]{2,1,0:T(8,128)(2,1)S(1)}, u32[]{:S(2)}, u32[]{:S(2)}) async-start(bf16[32,32,384]{2,1,0:T(8,128)(2,1)} %bitcast.15), calls=%async_computation.1 | async-start | bytes 1572864 | tf_op jit(solution)/shard_map/all_to_all | solution.py:395
  32.1 4.7 %query_side.1 = bf16[4,512,384]{2,1,0:T(8,128)(2,1)} custom-call(bf16[512,768]{1,0:T(8,128)(2,1)} %bitcast.9, bf16[768,2304]{1,0:T(8,128)(2,1)} %w_ref.5, bf16[512,768]{1,0:T(8,128)(2,1)} %bitcast.13, bf16[768,768]{1,0:T(8,128)(2,1)} %ow_ref.3), custom_call_target="tpu_custom_call" | custom-call | tf_op jit(solution)/shard_map/query_side/pallas_call | solution.py:132
  36.8 6.9 %all-to-all-done.1 = bf16[32,32,384]{2,1,0:T(8,128)(2,1)S(1)} async-done(((bf16[32,32,384]{2,1,0:T(8,128)(2,1)}), bf16[32,32,384]{2,1,0:T(8,128)(2,1)S(1)}, u32[]{:S(2)}, u32[]{:S(2)}) %all-to-all-start.1) | async-done | bytes 786464 | tf_op jit(solution)/shard_map/all_to_all | solution.py:395
  43.7 0.0 copy-start.3
  43.7 21.9 %all_to_all.40.qd_ref = bf16[4,512,384]{2,1,0:T(8,128)(2,1)} all-to-all(bf16[4,512,384]{2,1,0:T(8,128)(2,1)} %query_side.1), channel_id=1, replica_groups=mesh['dp_0'=2,'dp_1'=2,'tm_0'=2,'tm_1'=4,'tm_2'=4] {'tm_1'}, dimensions={0} | all-to-all | bytes 3145728 | tf_op jit(solution)/shard_map/all_to_all | solution.py:395
  65.6 0.0 copy-done.3
  65.6 31.9 %attention.1 = (bf16[4,512,384]{2,1,0:T(8,128)(2,1)}, bf16[1024,384]{1,0:T(8,128)(2,1)}) custom-call(bf16[4,512,384]{2,1,0:T(8,128)(2,1)} %all_to_all.40.qd_ref, bf16[1024,384]{1,0:T(8,128)(2,1)} %bitcast.12), custom_call_target="tpu_custom_call" | custom-call | tf_op jit(solution)/shard_map/attention/pallas_call | solution.py:211
  97.5 20.7 %all_to_all.41.md_ref = bf16[4,512,384]{2,1,0:T(8,128)(2,1)} all-to-all(bf16[4,512,384]{2,1,0:T(8,128)(2,1)} %get-tuple-element.31), channel_id=1, replica_groups=mesh['dp_0'=2,'dp_1'=2,'tm_0'=2,'tm_1'=4,'tm_2'=4] {'tm_1'}, dimensions={0} | all-to-all | bytes 3145728 | tf_op jit(solution)/shard_map/all_to_all | solution.py:395
  118.2 7.2 %all-to-all-start.3 = ((bf16[32,32,384]{2,1,0:T(8,128)(2,1)}), bf16[32,32,384]{2,1,0:T(8,128)(2,1)S(1)}, u32[]{:S(2)}, u32[]{:S(2)}) async-start(bf16[32,32,384]{2,1,0:T(8,128)(2,1)} %bitcast.5), calls=%async_computation.3 | async-start | bytes 1572864 | tf_op jit(solution)/shard_map/all_to_all | solution.py:395
  125.4 5.8 %output_side.1 = (bf16[512,768]{1,0:T(8,128)(2,1)}, bf16[512,768]{1,0:T(8,128)(2,1)}, bf16[32,24,1536]{2,1,0:T(8,128)(2,1)}) custom-call(bf16[4,512,384]{2,1,0:T(8,128)(2,1)} %all_to_all.41.md_ref, bf16[512,768]{1,0:T(8,128)(2,1)} %bitcast.10, bf16[512,768]{1,0:T(8,128)(2,1)} %bitcast.14, bf16[768,768]{1,0:T(8,128)(2,1)} %ow_ref.3), custom_call_target="tpu_custom_call" | custom-call | tf_op jit(solution)/shard_map/output_side/pallas_call | solution.py:321
  131.2 4.5 %all-to-all-done.3 = bf16[32,32,384]{2,1,0:T(8,128)(2,1)S(1)} async-done(((bf16[32,32,384]{2,1,0:T(8,128)(2,1)}), bf16[32,32,384]{2,1,0:T(8,128)(2,1)S(1)}, u32[]{:S(2)}, u32[]{:S(2)}) %all-to-all-start.3) | async-done | bytes 786464 | tf_op jit(solution)/shard_map/all_to_all | solution.py:395
  135.7 0.0 copy-start.2
  135.7 0.9 copy-done.2
  136.5 4.1 %all-to-all-start.4 = ((bf16[32,24,1536]{2,1,0:T(8,128)(2,1)}), bf16[32,24,1536]{2,1,0:T(8,128)(2,1)S(1)}, u32[]{:S(2)}, u32[]{:S(2)}) async-start(bf16[32,24,1536]{2,1,0:T(8,128)(2,1)} %get-tuple-element.42), calls=%async_computation.4 | async-start | bytes 4718592 | tf_op jit(solution)/shard_map/all_to_all | solution.py:395
  140.6 2.6 norm_back.1
  143.2 3.0 %collective-permute-start.3 = (f32[32,1536]{1,0:T(8,128)}, f32[32,1536]{1,0:T(8,128)S(1)}, u32[]{:S(2)}, u32[]{:S(2)}) collective-permute-start(f32[32,1536]{1,0:T(8,128)} %get-tuple-element.37.own_ref), channel_id=1, source_target_pairs={{0,1},{1,2},{2,3},{3,4},{4,5},{5,6},{6,7},{7,8},{8,9},{9,10},{10,1... | collective-permute-start | bytes 589832 | tf_op jit(solution)/shard_map/ppermute | solution.py:399
  146.2 1.3 collective-permute-start.2
  147.5 16.2 %collective-permute-done.3.low_ref = f32[32,1536]{1,0:T(8,128)S(1)} collective-permute-done((f32[32,1536]{1,0:T(8,128)}, f32[32,1536]{1,0:T(8,128)S(1)}, u32[]{:S(2)}, u32[]{:S(2)}) %collective-permute-start.3) | collective-permute-done | bytes 196640 | tf_op jit(solution)/shard_map/ppermute | solution.py:399
  163.7 0.0 copy-start.6
  163.7 8.2 %collective-permute-done.2.up_ref = f32[32,1536]{1,0:T(8,128)S(1)} collective-permute-done((f32[32,1536]{1,0:T(8,128)}, f32[32,1536]{1,0:T(8,128)S(1)}, u32[]{:S(2)}, u32[]{:S(2)}) %collective-permute-start.2) | collective-permute-done | bytes 196640 | tf_op jit(solution)/shard_map/ppermute | solution.py:403
  172.0 0.0 copy-start.7
  172.0 0.0 copy-done.6
  172.0 0.7 copy-done.7
  172.6 5.2 %pool_back.1 = (bf16[288,1536]{1,0:T(8,128)(2,1)}, bf16[32,24,1792]{2,1,0:T(8,128)(2,1)}) custom-call(f32[32,1536]{1,0:T(8,128)} %copy-done.7, f32[32,1536]{1,0:T(8,128)} %get-tuple-element.37.own_ref, f32[32,1536]{1,0:T(8,128)} %copy-done.6, bf16[288,1536]{1,0:T(8,128)(2,1)} %get-tuple-element.38.taps_ref, bf16[288,768]{1,0:T(8,128)(2,1)} %get-tuple-element.39.tt_ref, ...), custom_call_target="tpu_custom_call" | custom-call | tf_op jit(solution)/shard_map/pool_back/pallas_call | solution.py:296
  177.9 0.0 all-to-all-done.4.parts_ref
  177.9 0.0 copy-start.1
  177.9 1.5 copy-done.1
  179.4 7.5 %all-to-all-start.6 = ((bf16[32,24,1792]{2,1,0:T(8,128)(2,1)}), bf16[32,24,1792]{2,1,0:T(8,128)(2,1)S(1)}, u32[]{:S(2)}, u32[]{:S(2)}) async-start(bf16[32,24,1792]{2,1,0:T(8,128)(2,1)} %get-tuple-element.43), calls=%async_computation.6 | async-start | bytes 5505024 | tf_op jit(solution)/shard_map/all_to_all | solution.py:395
  186.9 2.8 %fold.2 = f32[4,24,1536]{2,1,0:T(8,128)} custom-call(bf16[32,24,1536]{2,1,0:T(8,128)(2,1)} %copy-done.1), custom_call_target="tpu_custom_call" | custom-call | tf_op jit(solution)/shard_map/fold/pallas_call | solution.py:357
  189.7 30.4 %all-to-all-done.6.parts_ref = bf16[32,24,1792]{2,1,0:T(8,128)(2,1)S(1)} async-done(((bf16[32,24,1792]{2,1,0:T(8,128)(2,1)}), bf16[32,24,1792]{2,1,0:T(8,128)(2,1)S(1)}, u32[]{:S(2)}, u32[]{:S(2)}) %all-to-all-start.6) | async-done | bytes 2752544 | tf_op jit(solution)/shard_map/all_to_all | solution.py:395
  220.1 0.0 copy-start
  220.1 8.8 %all-to-all-start.5 = ((f32[4,24,1536]{2,1,0:T(8,128)}), f32[4,24,1536]{2,1,0:T(8,128)S(1)}, u32[]{:S(2)}, u32[]{:S(2)}) async-start(f32[4,24,1536]{2,1,0:T(8,128)} %fold.2), calls=%async_computation.5 | async-start | bytes 1179648 | tf_op jit(solution)/shard_map/all_to_all | solution.py:395
  228.8 0.0 copy-done
  228.9 3.0 %fold.3 = f32[4,24,1792]{2,1,0:T(8,128)} custom-call(bf16[32,24,1792]{2,1,0:T(8,128)(2,1)} %copy-done), custom_call_target="tpu_custom_call" | custom-call | tf_op jit(solution)/shard_map/fold/pallas_call | solution.py:357
  231.8 7.1 %all-to-all-done.5.refs_0_ = f32[4,24,1536]{2,1,0:T(8,128)S(1)} async-done(((f32[4,24,1536]{2,1,0:T(8,128)}), f32[4,24,1536]{2,1,0:T(8,128)S(1)}, u32[]{:S(2)}, u32[]{:S(2)}) %all-to-all-start.5) | async-done | bytes 589856 | tf_op jit(solution)/shard_map/all_to_all | solution.py:395
  238.9 0.0 copy-start.5
  238.9 4.4 %all-to-all-start.7 = ((f32[4,24,1792]{2,1,0:T(8,128)}), f32[4,24,1792]{2,1,0:T(8,128)S(1)}, u32[]{:S(2)}, u32[]{:S(2)}) async-start(f32[4,24,1792]{2,1,0:T(8,128)} %fold.3), calls=%async_computation.7 | async-start | bytes 1376256 | tf_op jit(solution)/shard_map/all_to_all | solution.py:395
  243.3 6.7 %token_grad.1 = bf16[512,768]{1,0:T(8,128)(2,1)} custom-call(bf16[512,768]{1,0:T(8,128)(2,1)} %get-tuple-element.33.dq_ref, bf16[288,1536]{1,0:T(8,128)(2,1)} %get-tuple-element.41.dv_ref, bf16[768,2304]{1,0:T(8,128)(2,1)} %w_ref.5), custom_call_target="tpu_custom_call" | custom-call | tf_op jit(solution)/shard_map/token_grad/pallas_call | solution.py:340
  250.1 0.0 copy-done.5
  250.1 4.4 %all-to-all-done.7.refs_1_ = f32[4,24,1792]{2,1,0:T(8,128)S(1)} async-done(((f32[4,24,1792]{2,1,0:T(8,128)}), f32[4,24,1792]{2,1,0:T(8,128)S(1)}, u32[]{:S(2)}, u32[]{:S(2)}) %all-to-all-start.7) | async-done | bytes 688160 | tf_op jit(solution)/shard_map/all_to_all | solution.py:395
  254.4 0.0 copy-start.4
  254.4 0.8 copy-done.4
  255.3 2.0 finish.1
  257.3 1.4 copy.14
Async XLA Ops:
  6.1 7.9 %collective-permute-start = (f32[32,1536]{1,0:T(8,128)}, f32[32,1536]{1,0:T(8,128)S(1)}, u32[]{:S(2)}, u32[]{:S(2)}) collective-permute-start(f32[32,1536]{1,0:T(8,128)} %get-tuple-element.27), channel_id=1, source_target_pairs={{0,1},{1,2},{2,3},{3,4},{4,5},{5,6},{6,7},{7,8},{8,9},{9,10},{10,1... | collective-permute-start | bytes 589832 | tf_op jit(solution)/shard_map/ppermute | solution.py:399
  10.1 7.6 %collective-permute-start.1 = (f32[32,1536]{1,0:T(8,128)}, f32[32,1536]{1,0:T(8,128)S(1)}, u32[]{:S(2)}, u32[]{:S(2)}) collective-permute-start(f32[32,1536]{1,0:T(8,128)} %get-tuple-element.29), channel_id=1, source_target_pairs={{1,0},{2,1},{3,2},{4,3},{5,4},{6,5},{7,6},{8,7},{9,8},{10,9},{11,1... | collective-permute-start | bytes 589832 | tf_op jit(solution)/shard_map/ppermute | solution.py:403
  14.0 3.7 %copy-start.8 = (f32[32,1536]{1,0:T(8,128)}, f32[32,1536]{1,0:T(8,128)S(1)}, u32[]{:S(2)}) copy-start(f32[32,1536]{1,0:T(8,128)S(1)} %collective-permute-done.low_ref) | copy-start | bytes 589828
  17.7 0.7 copy-start.9
  21.3 22.4 %all-to-all-start.1 = ((bf16[32,32,384]{2,1,0:T(8,128)(2,1)}), bf16[32,32,384]{2,1,0:T(8,128)(2,1)S(1)}, u32[]{:S(2)}, u32[]{:S(2)}) async-start(bf16[32,32,384]{2,1,0:T(8,128)(2,1)} %bitcast.15), calls=%async_computation.1 | async-start | bytes 1572864 | tf_op jit(solution)/shard_map/all_to_all | solution.py:395
  43.7 21.9 %copy-start.3 = (bf16[32,32,384]{2,1,0:T(8,128)(2,1)}, bf16[32,32,384]{2,1,0:T(8,128)(2,1)S(1)}, u32[]{:S(2)}) copy-start(bf16[32,32,384]{2,1,0:T(8,128)(2,1)S(1)} %all-to-all-done.1) | copy-start | bytes 2359300
  118.2 17.4 %all-to-all-start.3 = ((bf16[32,32,384]{2,1,0:T(8,128)(2,1)}), bf16[32,32,384]{2,1,0:T(8,128)(2,1)S(1)}, u32[]{:S(2)}, u32[]{:S(2)}) async-start(bf16[32,32,384]{2,1,0:T(8,128)(2,1)} %bitcast.5), calls=%async_computation.3 | async-start | bytes 1572864 | tf_op jit(solution)/shard_map/all_to_all | solution.py:395
  135.7 0.9 copy-start.2
  136.5 41.3 %all-to-all-start.4 = ((bf16[32,24,1536]{2,1,0:T(8,128)(2,1)}), bf16[32,24,1536]{2,1,0:T(8,128)(2,1)S(1)}, u32[]{:S(2)}, u32[]{:S(2)}) async-start(bf16[32,24,1536]{2,1,0:T(8,128)(2,1)} %get-tuple-element.42), calls=%async_computation.4 | async-start | bytes 4718592 | tf_op jit(solution)/shard_map/all_to_all | solution.py:395
  143.2 20.6 %collective-permute-start.3 = (f32[32,1536]{1,0:T(8,128)}, f32[32,1536]{1,0:T(8,128)S(1)}, u32[]{:S(2)}, u32[]{:S(2)}) collective-permute-start(f32[32,1536]{1,0:T(8,128)} %get-tuple-element.37.own_ref), channel_id=1, source_target_pairs={{0,1},{1,2},{2,3},{3,4},{4,5},{5,6},{6,7},{7,8},{8,9},{9,10},{10,1... | collective-permute-start | bytes 589832 | tf_op jit(solution)/shard_map/ppermute | solution.py:399
  146.2 25.8 %collective-permute-start.2 = (f32[32,1536]{1,0:T(8,128)}, f32[32,1536]{1,0:T(8,128)S(1)}, u32[]{:S(2)}, u32[]{:S(2)}) collective-permute-start(f32[32,1536]{1,0:T(8,128)} %get-tuple-element.37.own_ref), channel_id=1, source_target_pairs={{1,0},{2,1},{3,2},{4,3},{5,4},{6,5},{7,6},{8,7},{9,8},{10,9},{11,1... | collective-permute-start | bytes 589832 | tf_op jit(solution)/shard_map/ppermute | solution.py:403
  163.7 8.2 %copy-start.6 = (f32[32,1536]{1,0:T(8,128)}, f32[32,1536]{1,0:T(8,128)S(1)}, u32[]{:S(2)}) copy-start(f32[32,1536]{1,0:T(8,128)S(1)} %collective-permute-done.3.low_ref) | copy-start | bytes 589828
  172.0 0.7 copy-start.7
  177.9 1.5 copy-start.1
  179.4 40.7 %all-to-all-start.6 = ((bf16[32,24,1792]{2,1,0:T(8,128)(2,1)}), bf16[32,24,1792]{2,1,0:T(8,128)(2,1)S(1)}, u32[]{:S(2)}, u32[]{:S(2)}) async-start(bf16[32,24,1792]{2,1,0:T(8,128)(2,1)} %get-tuple-element.43), calls=%async_computation.6 | async-start | bytes 5505024 | tf_op jit(solution)/shard_map/all_to_all | solution.py:395
  220.1 8.8 %copy-start = (bf16[32,24,1792]{2,1,0:T(8,128)(2,1)}, bf16[32,24,1792]{2,1,0:T(8,128)(2,1)S(1)}, u32[]{:S(2)}) copy-start(bf16[32,24,1792]{2,1,0:T(8,128)(2,1)S(1)} %all-to-all-done.6.parts_ref) | copy-start | bytes 8257540
  220.1 18.8 %all-to-all-start.5 = ((f32[4,24,1536]{2,1,0:T(8,128)}), f32[4,24,1536]{2,1,0:T(8,128)S(1)}, u32[]{:S(2)}, u32[]{:S(2)}) async-start(f32[4,24,1536]{2,1,0:T(8,128)} %fold.2), calls=%async_computation.5 | async-start | bytes 1179648 | tf_op jit(solution)/shard_map/all_to_all | solution.py:395
  238.9 11.2 %copy-start.5 = (f32[4,24,1536]{2,1,0:T(8,128)}, f32[4,24,1536]{2,1,0:T(8,128)S(1)}, u32[]{:S(2)}) copy-start(f32[4,24,1536]{2,1,0:T(8,128)S(1)} %all-to-all-done.5.refs_0_) | copy-start | bytes 1769476
  238.9 15.5 %all-to-all-start.7 = ((f32[4,24,1792]{2,1,0:T(8,128)}), f32[4,24,1792]{2,1,0:T(8,128)S(1)}, u32[]{:S(2)}, u32[]{:S(2)}) async-start(f32[4,24,1792]{2,1,0:T(8,128)} %fold.3), calls=%async_computation.7 | async-start | bytes 1376256 | tf_op jit(solution)/shard_map/all_to_all | solution.py:395
  254.4 0.8 copy-start.4

commit v2 on v1

--- a/solution.py
+++ b/solution.py
@@ -16,6 +16,7 @@
 TAPS = 288
 POS = 32
 EPSILON = 1e-05
+HALF_B = WIDTH + 128
 TM = ("tm_0", "tm_1", "tm_2")
 DP = ("dp_0", "dp_1")
 BF = jnp.bfloat16
@@ -79,7 +80,7 @@
     taps = dot(tt_ref[...], w_ref[...], 1, 0).astype(BF)
     taps_ref[...] = taps
     wide = taps.astype(F32)
-    kernel = over_heads(pk_ref[0])
+    kernel = over_heads(pk_ref[:, pl.program_id(0), :])
     for a, p_ref in enumerate((p0_ref, p1_ref, p2_ref)):
         total = None
         for be in range(9):
@@ -97,7 +98,7 @@
         in_specs=[
             pl.BlockSpec((HW, WIDTH), lambda s: (0, 0)),
             pl.BlockSpec((WIDTH, WIDTH), lambda s: (0, s + 1)),
-            pl.BlockSpec((1, 27, HEAD), lambda s: (s, 0, 0)),
+            pl.BlockSpec((27, 2, HEAD), lambda s: (0, 0, 0)),
         ],
         out_specs=[
             pl.BlockSpec((TAPS, WIDTH), lambda s: (0, s)),
@@ -118,12 +119,16 @@
     )(tokens, qkv_weight, pool_kernel)
 
 
-def query_kernel(tok_ref, w_ref, cot_ref, ow_ref, qd_ref):
+def query_kernel(tok_ref, w_ref, cot_ref, ow_ref, *refs):
+    *out_refs, group_ref = refs
     q = dot(tok_ref[...], w_ref[...], 1, 0).astype(BF)
     dm = dot(cot_ref[...], ow_ref[...], 1, 1).astype(BF)
     for g in range(GROUPS):
         lanes = slice(SPAN * g, SPAN * g + SPAN)
-        qd_ref[g] = jnp.concatenate([q[:, lanes], dm[:, lanes]], axis=-1)
+        group_ref[g] = jnp.concatenate([q[:, lanes], dm[:, lanes]], axis=-1)
+    mine = lax.axis_index("tm_1")
+    for step, out_ref in enumerate(out_refs):
+        out_ref[...] = group_ref[(mine + step) % GROUPS]
 
 
 def query_side(tokens, qkv_weight, cotangent, out_weight):
@@ -133,8 +138,9 @@
         query_kernel,
         grid=(1,),
         in_specs=[full, square, full, square],
-        out_specs=pl.BlockSpec((GROUPS, HW, 2 * SPAN), lambda i: (0, 0, 0)),
-        out_shape=jax.ShapeDtypeStruct((GROUPS, HW, 2 * SPAN), BF),
+        out_specs=[pl.BlockSpec((HW, 2 * SPAN), lambda i: (0, 0))] * GROUPS,
+        out_shape=[jax.ShapeDtypeStruct((HW, 2 * SPAN), BF)] * GROUPS,
+        scratch_shapes=[pltpu.VMEM((GROUPS, HW, 2 * SPAN), BF)],
         compiler_params=params("arbitrary"),
         name="query_side",
     )(tokens, qkv_weight, cotangent, out_weight)
@@ -171,19 +177,13 @@
     )(low, own, up, gain)
 
 
-def attention_kernel(qd_ref, kv_ref, md_ref, dkv_ref, acc_ref):
-    step = pl.program_id(0)
-
-    @pl.when(step == 0)
-    def _():
-        acc_ref[...] = jnp.zeros_like(acc_ref)
-
+def attend(qd, kv_ref, acc_ref):
     mixed, d_query = [], []
     for h in range(GROUP_HEADS):
         lo = slice(HEAD * h, HEAD * h + HEAD)
         hi = slice(SPAN + HEAD * h, SPAN + HEAD * h + HEAD)
-        q = qd_ref[0, :, lo]
-        dm = qd_ref[0, :, hi]
+        q = qd[:, lo]
+        dm = qd[:, hi]
         k = kv_ref[:, lo]
         v = kv_ref[:, hi]
         scores = dot(q * jnp.asarray(0.125, BF), k, 1, 1)
@@ -198,35 +198,48 @@
         d_scores = ((weights * inverse) * (dot(dm, v, 1, 1) - delta)).astype(BF)
         d_query.append((dot(d_scores, k, 1, 0) * 0.125 + wide).astype(BF))
         acc_ref[lo, :] += dot(q, d_scores, 0, 0) * 0.125
-    md_ref[0] = jnp.concatenate(mixed + d_query, axis=-1)
-
-    @pl.when(step == pl.num_programs(0) - 1)
-    def _():
-        dkv_ref[...] = jnp.transpose(acc_ref[...]).astype(BF)
-
-
-def attention(qd, kv):
-    frames, rows, lanes = qd.shape
-    keys = kv.shape[0]
-    return pl.pallas_call(
-        attention_kernel,
-        grid=(frames,),
-        in_specs=[
-            pl.BlockSpec((1, rows, lanes), lambda f: (f, 0, 0)),
-            pl.BlockSpec((keys, lanes), lambda f: (0, 0)),
-        ],
-        out_specs=[
-            pl.BlockSpec((1, rows, lanes), lambda f: (f, 0, 0)),
-            pl.BlockSpec((keys, lanes), lambda f: (0, 0)),
-        ],
-        out_shape=[
-            jax.ShapeDtypeStruct(qd.shape, BF),
-            jax.ShapeDtypeStruct(kv.shape, BF),
-        ],
-        scratch_shapes=[pltpu.VMEM((lanes, keys), F32)],
-        compiler_params=params("arbitrary"),
-        name="attention",
-    )(qd, kv)
+    return jnp.concatenate(mixed + d_query, axis=-1)
+
+
+def others_kernel(q0_ref, q1_ref, q2_ref, kv_ref, m0_ref, m1_ref, m2_ref, acc_ref, work_ref):
+    acc_ref[...] = jnp.zeros_like(acc_ref)
+    for n, ref in enumerate((q0_ref, q1_ref, q2_ref)):
+        work_ref[n] = ref[...]
+
+    def step(n, carry):
+        work_ref[n] = attend(work_ref[n], kv_ref, acc_ref)
+        return carry
+
+    lax.fori_loop(0, 3, step, 0)
+    for n, ref in enumerate((m0_ref, m1_ref, m2_ref)):
+        ref[...] = work_ref[n]
+
+
+def others(qds, kv):
+    block = jax.ShapeDtypeStruct(qds[0].shape, BF)
+    return pl.pallas_call(
+        others_kernel,
+        out_shape=[block, block, block, jax.ShapeDtypeStruct((kv.shape[1], kv.shape[0]), F32)],
+        scratch_shapes=[pltpu.VMEM((3,) + block.shape, BF)],
+        compiler_params=params(),
+        name="attend_others",
+    )(*qds, kv)
+
+
+def own_kernel(qd_ref, kv_ref, start_ref, md_ref, dkv_ref, acc_ref):
+    acc_ref[...] = start_ref[...]
+    md_ref[...] = attend(qd_ref[...], kv_ref, acc_ref)
+    dkv_ref[...] = jnp.transpose(acc_ref[...]).astype(BF)
+
+
+def own(qd, kv, start):
+    return pl.pallas_call(
+        own_kernel,
+        out_shape=[jax.ShapeDtypeStruct(qd.shape, BF), jax.ShapeDtypeStruct(kv.shape, BF)],
+        scratch_shapes=[pltpu.VMEM(start.shape, F32)],
+        compiler_params=params(),
+        name="attend_own",
+    )(qd, kv, start)
 
 
 def norm_back_kernel(parts_ref, normed_ref, inv_ref, gain_ref, d_ref, gsum_ref):
@@ -268,8 +281,8 @@
     return jnp.concatenate(out, axis=-1)
 
 
-def pool_back_kernel(up_ref, own_ref, low_ref, taps_ref, tt_ref, pk_ref, gsum_ref, dv_ref, pay_ref):
-    kernel = jnp.concatenate([over_heads(pk_ref[0]), over_heads(pk_ref[1])], axis=-1)
+def pool_back_kernel(up_ref, own_ref, low_ref, taps_ref, tt_ref, pk_ref, gsum_ref, dv_ref, *pays):
+    kernel = jnp.concatenate([over_heads(pk_ref[:, 0, :]), over_heads(pk_ref[:, 1, :])], axis=-1)
     sources = (up_ref[...], own_ref[...], low_ref[...])
     tap_rows = []
     for a in range(3):
@@ -287,9 +300,14 @@
     second = jnp.concatenate([small[24:28], jnp.zeros((20, 128), F32)], axis=0)
     extra = jnp.concatenate([first, second], axis=-1).astype(BF)
     grads = dot(tt_ref[...], dv_ref[...], 0, 0)
+    keep_ref, send_ref, half_ref = pays
     for f in range(32):
-        pay_ref[f, :, : 2 * WIDTH] = grads[24 * f : 24 * f + 24].astype(BF)
-        pay_ref[f, :, 2 * WIDTH :] = extra
+        rows = jnp.concatenate([grads[24 * f : 24 * f + 24].astype(BF), extra], axis=-1)
+        half_ref[0, f] = rows[:, :HALF_B]
+        half_ref[1, f] = rows[:, HALF_B:]
+    core = lax.axis_index("dp_1")
+    keep_ref[...] = half_ref[core]
+    send_ref[...] = half_ref[1 - core]
 
 
 def pool_back(up, own, low, taps, tap_tokens, pool_kernel, gain_sum):
@@ -297,37 +315,48 @@
         pool_back_kernel,
         out_shape=[
             jax.ShapeDtypeStruct((TAPS, 2 * WIDTH), BF),
-            jax.ShapeDtypeStruct((32, 24, 2 * WIDTH + 256), BF),
-        ],
+            jax.ShapeDtypeStruct((32, 24, HALF_B), BF),
+            jax.ShapeDtypeStruct((32, 24, HALF_B), BF),
+        ],
+        scratch_shapes=[pltpu.VMEM((2, 32, 24, HALF_B), BF)],
         compiler_params=params(),
         name="pool_back",
     )(up, own, low, taps, tap_tokens, pool_kernel, gain_sum)
 
 
-def output_kernel(md_ref, tok_ref, cot_ref, ow_ref, out_ref, dq_ref, pay_ref):
-    mixed = jnp.concatenate([md_ref[g, :, :SPAN] for g in range(GROUPS)], axis=-1)
-    dq = jnp.concatenate([md_ref[g, :, SPAN:] for g in range(GROUPS)], axis=-1)
+def output_kernel(m0_ref, m1_ref, m2_ref, m3_ref, tok_ref, cot_ref, ow_ref, *refs):
+    out_ref, dq_ref, keep_ref, send_ref, group_ref, half_ref = refs
+    mine = lax.axis_index("tm_1")
+    for step, ref in enumerate((m0_ref, m1_ref, m2_ref, m3_ref)):
+        group_ref[(mine + step) % GROUPS] = ref[...]
+    mixed = jnp.concatenate([group_ref[g, :, :SPAN] for g in range(GROUPS)], axis=-1)
+    dq = jnp.concatenate([group_ref[g, :, SPAN:] for g in range(GROUPS)], axis=-1)
     dq_ref[...] = dq
     out_ref[...] = dot(mixed, ow_ref[...], 1, 0).astype(BF)
     q_grad = dot(tok_ref[...], dq, 0, 0)
     o_grad = dot(mixed, cot_ref[...], 0, 0)
     for f in range(32):
         rows = slice(24 * f, 24 * f + 24)
-        pay_ref[f, :, :WIDTH] = q_grad[rows].astype(BF)
-        pay_ref[f, :, WIDTH:] = o_grad[rows].astype(BF)
-
-
-def output_side(md, tokens, cotangent, out_weight):
+        half_ref[0, f] = q_grad[rows].astype(BF)
+        half_ref[1, f] = o_grad[rows].astype(BF)
+    core = lax.axis_index("dp_1")
+    keep_ref[...] = half_ref[core]
+    send_ref[...] = half_ref[1 - core]
+
+
+def output_side(mds, tokens, cotangent, out_weight):
+    half = jax.ShapeDtypeStruct((32, 24, WIDTH), BF)
+    rows = jax.ShapeDtypeStruct((HW, WIDTH), BF)
     return pl.pallas_call(
         output_kernel,
-        out_shape=[
-            jax.ShapeDtypeStruct((HW, WIDTH), BF),
-            jax.ShapeDtypeStruct((HW, WIDTH), BF),
-            jax.ShapeDtypeStruct((32, 24, 2 * WIDTH), BF),
+        out_shape=[rows, rows, half, half],
+        scratch_shapes=[
+            pltpu.VMEM((GROUPS, HW, 2 * SPAN), BF),
+            pltpu.VMEM((2, 32, 24, WIDTH), BF),
         ],
         compiler_params=params(),
         name="output_side",
-    )(md, tokens, cotangent, out_weight)
+    )(*mds, tokens, cotangent, out_weight)
 
 
 def token_grad_kernel(dq_ref, dv_ref, w_ref, out_ref):
@@ -349,31 +378,34 @@
     total = parts_ref[0].astype(F32)
     for f in range(1, 32):
         total = total + parts_ref[f].astype(F32)
-    for c in range(4):
-        out_ref[c] = total
+    out_ref[...] = total
 
 
 def fold(parts):
     return pl.pallas_call(
         fold_kernel,
-        out_shape=jax.ShapeDtypeStruct((4,) + parts.shape[1:], F32),
+        out_shape=jax.ShapeDtypeStruct(parts.shape[1:], F32),
         compiler_params=params(),
         name="fold",
     )(parts)
 
 
-def finish_kernel(scale, a_ref, b_ref, qkv_ref, out_ref, kernel_ref, gain_ref):
-    a = (a_ref[0] + a_ref[1] + a_ref[2] + a_ref[3]) * scale
-    b = (b_ref[0] + b_ref[1] + b_ref[2] + b_ref[3]) * scale
-    qkv_ref[:, :WIDTH] = a[:, :WIDTH]
-    qkv_ref[:, WIDTH:] = b[:, : 2 * WIDTH]
-    out_ref[...] = a[:, WIDTH:]
-    first = b[:, 2 * WIDTH : 2 * WIDTH + 128]
-    second = b[:, 2 * WIDTH + 128 :]
+def finish_kernel(scale, a0, a1, a2, a3, b0, b1, b2, b3, qkv_ref, out_ref, kernel_ref, gain_ref, a_ref, b_ref):
+    core = lax.axis_index("dp_1")
+    a_ref[core] = (a0[...] + a2[...]) * scale
+    a_ref[1 - core] = (a1[...] + a3[...]) * scale
+    b_ref[core] = (b0[...] + b2[...]) * scale
+    b_ref[1 - core] = (b1[...] + b3[...]) * scale
+    qkv_ref[:, :WIDTH] = a_ref[0]
+    qkv_ref[:, WIDTH : WIDTH + HALF_B] = b_ref[0]
+    qkv_ref[:, WIDTH + HALF_B :] = b_ref[1, :, : 2 * WIDTH - HALF_B]
+    out_ref[...] = a_ref[1]
+    first = b_ref[1, :, HALF_B - 256 : HALF_B - 128]
+    second = b_ref[1, :, HALF_B - 128 :]
     for s in range(2):
         lanes = slice(HEAD * s, HEAD * s + HEAD)
-        kernel_ref[s, 0:24, :] = first[:, lanes]
-        kernel_ref[s, 24:27, :] = second[0:3, lanes]
+        kernel_ref[0:24, s, :] = first[:, lanes]
+        kernel_ref[24:27, s, :] = second[0:3, lanes]
         gain_ref[s : s + 1, :] = second[3:4, lanes]
 
 
@@ -383,12 +415,13 @@
         out_shape=[
             jax.ShapeDtypeStruct((24, 3 * WIDTH), F32),
             jax.ShapeDtypeStruct((24, WIDTH), F32),
-            jax.ShapeDtypeStruct((2, 27, HEAD), F32),
+            jax.ShapeDtypeStruct((27, 2, HEAD), F32),
             jax.ShapeDtypeStruct((2, HEAD), F32),
         ],
+        scratch_shapes=[pltpu.VMEM((2, 24, WIDTH), F32), pltpu.VMEM((2, 24, HALF_B), F32)],
         compiler_params=params(),
         name="finish",
-    )(a, b)
+    )(*a, *b)
 
 
 def exchange(array, axis):
@@ -403,42 +436,66 @@
     return lax.ppermute(array, TM, [(i + 1, i) for i in range(lax.axis_size(TM) - 1)])
 
 
-def shards(tokens, qkv_weight, pool_kernel, norm_gain, out_weight, out_cotangent):
+def rotate(array, steps):
+    return lax.ppermute(array, "tm_1", [(i, (i + steps) % GROUPS) for i in range(GROUPS)])
+
+
+def core_sum(keep, send):
+    other = lax.ppermute(send, "dp_1", [(0, 1), (1, 0)])
+    return (keep.astype(F32) + other.astype(F32)).astype(BF)
+
+
+def copies(array):
+    return [array] + [lax.ppermute(array, DP, [(i, i ^ k) for i in range(4)]) for k in (1, 2, 3)]
+
+
+def block(tokens, qkv_weight, pool_kernel, norm_gain, out_weight, out_cotangent):
     shape = tokens.shape
     token_rows = tokens.reshape(HW, WIDTH)
     cotangent_rows = out_cotangent.reshape(HW, WIDTH)
+    pool_kernel = jnp.transpose(pool_kernel, (1, 0, 2))
     taps, tap_tokens, part0, part1, part2 = tap_sums(token_rows, qkv_weight, pool_kernel)
     low = to_next(part0)
     up = to_previous(part2)
-    qd = query_side(token_rows, qkv_weight, cotangent_rows, out_weight)
-    qd = exchange(qd, "tm_1")
+    qd, *qds = query_side(token_rows, qkv_weight, cotangent_rows, out_weight)
+    received = [rotate(q, k) for k, q in zip((1, 2, 3), qds)]
     kv, normed, inv = norm_side(low, part1, up, norm_gain)
     kv = exchange(kv.reshape(32, POS, 2 * SPAN), TM)
-    md, dkv = attention(qd, kv.reshape(32 * POS, 2 * SPAN))
+    kv = kv.reshape(32 * POS, 2 * SPAN)
+    *mds, start = others(received, kv)
+    mds = [rotate(m, -k) for k, m in zip((1, 2, 3), mds)]
+    md, dkv = own(qd, kv, start)
     parts = exchange(dkv.reshape(32, POS, 2 * SPAN), TM)
-    md = exchange(md, "tm_1")
-    d_summed, gain_sum = norm_back(
-        parts.reshape(2, GROUPS, 4, POS, 2 * SPAN), normed, inv, norm_gain
-    )
+    parts = parts.reshape(2, GROUPS, 4, POS, 2 * SPAN)
+    d_summed, gain_sum = norm_back(parts, normed, inv, norm_gain)
     d_low = to_next(d_summed)
     d_up = to_previous(d_summed)
-    block_out, dq, pay_a = output_side(md, token_rows, cotangent_rows, out_weight)
-    pay_a = fold(exchange(pay_a, TM))
-    pay_a = exchange(pay_a, DP)
-    dv, pay_b = pool_back(d_up, d_summed, d_low, taps, tap_tokens, pool_kernel, gain_sum)
-    pay_b = fold(exchange(pay_b, TM))
+    block_out, dq, *pay_a = output_side([md] + mds, token_rows, cotangent_rows, out_weight)
+    pay_a = core_sum(*pay_a)
+    pay_a = exchange(pay_a, TM)
+    pay_a = copies(fold(pay_a))
+    dv, *pay_b = pool_back(d_up, d_summed, d_low, taps, tap_tokens, pool_kernel, gain_sum)
+    pay_b = core_sum(*pay_b)
+    pay_b = exchange(pay_b, TM)
+    pay_b = copies(fold(pay_b))
     grad_tokens = token_grad(dq, dv, qkv_weight)
-    pay_b = exchange(pay_b, DP)
     scale = float(HW * lax.axis_size(DP) * lax.axis_size(TM)) ** (-0.5)
-    grads = finish(pay_a, pay_b, scale)
-    return (block_out.reshape(shape), grad_tokens.reshape(shape), *grads)
+    qkv_grad, out_grad, kernel_grad, gain_grad = finish(pay_a, pay_b, scale)
+    return (
+        block_out.reshape(shape),
+        grad_tokens.reshape(shape),
+        qkv_grad,
+        out_grad,
+        jnp.transpose(kernel_grad, (1, 0, 2)),
+        gain_grad,
+    )
 
 
 def solution(mesh):
     torus = Mesh(mesh.devices.reshape(2, 2, 2, 4, 4), DP + TM)
     placed = (P(DP, TM, None, None), P(), P(), P(), P(), P(DP, TM, None, None))
     return jax.shard_map(
-        shards,
+        block,
         mesh=torus,
         in_specs=placed,
         out_specs=(

time: 260 us -> 215 us (0.83)
  blocking collectives: 42.6 us -> 0 us
  waiting for transfers between devices: 84 us -> 59 us
  starting transfers between devices: 52.3 us -> 71.4 us
  other arithmetic: 0 us -> 4.11 us
    all_to_all x2 -> x0, blocking collectives: 42.6 us -> none  [exchange(): return lax.all_to_all(array, axis, split_axis=0, concat_axis=0, tiled=True)]
    ppermute x0 -> x14, starting transfers between devices: none -> 27.8 us  [the longest x6 14.2 us: copies(): lax.ppermute(array, DP, [(i, i ^ k) for i in range(4)])]
    all_to_all x6 -> x4, waiting for transfers between devices: 53.2 us -> 26.9 us  [exchange(): return lax.all_to_all(array, axis, split_axis=0, concat_axis=0, tiled=True)]
    ppermute x0 -> x14, waiting for transfers between devices: none -> 20.7 us  [the longest x6 20.7 us: rotate(): lax.ppermute(array, 'tm_1', [(i, (i + steps) % GROUPS) for i in range(GRO...]
    ppermute x2, waiting for transfers between devices: 18.8 us -> 3.95 us  [to_next(): lax.ppermute(array, TM, [(i, i + 1) for i in range(lax.axis_size(TM) - 1)])]
    all_to_all x6 -> x4, starting transfers between devices: 42.7 us -> 33.4 us  [exchange(): return lax.all_to_all(array, axis, split_axis=0, concat_axis=0, tiled=True)]
    ppermute x2, waiting for transfers between devices: 12 us -> 7.46 us  [to_previous(): lax.ppermute(array, TM, [(i + 1, i) for i in range(lax.axis_size(TM) - 1)])]
    convert_element_type x0 -> x2, other arithmetic: none -> 4.11 us  [core_sum(): return (keep.astype(F32) + other.astype(F32)).astype(BF)]
  transfers between devices with their start and end apart: 10 -> 22, of which waited for: 9 -> 9; matrix products, arithmetic and copies ran while one was open for 0% -> 2% of each run, Pallas kernels for 12% -> 18%
where the time goes in v2:
time: 215 us
  Pallas kernels  71.7 us (33%)
  starting transfers between devices  71.4 us (33%)
  waiting for transfers between devices  59 us (27%)
  local copies, waits for them, and re-layouts  7.56 us (4%)
  other arithmetic  4.11 us (2%)
    all_to_all x4, starting transfers between devices, exchange(): return lax.all_to_all(array, axis, split_axis=0, concat_axis=0, tiled=True)  33.4 us
    all_to_all x4, waiting for transfers between devices, exchange(): return lax.all_to_all(array, axis, split_axis=0, concat_axis=0, tiled=True)  26.9 us
    pallas_call x1, Pallas kernels, others(): pl.pallas_call(others_kernel, out_shape=[block, block, block, jax.ShapeDt...  23 us
    ppermute x6, waiting for transfers between devices, rotate(): lax.ppermute(array, 'tm_1', [(i, (i + steps) % GROUPS) for i in range(GRO...  20.7 us
    ppermute x6, starting transfers between devices, copies(): lax.ppermute(array, DP, [(i, i ^ k) for i in range(4)])  14.2 us
    pallas_call x1, Pallas kernels, own(): pl.pallas_call(own_kernel, out_shape=[jax.ShapeDtypeStruct(qd.shape, BF),...  9.54 us
    ppermute x6, starting transfers between devices, rotate(): lax.ppermute(array, 'tm_1', [(i, (i + steps) % GROUPS) for i in range(GRO...  8.52 us
    unnamed x46, local copies, waits for them, and re-layouts  7.56 us
  transfers between devices with their start and end apart: 22, of which 9 were waited for; matrix products, arithmetic and copies ran while one was open for 2% of the time, Pallas kernels for 18%

profile of v2, /device:TPU:1, one launch (start us, length us, event | category | flops | bytes accessed | tf_op | source)
XLA Modules:
  0.0 214.6 jit_solution(18211474496329278938)
XLA Ops:
  0.6 4.1 %tap_sums.1 = (bf16[288,1536]{1,0:T(8,128)(2,1)}, bf16[288,768]{1,0:T(8,128)(2,1)}, f32[32,1536]{1,0:T(8,128)}, f32[32,1536]{1,0:T(8,128)}, f32[32,1536]{1,0:T(8,128)}) custom-call(bf16[512,768]{1,0:T(8,128)(2,1)} %bitcast.12, bf16[768,2304]{1,0:T(8,128)(2,1)} %w_ref.5, f32[27,2,64]{2,1,0:T(2,128)} %bitcast.21), custom_call_target="tpu_custom_call" | custom-call | tf_op jit(solution)/shard_map/tap_sums/pallas_call | solution.py:95
  4.7 4.0 %collective-permute-start = (f32[32,1536]{1,0:T(8,128)}, f32[32,1536]{1,0:T(8,128)S(1)}, u32[]{:S(2)}, u32[]{:S(2)}) collective-permute-start(f32[32,1536]{1,0:T(8,128)} %get-tuple-element.38), channel_id=1, source_target_pairs={{0,1},{1,2},{2,3},{3,4},{4,5},{5,6},{6,7},{7,8},{8,9},{9,10},{10,1... | collective-permute-start | bytes 589832 | tf_op jit(solution)/shard_map/ppermute | solution.py:432
  8.8 1.3 collective-permute-start.1
  10.1 2.6 %collective-permute-done.low_ref = f32[32,1536]{1,0:T(8,128)S(1)} collective-permute-done((f32[32,1536]{1,0:T(8,128)}, f32[32,1536]{1,0:T(8,128)S(1)}, u32[]{:S(2)}, u32[]{:S(2)}) %collective-permute-start) | collective-permute-done | bytes 196640 | tf_op jit(solution)/shard_map/ppermute | solution.py:432
  12.6 3.7 %collective-permute-done.1.up_ref = f32[32,1536]{1,0:T(8,128)S(1)} collective-permute-done((f32[32,1536]{1,0:T(8,128)}, f32[32,1536]{1,0:T(8,128)S(1)}, u32[]{:S(2)}, u32[]{:S(2)}) %collective-permute-start.1) | collective-permute-done | bytes 196640 | tf_op jit(solution)/shard_map/ppermute | solution.py:436
  16.4 0.7 copy-done.16
  17.0 3.0 %norm_side.1 = (bf16[2,4,4,32,384]{4,3,2,1,0:T(8,128)(2,1)}, f32[32,1536]{1,0:T(8,128)}, f32[32,1536]{1,0:T(8,128)}) custom-call(f32[32,1536]{1,0:T(8,128)} %copy-done.15, f32[32,1536]{1,0:T(8,128)} %get-tuple-element.39.own_ref, f32[32,1536]{1,0:T(8,128)} %copy-done.16, f32[2,64]{1,0:T(2,128)} %gain_ref.3), custom_call_target="tpu_custom_call" | custom-call | tf_op jit(solution)/shard_map/norm_side/pallas_call | solution.py:172
  20.0 10.7 %all-to-all-start = ((bf16[32,32,384]{2,1,0:T(8,128)(2,1)}), bf16[32,32,384]{2,1,0:T(8,128)(2,1)S(1)}, u32[]{:S(2)}, u32[]{:S(2)}) async-start(bf16[32,32,384]{2,1,0:T(8,128)(2,1)} %bitcast.18), calls=%async_computation | async-start | bytes 1572864 | tf_op jit(solution)/shard_map/all_to_all | solution.py:428
  30.7 4.7 %query_side.1 = (bf16[512,384]{1,0:T(8,128)(2,1)}, bf16[512,384]{1,0:T(8,128)(2,1)}, bf16[512,384]{1,0:T(8,128)(2,1)}, bf16[512,384]{1,0:T(8,128)(2,1)}) custom-call(bf16[512,768]{1,0:T(8,128)(2,1)} %bitcast.13, bf16[768,2304]{1,0:T(8,128)(2,1)} %w_ref.5, bf16[512,768]{1,0:T(8,128)(2,1)} %bitcast.16, bf16[768,768]{1,0:T(8,128)(2,1)} %ow_ref.3), custom_call_target="tpu_custom_call" | custom-call | tf_op jit(solution)/shard_map/query_side/pallas_call | solution.py:137
  35.5 1.2 collective-permute-start.2
  36.7 2.4 %collective-permute-start.3 = (bf16[512,384]{1,0:T(8,128)(2,1)}, bf16[512,384]{1,0:T(8,128)(2,1)S(1)}, u32[]{:S(2)}, u32[]{:S(2)}) collective-permute-start(bf16[512,384]{1,0:T(8,128)(2,1)} %get-tuple-element.43), channel_id=1, source_target_pairs={{0,8},{4,12},{8,0},{12,4},{1,9},{5,13},{9,1},{13,5},{2,10},{6,14},... | collective-permute-start | bytes 1179656 | tf_op jit(solution)/shard_map/ppermute | solution.py:440
  39.1 1.2 collective-permute-start.4
  40.3 10.9 %collective-permute-done.2.q0_ref = bf16[512,384]{1,0:T(8,128)(2,1)S(1)} collective-permute-done((bf16[512,384]{1,0:T(8,128)(2,1)}, bf16[512,384]{1,0:T(8,128)(2,1)S(1)}, u32[]{:S(2)}, u32[]{:S(2)}) %collective-permute-start.2) | collective-permute-done | bytes 393248 | tf_op jit(solution)/shard_map/ppermute | solution.py:440
  51.2 6.4 %collective-permute-done.3.q1_ref = bf16[512,384]{1,0:T(8,128)(2,1)S(1)} collective-permute-done((bf16[512,384]{1,0:T(8,128)(2,1)}, bf16[512,384]{1,0:T(8,128)(2,1)S(1)}, u32[]{:S(2)}, u32[]{:S(2)}) %collective-permute-start.3) | collective-permute-done | bytes 393248 | tf_op jit(solution)/shard_map/ppermute | solution.py:440
  57.6 0.0 copy-start
  57.6 0.8 copy-done.10
  58.3 0.1 copy-done.11
  58.5 0.2 copy-done
  58.7 23.0 %attend_others.1 = (bf16[512,384]{1,0:T(8,128)(2,1)}, bf16[512,384]{1,0:T(8,128)(2,1)}, bf16[512,384]{1,0:T(8,128)(2,1)}, f32[384,1024]{1,0:T(8,128)}) custom-call(bf16[512,384]{1,0:T(8,128)(2,1)} %copy-done.9, bf16[512,384]{1,0:T(8,128)(2,1)} %copy-done.10, bf16[512,384]{1,0:T(8,128)(2,1)} %copy-done.11, bf16[1024,384]{1,0:T(8,128)(2,1)} %bitcast.10), custom_call_target="tpu_custom_call" | custom-call | tf_op jit(solution)/shard_map/attend_others/pallas_call | solution.py:220
  81.7 3.1 %collective-permute-start.5 = (bf16[512,384]{1,0:T(8,128)(2,1)}, bf16[512,384]{1,0:T(8,128)(2,1)S(1)}, u32[]{:S(2)}, u32[]{:S(2)}) collective-permute-start(bf16[512,384]{1,0:T(8,128)(2,1)} %get-tuple-element.47), channel_id=1, source_target_pairs={{0,12},{4,0},{8,4},{12,8},{1,13},{5,1},{9,5},{13,9},{2,14},{6,2},{... | collective-permute-start | bytes 1179656 | tf_op jit(solution)/shard_map/ppermute | solution.py:440
  84.8 0.2 collective-permute-start.6
  85.0 0.4 collective-permute-start.7
  85.4 9.5 %attend_own.1 = (bf16[512,384]{1,0:T(8,128)(2,1)}, bf16[1024,384]{1,0:T(8,128)(2,1)}) custom-call(bf16[512,384]{1,0:T(8,128)(2,1)} %get-tuple-element.37.qd_ref, bf16[1024,384]{1,0:T(8,128)(2,1)} %bitcast.11, f32[384,1024]{1,0:T(8,128)} %get-tuple-element.45.start_ref), custom_call_target="tpu_custom_call" | custom-call | tf_op jit(solution)/shard_map/attend_own/pallas_call | solution.py:236
  95.0 7.2 %all-to-all-start.1 = ((bf16[32,32,384]{2,1,0:T(8,128)(2,1)}), bf16[32,32,384]{2,1,0:T(8,128)(2,1)S(1)}, u32[]{:S(2)}, u32[]{:S(2)}) async-start(bf16[32,32,384]{2,1,0:T(8,128)(2,1)} %bitcast.19), calls=%async_computation.1 | async-start | bytes 1572864 | tf_op jit(solution)/shard_map/all_to_all | solution.py:428
  102.2 0.0 collective-permute-done.5.m1_ref
  102.2 0.0 copy-start.6
  102.2 0.0 collective-permute-done.6.m2_ref
  102.2 3.5 %collective-permute-done.7.m3_ref = bf16[512,384]{1,0:T(8,128)(2,1)S(1)} collective-permute-done((bf16[512,384]{1,0:T(8,128)(2,1)}, bf16[512,384]{1,0:T(8,128)(2,1)S(1)}, u32[]{:S(2)}, u32[]{:S(2)}) %collective-permute-start.7) | collective-permute-done | bytes 393248 | tf_op jit(solution)/shard_map/ppermute | solution.py:440
  105.7 0.8 copy-done.8
  106.5 6.3 %output_side.1 = (bf16[512,768]{1,0:T(8,128)(2,1)}, bf16[512,768]{1,0:T(8,128)(2,1)}, bf16[32,24,768]{2,1,0:T(8,128)(2,1)}, bf16[32,24,768]{2,1,0:T(8,128)(2,1)}) custom-call(bf16[512,384]{1,0:T(8,128)(2,1)} %get-tuple-element.46.m0_ref, bf16[512,384]{1,0:T(8,128)(2,1)} %copy-done.6, bf16[512,384]{1,0:T(8,128)(2,1)} %copy-done.7, ...), custom_call_target="tpu_custom_call" | custom-call | tf_op jit(solution)/shard_map/output_side/pallas_call | solution.py:350
  112.8 0.6 collective-permute-start.10
  113.4 0.0 all-to-all-done.1
  113.4 0.9 copy-done.3
  114.2 2.6 %norm_back.1 = (f32[32,1536]{1,0:T(8,128)}, f32[1,1536]{1,0:T(1,128)}) custom-call(bf16[2,4,4,32,384]{4,3,2,1,0:T(8,128)(2,1)} %bitcast.15, f32[32,1536]{1,0:T(8,128)} %get-tuple-element.53.normed_ref, f32[32,1536]{1,0:T(8,128)} %get-tuple-element.54.inv_ref, f32[2,64]{1,0:T(2,128)} %gain_ref.3), custom_call_target="tpu_custom_call" | custom-call | tf_op jit(solution)/shard_map/norm_back/pallas_call | solution.py:263
  116.9 3.4 %collective-permute-start.9 = (f32[32,1536]{1,0:T(8,128)}, f32[32,1536]{1,0:T(8,128)S(1)}, u32[]{:S(2)}, u32[]{:S(2)}) collective-permute-start(f32[32,1536]{1,0:T(8,128)} %get-tuple-element.55.own_ref), channel_id=1, source_target_pairs={{0,1},{1,2},{2,3},{3,4},{4,5},{5,6},{6,7},{7,8},{8,9},{9,10},{10,1... | collective-permute-start | bytes 589832 | tf_op jit(solution)/shard_map/ppermute | solution.py:432
  120.2 1.5 collective-permute-start.8
  121.8 1.4 collective-permute-done.9.low_ref
  123.2 3.7 %collective-permute-done.8.up_ref = f32[32,1536]{1,0:T(8,128)S(1)} collective-permute-done((f32[32,1536]{1,0:T(8,128)}, f32[32,1536]{1,0:T(8,128)S(1)}, u32[]{:S(2)}, u32[]{:S(2)}) %collective-permute-start.8) | collective-permute-done | bytes 196640 | tf_op jit(solution)/shard_map/ppermute | solution.py:436
  126.9 0.7 copy-done.14
  127.6 5.5 %pool_back.1 = (bf16[288,1536]{1,0:T(8,128)(2,1)}, bf16[32,24,896]{2,1,0:T(8,128)(2,1)}, bf16[32,24,896]{2,1,0:T(8,128)(2,1)}) custom-call(f32[32,1536]{1,0:T(8,128)} %copy-done.14, f32[32,1536]{1,0:T(8,128)} %get-tuple-element.55.own_ref, f32[32,1536]{1,0:T(8,128)} %copy-done.13, bf16[288,1536]{1,0:T(8,128)(2,1)} %get-tuple-element.56.taps_ref, ...), custom_call_target="tpu_custom_call" | custom-call | tf_op jit(solution)/shard_map/pool_back/pallas_call | solution.py:314
  133.1 4.5 %collective-permute-start.14 = (bf16[32,24,896]{2,1,0:T(8,128)(2,1)}, bf16[32,24,896]{2,1,0:T(8,128)(2,1)}, u32[]{:S(2)}, u32[]{:S(2)}) collective-permute-start(bf16[32,24,896]{2,1,0:T(8,128)(2,1)} %get-tuple-element.63), channel_id=1, source_target_pairs={{0,32},{32,0},{1,33},{33,1},{2,34},{34,2},{3,35},{35,3},{4,36},{36... | collective-permute-start | bytes 4128776 | tf_op jit(solution)/shard_map/ppermute | solution.py:444
  137.5 1.3 add_convert_fusion.1
  138.9 10.8 %all-to-all-start.2 = ((bf16[32,24,768]{2,1,0:T(8,128)(2,1)}), bf16[32,24,768]{2,1,0:T(8,128)(2,1)S(1)}, u32[]{:S(2)}, u32[]{:S(2)}) async-start(bf16[32,24,768]{2,1,0:T(8,128)(2,1)} %add_convert_fusion.1), calls=%async_computation.2 | async-start | bytes 2359296 | tf_op jit(solution)/shard_map/all_to_all | solution.py:428
  149.7 0.0 collective-permute-done.14
  149.7 2.8 %add_convert_fusion = bf16[32,24,896]{2,1,0:T(8,128)(2,1)} fusion(bf16[32,24,896]{2,1,0:T(8,128)(2,1)} %collective-permute-done.14, bf16[32,24,896]{2,1,0:T(8,128)(2,1)S(1)} %copy-done.4), kind=kLoop, calls=%fused_computation | loop fusion | flops 2752512 | bytes 4128768 | tf_op jit(solution)/shard_map/convert_element_type | solution.py:445
  152.5 15.1 %all-to-all-done.2.parts_ref = bf16[32,24,768]{2,1,0:T(8,128)(2,1)S(1)} async-done(((bf16[32,24,768]{2,1,0:T(8,128)(2,1)}), bf16[32,24,768]{2,1,0:T(8,128)(2,1)S(1)}, u32[]{:S(2)}, u32[]{:S(2)}) %all-to-all-start.2) | async-done | bytes 1179680 | tf_op jit(solution)/shard_map/all_to_all | solution.py:428
  167.6 1.0 copy-done.2
  168.6 4.6 %all-to-all-start.3 = ((bf16[32,24,896]{2,1,0:T(8,128)(2,1)}), bf16[32,24,896]{2,1,0:T(8,128)(2,1)S(1)}, u32[]{:S(2)}, u32[]{:S(2)}) async-start(bf16[32,24,896]{2,1,0:T(8,128)(2,1)} %add_convert_fusion), calls=%async_computation.3 | async-start | bytes 2752512 | tf_op jit(solution)/shard_map/all_to_all | solution.py:428
  173.2 2.1 fold.2.refs_0_
  175.3 4.5 %collective-permute-start.13 = (f32[24,768]{1,0:T(8,128)}, f32[24,768]{1,0:T(8,128)S(1)}, u32[]{:S(2)}, u32[]{:S(2)}) collective-permute-start(f32[24,768]{1,0:T(8,128)} %fold.2.refs_0_), channel_id=1, source_target_pairs={{0,96},{32,64},{64,32},{96,0},{1,97},{33,65},{65,33},{97,1},{2,98}... | collective-permute-start | bytes 221192 | tf_op jit(solution)/shard_map/ppermute | solution.py:449
  179.8 11.7 %all-to-all-done.3.parts_ref = bf16[32,24,896]{2,1,0:T(8,128)(2,1)S(1)} async-done(((bf16[32,24,896]{2,1,0:T(8,128)(2,1)}), bf16[32,24,896]{2,1,0:T(8,128)(2,1)S(1)}, u32[]{:S(2)}, u32[]{:S(2)}) %all-to-all-start.3) | async-done | bytes 1376288 | tf_op jit(solution)/shard_map/all_to_all | solution.py:428
  191.5 1.1 copy-done.1
  192.6 2.2 %fold.3.refs_4_ = f32[24,896]{1,0:T(8,128)} custom-call(bf16[32,24,896]{2,1,0:T(8,128)(2,1)} %copy-done.1), custom_call_target="tpu_custom_call" | custom-call | tf_op jit(solution)/shard_map/fold/pallas_call | solution.py:385
  194.8 6.0 %collective-permute-start.17 = (f32[24,896]{1,0:T(8,128)}, f32[24,896]{1,0:T(8,128)S(1)}, u32[]{:S(2)}, u32[]{:S(2)}) collective-permute-start(f32[24,896]{1,0:T(8,128)} %fold.3.refs_4_), channel_id=1, source_target_pairs={{0,96},{32,64},{64,32},{96,0},{1,97},{33,65},{65,33},{97,1},{2,98}... | collective-permute-start | bytes 258056 | tf_op jit(solution)/shard_map/ppermute | solution.py:449
  200.8 0.4 collective-permute-start.15
  201.2 2.6 %collective-permute-start.12 = (f32[24,768]{1,0:T(8,128)S(1)}, f32[24,768]{1,0:T(8,128)S(1)}, u32[]{:S(2)}, u32[]{:S(2)}) collective-permute-start(f32[24,768]{1,0:T(8,128)S(1)} %copy-done.12), channel_id=1, source_target_pairs={{0,64},{32,96},{64,0},{96,32},{1,65},{33,97},{65,1},{97,33},{2,66}... | collective-permute-start | bytes 221192 | tf_op jit(solution)/shard_map/ppermute | solution.py:449
  203.7 0.8 collective-permute-start.11
  204.5 6.7 %token_grad.1 = bf16[512,768]{1,0:T(8,128)(2,1)} custom-call(bf16[512,768]{1,0:T(8,128)(2,1)} %get-tuple-element.51.dq_ref, bf16[288,1536]{1,0:T(8,128)(2,1)} %get-tuple-element.59.dv_ref, bf16[768,2304]{1,0:T(8,128)(2,1)} %w_ref.5), custom_call_target="tpu_custom_call" | custom-call | tf_op jit(solution)/shard_map/token_grad/pallas_call | solution.py:369
  211.3 0.6 copy-done.21
  211.9 0.0 copy-done.22
  211.9 0.0 copy-done.17
  212.0 0.0 copy-done.18
  212.0 0.6 copy-done.19
  212.6 1.9 finish.1
  (40 shorter events, 0.1 us)
Async XLA Ops:
  4.7 7.9 %collective-permute-start = (f32[32,1536]{1,0:T(8,128)}, f32[32,1536]{1,0:T(8,128)S(1)}, u32[]{:S(2)}, u32[]{:S(2)}) collective-permute-start(f32[32,1536]{1,0:T(8,128)} %get-tuple-element.38), channel_id=1, source_target_pairs={{0,1},{1,2},{2,3},{3,4},{4,5},{5,6},{6,7},{7,8},{8,9},{9,10},{10,1... | collective-permute-start | bytes 589832 | tf_op jit(solution)/shard_map/ppermute | solution.py:432
  8.8 7.6 %collective-permute-start.1 = (f32[32,1536]{1,0:T(8,128)}, f32[32,1536]{1,0:T(8,128)S(1)}, u32[]{:S(2)}, u32[]{:S(2)}) collective-permute-start(f32[32,1536]{1,0:T(8,128)} %get-tuple-element.40), channel_id=1, source_target_pairs={{1,0},{2,1},{3,2},{4,3},{5,4},{6,5},{7,6},{8,7},{9,8},{10,9},{11,1... | collective-permute-start | bytes 589832 | tf_op jit(solution)/shard_map/ppermute | solution.py:436
  12.6 3.7 %copy-start.15 = (f32[32,1536]{1,0:T(8,128)}, f32[32,1536]{1,0:T(8,128)S(1)}, u32[]{:S(2)}) copy-start(f32[32,1536]{1,0:T(8,128)S(1)} %collective-permute-done.low_ref) | copy-start | bytes 589828
  16.4 0.7 copy-start.16
  20.0 37.6 %all-to-all-start = ((bf16[32,32,384]{2,1,0:T(8,128)(2,1)}), bf16[32,32,384]{2,1,0:T(8,128)(2,1)S(1)}, u32[]{:S(2)}, u32[]{:S(2)}) async-start(bf16[32,32,384]{2,1,0:T(8,128)(2,1)} %bitcast.18), calls=%async_computation | async-start | bytes 1572864 | tf_op jit(solution)/shard_map/all_to_all | solution.py:428
  35.5 15.7 %collective-permute-start.2 = (bf16[512,384]{1,0:T(8,128)(2,1)}, bf16[512,384]{1,0:T(8,128)(2,1)S(1)}, u32[]{:S(2)}, u32[]{:S(2)}) collective-permute-start(bf16[512,384]{1,0:T(8,128)(2,1)} %get-tuple-element.42), channel_id=1, source_target_pairs={{0,4},{4,8},{8,12},{12,0},{1,5},{5,9},{9,13},{13,1},{2,6},{6,10},{... | collective-permute-start | bytes 1179656 | tf_op jit(solution)/shard_map/ppermute | solution.py:440
  36.7 20.8 %collective-permute-start.3 = (bf16[512,384]{1,0:T(8,128)(2,1)}, bf16[512,384]{1,0:T(8,128)(2,1)S(1)}, u32[]{:S(2)}, u32[]{:S(2)}) collective-permute-start(bf16[512,384]{1,0:T(8,128)(2,1)} %get-tuple-element.43), channel_id=1, source_target_pairs={{0,8},{4,12},{8,0},{12,4},{1,9},{5,13},{9,1},{13,5},{2,10},{6,14},... | collective-permute-start | bytes 1179656 | tf_op jit(solution)/shard_map/ppermute | solution.py:440
  39.1 18.4 %collective-permute-start.4 = (bf16[512,384]{1,0:T(8,128)(2,1)}, bf16[512,384]{1,0:T(8,128)(2,1)S(1)}, u32[]{:S(2)}, u32[]{:S(2)}) collective-permute-start(bf16[512,384]{1,0:T(8,128)(2,1)} %get-tuple-element.44), channel_id=1, source_target_pairs={{0,12},{4,0},{8,4},{12,8},{1,13},{5,1},{9,5},{13,9},{2,14},{6,2},{... | collective-permute-start | bytes 1179656 | tf_op jit(solution)/shard_map/ppermute | solution.py:440
  51.2 6.4 %copy-start.9 = (bf16[512,384]{1,0:T(8,128)(2,1)}, bf16[512,384]{1,0:T(8,128)(2,1)S(1)}, u32[]{:S(2)}) copy-start(bf16[512,384]{1,0:T(8,128)(2,1)S(1)} %collective-permute-done.2.q0_ref) | copy-start | bytes 1179652
  57.5 0.8 copy-start.10
  57.6 0.9 copy-start.11
  57.6 1.1 copy-start
  81.7 20.5 %collective-permute-start.5 = (bf16[512,384]{1,0:T(8,128)(2,1)}, bf16[512,384]{1,0:T(8,128)(2,1)S(1)}, u32[]{:S(2)}, u32[]{:S(2)}) collective-permute-start(bf16[512,384]{1,0:T(8,128)(2,1)} %get-tuple-element.47), channel_id=1, source_target_pairs={{0,12},{4,0},{8,4},{12,8},{1,13},{5,1},{9,5},{13,9},{2,14},{6,2},{... | collective-permute-start | bytes 1179656 | tf_op jit(solution)/shard_map/ppermute | solution.py:440
  84.8 17.4 %collective-permute-start.6 = (bf16[512,384]{1,0:T(8,128)(2,1)}, bf16[512,384]{1,0:T(8,128)(2,1)S(1)}, u32[]{:S(2)}, u32[]{:S(2)}) collective-permute-start(bf16[512,384]{1,0:T(8,128)(2,1)} %get-tuple-element.48), channel_id=1, source_target_pairs={{0,8},{4,12},{8,0},{12,4},{1,9},{5,13},{9,1},{13,5},{2,10},{6,14},... | collective-permute-start | bytes 1179656 | tf_op jit(solution)/shard_map/ppermute | solution.py:440
  85.0 20.7 %collective-permute-start.7 = (bf16[512,384]{1,0:T(8,128)(2,1)}, bf16[512,384]{1,0:T(8,128)(2,1)S(1)}, u32[]{:S(2)}, u32[]{:S(2)}) collective-permute-start(bf16[512,384]{1,0:T(8,128)(2,1)} %get-tuple-element.49), channel_id=1, source_target_pairs={{0,4},{4,8},{8,12},{12,0},{1,5},{5,9},{9,13},{13,1},{2,6},{6,10},{... | collective-permute-start | bytes 1179656 | tf_op jit(solution)/shard_map/ppermute | solution.py:440
  95.0 18.4 %all-to-all-start.1 = ((bf16[32,32,384]{2,1,0:T(8,128)(2,1)}), bf16[32,32,384]{2,1,0:T(8,128)(2,1)S(1)}, u32[]{:S(2)}, u32[]{:S(2)}) async-start(bf16[32,32,384]{2,1,0:T(8,128)(2,1)} %bitcast.19), calls=%async_computation.1 | async-start | bytes 1572864 | tf_op jit(solution)/shard_map/all_to_all | solution.py:428
  102.2 3.5 %copy-start.6 = (bf16[512,384]{1,0:T(8,128)(2,1)}, bf16[512,384]{1,0:T(8,128)(2,1)S(1)}, u32[]{:S(2)}) copy-start(bf16[512,384]{1,0:T(8,128)(2,1)S(1)} %collective-permute-done.5.m1_ref) | copy-start | bytes 1179652
  102.2 3.5 %copy-start.7 = (bf16[512,384]{1,0:T(8,128)(2,1)}, bf16[512,384]{1,0:T(8,128)(2,1)S(1)}, u32[]{:S(2)}) copy-start(bf16[512,384]{1,0:T(8,128)(2,1)S(1)} %collective-permute-done.6.m2_ref) | copy-start | bytes 1179652
  105.7 0.8 copy-start.8
  112.8 24.8 %collective-permute-start.10 = (bf16[32,24,768]{2,1,0:T(8,128)(2,1)}, bf16[32,24,768]{2,1,0:T(8,128)(2,1)S(1)}, u32[]{:S(2)}, u32[]{:S(2)}) collective-permute-start(bf16[32,24,768]{2,1,0:T(8,128)(2,1)} %get-tuple-element.61), channel_id=1, source_target_pairs={{0,32},{32,0},{1,33},{33,1},{2,34},{34,2},{3,35},{35,3},{4,36},{36... | collective-permute-start | bytes 3538952 | tf_op jit(solution)/shard_map/ppermute | solution.py:444
  113.4 0.9 copy-start.3
  114.2 23.3 %copy-start.5 = (bf16[32,24,768]{2,1,0:T(8,128)(2,1)S(1)}, bf16[32,24,768]{2,1,0:T(8,128)(2,1)}, u32[]{:S(2)}) copy-start(bf16[32,24,768]{2,1,0:T(8,128)(2,1)} %get-tuple-element.60) | copy-start | bytes 3538948
  116.9 6.3 %collective-permute-start.9 = (f32[32,1536]{1,0:T(8,128)}, f32[32,1536]{1,0:T(8,128)S(1)}, u32[]{:S(2)}, u32[]{:S(2)}) collective-permute-start(f32[32,1536]{1,0:T(8,128)} %get-tuple-element.55.own_ref), channel_id=1, source_target_pairs={{0,1},{1,2},{2,3},{3,4},{4,5},{5,6},{6,7},{7,8},{8,9},{9,10},{10,1... | collective-permute-start | bytes 589832 | tf_op jit(solution)/shard_map/ppermute | solution.py:432
  120.2 6.6 %collective-permute-start.8 = (f32[32,1536]{1,0:T(8,128)}, f32[32,1536]{1,0:T(8,128)S(1)}, u32[]{:S(2)}, u32[]{:S(2)}) collective-permute-start(f32[32,1536]{1,0:T(8,128)} %get-tuple-element.55.own_ref), channel_id=1, source_target_pairs={{1,0},{2,1},{3,2},{4,3},{5,4},{6,5},{7,6},{8,7},{9,8},{10,9},{11,1... | collective-permute-start | bytes 589832 | tf_op jit(solution)/shard_map/ppermute | solution.py:436
  123.2 3.7 %copy-start.13 = (f32[32,1536]{1,0:T(8,128)}, f32[32,1536]{1,0:T(8,128)S(1)}, u32[]{:S(2)}) copy-start(f32[32,1536]{1,0:T(8,128)S(1)} %collective-permute-done.9.low_ref) | copy-start | bytes 589828
  126.9 0.7 copy-start.14
  133.1 16.6 %collective-permute-start.14 = (bf16[32,24,896]{2,1,0:T(8,128)(2,1)}, bf16[32,24,896]{2,1,0:T(8,128)(2,1)}, u32[]{:S(2)}, u32[]{:S(2)}) collective-permute-start(bf16[32,24,896]{2,1,0:T(8,128)(2,1)} %get-tuple-element.63), channel_id=1, source_target_pairs={{0,32},{32,0},{1,33},{33,1},{2,34},{34,2},{3,35},{35,3},{4,36},{36... | collective-permute-start | bytes 4128776 | tf_op jit(solution)/shard_map/ppermute | solution.py:444
  138.9 10.9 %copy-start.4 = (bf16[32,24,896]{2,1,0:T(8,128)(2,1)S(1)}, bf16[32,24,896]{2,1,0:T(8,128)(2,1)}, u32[]{:S(2)}) copy-start(bf16[32,24,896]{2,1,0:T(8,128)(2,1)} %get-tuple-element.62) | copy-start | bytes 4128772
  138.9 28.8 %all-to-all-start.2 = ((bf16[32,24,768]{2,1,0:T(8,128)(2,1)}), bf16[32,24,768]{2,1,0:T(8,128)(2,1)S(1)}, u32[]{:S(2)}, u32[]{:S(2)}) async-start(bf16[32,24,768]{2,1,0:T(8,128)(2,1)} %add_convert_fusion.1), calls=%async_computation.2 | async-start | bytes 2359296 | tf_op jit(solution)/shard_map/all_to_all | solution.py:428
  167.6 1.0 copy-start.2
  168.6 22.9 %all-to-all-start.3 = ((bf16[32,24,896]{2,1,0:T(8,128)(2,1)}), bf16[32,24,896]{2,1,0:T(8,128)(2,1)S(1)}, u32[]{:S(2)}, u32[]{:S(2)}) async-start(bf16[32,24,896]{2,1,0:T(8,128)(2,1)} %add_convert_fusion), calls=%async_computation.3 | async-start | bytes 2752512 | tf_op jit(solution)/shard_map/all_to_all | solution.py:428
  175.3 25.9 %copy-start.12 = (f32[24,768]{1,0:T(8,128)S(1)}, f32[24,768]{1,0:T(8,128)}, u32[]{:S(2)}) copy-start(f32[24,768]{1,0:T(8,128)} %fold.2.refs_0_) | copy-start | bytes 221188
  175.3 28.4 %collective-permute-start.13 = (f32[24,768]{1,0:T(8,128)}, f32[24,768]{1,0:T(8,128)S(1)}, u32[]{:S(2)}, u32[]{:S(2)}) collective-permute-start(f32[24,768]{1,0:T(8,128)} %fold.2.refs_0_), channel_id=1, source_target_pairs={{0,96},{32,64},{64,32},{96,0},{1,97},{33,65},{65,33},{97,1},{2,98}... | collective-permute-start | bytes 221192 | tf_op jit(solution)/shard_map/ppermute | solution.py:449
  191.5 1.1 copy-start.1
  194.8 16.5 %collective-permute-start.17 = (f32[24,896]{1,0:T(8,128)}, f32[24,896]{1,0:T(8,128)S(1)}, u32[]{:S(2)}, u32[]{:S(2)}) collective-permute-start(f32[24,896]{1,0:T(8,128)} %fold.3.refs_4_), channel_id=1, source_target_pairs={{0,96},{32,64},{64,32},{96,0},{1,97},{33,65},{65,33},{97,1},{2,98}... | collective-permute-start | bytes 258056 | tf_op jit(solution)/shard_map/ppermute | solution.py:449
  200.8 10.5 %collective-permute-start.16 = (f32[24,896]{1,0:T(8,128)}, f32[24,896]{1,0:T(8,128)S(1)}, u32[]{:S(2)}, u32[]{:S(2)}) collective-permute-start(f32[24,896]{1,0:T(8,128)} %fold.3.refs_4_), channel_id=1, source_target_pairs={{0,64},{32,96},{64,0},{96,32},{1,65},{33,97},{65,1},{97,33},{2,66}... | collective-permute-start | bytes 258056 | tf_op jit(solution)/shard_map/ppermute | solution.py:449
  200.8 10.6 %collective-permute-start.15 = (f32[24,896]{1,0:T(8,128)}, f32[24,896]{1,0:T(8,128)S(1)}, u32[]{:S(2)}, u32[]{:S(2)}) collective-permute-start(f32[24,896]{1,0:T(8,128)} %fold.3.refs_4_), channel_id=1, source_target_pairs={{0,32},{32,0},{64,96},{96,64},{1,33},{33,1},{65,97},{97,65},{2,34}... | collective-permute-start | bytes 258056 | tf_op jit(solution)/shard_map/ppermute | solution.py:449
  201.2 10.1 %collective-permute-start.12 = (f32[24,768]{1,0:T(8,128)S(1)}, f32[24,768]{1,0:T(8,128)S(1)}, u32[]{:S(2)}, u32[]{:S(2)}) collective-permute-start(f32[24,768]{1,0:T(8,128)S(1)} %copy-done.12), channel_id=1, source_target_pairs={{0,64},{32,96},{64,0},{96,32},{1,65},{33,97},{65,1},{97,33},{2,66}... | collective-permute-start | bytes 221192 | tf_op jit(solution)/shard_map/ppermute | solution.py:449
  203.7 7.5 %copy-start.20 = (f32[24,768]{1,0:T(8,128)}, f32[24,768]{1,0:T(8,128)S(1)}, u32[]{:S(2)}) copy-start(f32[24,768]{1,0:T(8,128)S(1)} %collective-permute-done.13.refs_3_) | copy-start | bytes 221188
  203.7 7.5 %collective-permute-start.11 = (f32[24,768]{1,0:T(8,128)S(1)}, f32[24,768]{1,0:T(8,128)S(1)}, u32[]{:S(2)}, u32[]{:S(2)}) collective-permute-start(f32[24,768]{1,0:T(8,128)S(1)} %copy-done.12), channel_id=1, source_target_pairs={{0,32},{32,0},{64,96},{96,64},{1,33},{33,1},{65,97},{97,65},{2,34}... | collective-permute-start | bytes 221192 | tf_op jit(solution)/shard_map/ppermute | solution.py:449
  211.3 0.6 copy-start.21
  211.3 0.7 copy-start.22
  211.3 0.7 copy-start.17
  211.3 0.7 copy-start.18
  212.0 0.6 copy-start.19

commit v3 on v2

--- a/solution.py
+++ b/solution.py
@@ -16,7 +16,7 @@
 TAPS = 288
 POS = 32
 EPSILON = 1e-05
-HALF_B = WIDTH + 128
+PAY_B = WIDTH + 256
 TM = ("tm_0", "tm_1", "tm_2")
 DP = ("dp_0", "dp_1")
 BF = jnp.bfloat16
@@ -178,27 +178,44 @@
 
 
 def attend(qd, kv_ref, acc_ref):
-    mixed, d_query = [], []
-    for h in range(GROUP_HEADS):
-        lo = slice(HEAD * h, HEAD * h + HEAD)
-        hi = slice(SPAN + HEAD * h, SPAN + HEAD * h + HEAD)
-        q = qd[:, lo]
-        dm = qd[:, hi]
-        k = kv_ref[:, lo]
-        v = kv_ref[:, hi]
-        scores = dot(q * jnp.asarray(0.125, BF), k, 1, 1)
-        weights = jnp.exp(scores - jnp.max(scores, axis=-1, keepdims=True))
-        inverse = 1.0 / jnp.sum(weights, axis=-1, keepdims=True)
-        rounded = weights.astype(BF)
-        attended = dot(rounded, v, 1, 0) * inverse
-        mixed.append((attended + q.astype(F32)).astype(BF))
-        wide = dm.astype(F32)
-        delta = jnp.sum(wide * attended, axis=-1, keepdims=True)
-        acc_ref[hi, :] += dot((wide * inverse).astype(BF), rounded, 0, 0)
-        d_scores = ((weights * inverse) * (dot(dm, v, 1, 1) - delta)).astype(BF)
-        d_query.append((dot(d_scores, k, 1, 0) * 0.125 + wide).astype(BF))
-        acc_ref[lo, :] += dot(q, d_scores, 0, 0) * 0.125
-    return jnp.concatenate(mixed + d_query, axis=-1)
+    n = GROUP_HEADS
+    lo = [slice(HEAD * h, HEAD * h + HEAD) for h in range(n)]
+    hi = [slice(SPAN + HEAD * h, SPAN + HEAD * h + HEAD) for h in range(n)]
+    q = [qd[:, lo[h]] for h in range(n)]
+    dm = [qd[:, hi[h]] for h in range(n)]
+    k = [kv_ref[:, lo[h]] for h in range(n)]
+    v = [kv_ref[:, hi[h]] for h in range(n)]
+    s, w, inv, rounded, dp, ds, delta = ({} for _ in range(7))
+    mixed, dq = {}, {}
+    def score(h):
+        s[h] = dot(q[h] * jnp.asarray(0.125, BF), k[h], 1, 1)
+    def grad_probs(h):
+        dp[h] = dot(dm[h], v[h], 1, 1)
+    def soften(h):
+        w[h] = jnp.exp(s[h] - jnp.max(s[h], axis=-1, keepdims=True))
+        inv[h] = 1.0 / jnp.sum(w[h], axis=-1, keepdims=True)
+        rounded[h] = w[h].astype(BF)
+    def mix(h):
+        attended = lax.transpose(dot(v[h], rounded[h], 0, 1), (1, 0)) * inv[h]
+        mixed[h] = (attended + q[h].astype(F32)).astype(BF)
+        wide = dm[h].astype(F32)
+        delta[h] = jnp.sum(wide * attended, axis=-1, keepdims=True)
+    def grad_values(h):
+        acc_ref[hi[h], :] += dot((dm[h].astype(F32) * inv[h]).astype(BF), rounded[h], 0, 0)
+    def grad_scores(h):
+        ds[h] = ((w[h] * inv[h]) * (dp[h] - delta[h])).astype(BF)
+    def grad_rest(h):
+        dq[h] = (dot(ds[h], k[h], 1, 0) * 0.125 + dm[h].astype(F32)).astype(BF)
+        acc_ref[lo[h], :] += dot(q[h], ds[h], 0, 0) * 0.125
+    order = (
+        (score, 0), (soften, 0), (score, 1), (grad_probs, 0), (mix, 0), (soften, 1),
+        (grad_values, 0), (grad_scores, 0), (mix, 1), (grad_probs, 1), (score, 2), (grad_rest, 0),
+        (soften, 2), (grad_scores, 1), (grad_values, 1), (mix, 2), (grad_probs, 2), (grad_rest, 1),
+        (grad_scores, 2), (grad_values, 2), (grad_rest, 2),
+    )
+    for function, h in order:
+        function(h)
+    return jnp.concatenate([mixed[h] for h in range(n)] + [dq[h] for h in range(n)], axis=-1)
 
 
 def others_kernel(q0_ref, q1_ref, q2_ref, kv_ref, m0_ref, m1_ref, m2_ref, acc_ref, work_ref):
@@ -281,47 +298,67 @@
     return jnp.concatenate(out, axis=-1)
 
 
-def pool_back_kernel(up_ref, own_ref, low_ref, taps_ref, tt_ref, pk_ref, gsum_ref, dv_ref, *pays):
-    kernel = jnp.concatenate([over_heads(pk_ref[:, 0, :]), over_heads(pk_ref[:, 1, :])], axis=-1)
+def dest_rows(f):
+    return slice(24 * f, 24 * f + 24)
+
+
+def pool_back_kernel(up_ref, own_ref, low_ref, taps_ref, tt_ref, pk_ref, gsum_ref, *out_refs):
+    dv_ref, send_ref, small_ref = out_refs
     sources = (up_ref[...], own_ref[...], low_ref[...])
+    for s in range(2):
+        lanes = slice(WIDTH * s, WIDTH * s + WIDTH)
+        kernel = over_heads(pk_ref[:, s, :])
+        for be in range(9):
+            total = None
+            for a in range(3):
+                term = sources[a][:, lanes] * kernel[9 * a + be : 9 * a + be + 1]
+                total = term if total is None else total + term
+            dv_ref[s, 32 * be : 32 * be + 32, :] = total.astype(BF)
+    grads = dot(tt_ref[...], dv_ref[1 - lax.axis_index("dp_1")], 0, 0)
+    for f in range(32):
+        send_ref[f] = grads[dest_rows(f)].astype(BF)
     tap_rows = []
     for a in range(3):
         for be in range(9):
             tap = taps_ref[32 * be : 32 * be + 32, :].astype(F32)
             tap_rows.append(jnp.sum(sources[a] * tap, axis=0, keepdims=True))
-    for be in range(9):
-        total = None
-        for a in range(3):
-            term = sources[a] * kernel[9 * a + be : 9 * a + be + 1]
-            total = term if total is None else total + term
-        dv_ref[32 * be : 32 * be + 32, :] = total.astype(BF)
     small = head_sum(jnp.concatenate(tap_rows + [gsum_ref[...]], axis=0))
-    first = small[0:24]
     second = jnp.concatenate([small[24:28], jnp.zeros((20, 128), F32)], axis=0)
-    extra = jnp.concatenate([first, second], axis=-1).astype(BF)
-    grads = dot(tt_ref[...], dv_ref[...], 0, 0)
-    keep_ref, send_ref, half_ref = pays
-    for f in range(32):
-        rows = jnp.concatenate([grads[24 * f : 24 * f + 24].astype(BF), extra], axis=-1)
-        half_ref[0, f] = rows[:, :HALF_B]
-        half_ref[1, f] = rows[:, HALF_B:]
-    core = lax.axis_index("dp_1")
-    keep_ref[...] = half_ref[core]
-    send_ref[...] = half_ref[1 - core]
+    small_ref[...] = jnp.concatenate([small[0:24], second], axis=-1)
 
 
 def pool_back(up, own, low, taps, tap_tokens, pool_kernel, gain_sum):
     return pl.pallas_call(
         pool_back_kernel,
         out_shape=[
-            jax.ShapeDtypeStruct((TAPS, 2 * WIDTH), BF),
-            jax.ShapeDtypeStruct((32, 24, HALF_B), BF),
-            jax.ShapeDtypeStruct((32, 24, HALF_B), BF),
-        ],
-        scratch_shapes=[pltpu.VMEM((2, 32, 24, HALF_B), BF)],
+            jax.ShapeDtypeStruct((2, TAPS, WIDTH), BF),
+            jax.ShapeDtypeStruct((32, 24, WIDTH), BF),
+            jax.ShapeDtypeStruct((24, 256), F32),
+        ],
         compiler_params=params(),
         name="pool_back",
     )(up, own, low, taps, tap_tokens, pool_kernel, gain_sum)
+
+
+def pay_b_kernel(tt_ref, dv_ref, other_ref, small_ref, other_small_ref, out_ref):
+    core = lax.axis_index("dp_1")
+    grads = dot(tt_ref[...], dv_ref[core], 0, 0)
+    small = small_ref[...] + other_small_ref[...]
+    high = small.astype(BF).astype(F32)
+    extra = jnp.where(core == 0, high, small - high).astype(BF)
+    for f in range(32):
+        total = grads[dest_rows(f)] + other_ref[f].astype(F32)
+        out_ref[f, :, :WIDTH] = total.astype(BF)
+        out_ref[f, :, WIDTH:] = extra
+
+
+def pay_b_rows(tap_tokens, dv, other, small, other_small):
+    return pl.pallas_call(
+        pay_b_kernel,
+        out_shape=jax.ShapeDtypeStruct((32, 24, PAY_B), BF),
+        compiler_params=params(),
+        name="pay_b_rows",
+    )(tap_tokens, dv, other, small, other_small)
 
 
 def output_kernel(m0_ref, m1_ref, m2_ref, m3_ref, tok_ref, cot_ref, ow_ref, *refs):
@@ -360,8 +397,11 @@
 
 
 def token_grad_kernel(dq_ref, dv_ref, w_ref, out_ref):
-    spread = dot(scatter_matrix(), dv_ref[...], 1, 0).astype(BF)
-    total = dot(dq_ref[...], w_ref[:, :WIDTH], 1, 1) + dot(spread, w_ref[:, WIDTH:], 1, 1)
+    scatter = scatter_matrix()
+    total = dot(dq_ref[...], w_ref[:, :WIDTH], 1, 1)
+    for s in range(2):
+        spread = dot(scatter, dv_ref[s], 1, 0).astype(BF)
+        total += dot(spread, w_ref[:, WIDTH * (s + 1) : WIDTH * (s + 2)], 1, 1)
     out_ref[...] = total.astype(BF)
 
 
@@ -397,11 +437,12 @@
     b_ref[core] = (b0[...] + b2[...]) * scale
     b_ref[1 - core] = (b1[...] + b3[...]) * scale
     qkv_ref[:, :WIDTH] = a_ref[0]
-    qkv_ref[:, WIDTH : WIDTH + HALF_B] = b_ref[0]
-    qkv_ref[:, WIDTH + HALF_B :] = b_ref[1, :, : 2 * WIDTH - HALF_B]
+    qkv_ref[:, WIDTH : 2 * WIDTH] = b_ref[0, :, :WIDTH]
+    qkv_ref[:, 2 * WIDTH :] = b_ref[1, :, :WIDTH]
     out_ref[...] = a_ref[1]
-    first = b_ref[1, :, HALF_B - 256 : HALF_B - 128]
-    second = b_ref[1, :, HALF_B - 128 :]
+    small = b_ref[0, :, WIDTH:] + b_ref[1, :, WIDTH:]
+    first = small[:, :128]
+    second = small[:, 128:]
     for s in range(2):
         lanes = slice(HEAD * s, HEAD * s + HEAD)
         kernel_ref[0:24, s, :] = first[:, lanes]
@@ -418,7 +459,7 @@
             jax.ShapeDtypeStruct((27, 2, HEAD), F32),
             jax.ShapeDtypeStruct((2, HEAD), F32),
         ],
-        scratch_shapes=[pltpu.VMEM((2, 24, WIDTH), F32), pltpu.VMEM((2, 24, HALF_B), F32)],
+        scratch_shapes=[pltpu.VMEM((2, 24, WIDTH), F32), pltpu.VMEM((2, 24, PAY_B), F32)],
         compiler_params=params(),
         name="finish",
     )(*a, *b)
@@ -440,9 +481,12 @@
     return lax.ppermute(array, "tm_1", [(i, (i + steps) % GROUPS) for i in range(GROUPS)])
 
 
+def swap_cores(array):
+    return lax.ppermute(array, "dp_1", [(0, 1), (1, 0)])
+
+
 def core_sum(keep, send):
-    other = lax.ppermute(send, "dp_1", [(0, 1), (1, 0)])
-    return (keep.astype(F32) + other.astype(F32)).astype(BF)
+    return (keep.astype(F32) + swap_cores(send).astype(F32)).astype(BF)
 
 
 def copies(array):
@@ -474,8 +518,10 @@
     pay_a = core_sum(*pay_a)
     pay_a = exchange(pay_a, TM)
     pay_a = copies(fold(pay_a))
-    dv, *pay_b = pool_back(d_up, d_summed, d_low, taps, tap_tokens, pool_kernel, gain_sum)
-    pay_b = core_sum(*pay_b)
+    dv, send_b, small = pool_back(d_up, d_summed, d_low, taps, tap_tokens, pool_kernel, gain_sum)
+    other_small = swap_cores(small)
+    other_b = swap_cores(send_b)
+    pay_b = pay_b_rows(tap_tokens, dv, other_b, small, other_small)
     pay_b = exchange(pay_b, TM)
     pay_b = copies(fold(pay_b))
     grad_tokens = token_grad(dq, dv, qkv_weight)

time: 215 us -> 228 us (1.060)
  blocking collectives: 0 us -> 18.5 us
  starting transfers between devices: 71.4 us -> 62.6 us
  waiting for transfers between devices: 59 us -> 67.6 us
  Pallas kernels: 71.7 us -> 68.4 us
  other arithmetic: 4.11 us -> 1.32 us
    all_to_all x0 -> x1, blocking collectives: none -> 18.5 us  [exchange(): return lax.all_to_all(array, axis, split_axis=0, concat_axis=0, tiled=True)]
    ppermute x6, waiting for transfers between devices: 20.7 us -> 29.2 us  [rotate(): lax.ppermute(array, 'tm_1', [(i, (i + steps) % GROUPS) for i in range(GRO...]
    all_to_all x4 -> x3, starting transfers between devices: 33.4 us -> 26.1 us  [exchange(): return lax.all_to_all(array, axis, split_axis=0, concat_axis=0, tiled=True)]
    pallas_call x1, Pallas kernels: 23 us -> 18.9 us  [others(): pl.pallas_call(others_kernel, out_shape=[block, block, block, jax.ShapeDt...]
    convert_element_type x2 -> x1, other arithmetic: 4.11 us -> 1.32 us  [core_sum(): return (keep.astype(F32) + swap_cores(send).astype(F32)).astype(BF)]
    pallas_call x1 -> x2, Pallas kernels: 5.5 us -> 7.92 us  [the longest x1 4.21 us: pool_back(): pl.pallas_call(pool_back_kernel, out_shape=[jax.ShapeDtypeStruct((2, TAPS...]
    ppermute x2 -> x3, starting transfers between devices: 5.07 us -> 4.1 us  [swap_cores(): return lax.ppermute(array, 'dp_1', [(0, 1), (1, 0)])]
    all_to_all x4 -> x3, waiting for transfers between devices: 26.9 us -> 25.9 us  [exchange(): return lax.all_to_all(array, axis, split_axis=0, concat_axis=0, tiled=True)]
  transfers between devices with their start and end apart: 22 -> 22, of which waited for: 9 -> 11; matrix products, arithmetic and copies ran while one was open for 2% -> 1% of each run, Pallas kernels for 18% -> 15%
where the time goes in v3:
time: 228 us; the launch traced here: 227 us
  Pallas kernels  68.4 us (30%)
  waiting for transfers between devices  67.6 us (30%)
  starting transfers between devices  62.6 us (27%)
  blocking collectives  18.5 us (8%)
  local copies, waits for them, and re-layouts  7.82 us (3%)
    ppermute x6, waiting for transfers between devices, rotate(): lax.ppermute(array, 'tm_1', [(i, (i + steps) % GROUPS) for i in range(GRO...  29.2 us
    all_to_all x3, starting transfers between devices, exchange(): return lax.all_to_all(array, axis, split_axis=0, concat_axis=0, tiled=True)  26.1 us
    all_to_all x3, waiting for transfers between devices, exchange(): return lax.all_to_all(array, axis, split_axis=0, concat_axis=0, tiled=True)  25.9 us
    pallas_call x1, Pallas kernels, others(): pl.pallas_call(others_kernel, out_shape=[block, block, block, jax.ShapeDt...  18.9 us
    all_to_all x1, blocking collectives, exchange(): return lax.all_to_all(array, axis, split_axis=0, concat_axis=0, tiled=True)  18.5 us
    ppermute x6, starting transfers between devices, copies(): lax.ppermute(array, DP, [(i, i ^ k) for i in range(4)])  14.1 us
    ppermute x6, starting transfers between devices, rotate(): lax.ppermute(array, 'tm_1', [(i, (i + steps) % GROUPS) for i in range(GRO...  8.6 us
    pallas_call x1, Pallas kernels, own(): pl.pallas_call(own_kernel, out_shape=[jax.ShapeDtypeStruct(qd.shape, BF),...  8.2 us
  transfers between devices with their start and end apart: 22, of which 11 were waited for; matrix products, arithmetic and copies ran while one was open for 1% of the time, Pallas kernels for 15%

profile of v3, /device:TPU:1, one launch (start us, length us, event | category | flops | bytes accessed | tf_op | source)
XLA Modules:
  0.0 227.0 jit_solution(15184785750309513561)
XLA Ops:
  0.6 4.1 %tap_sums.1 = (bf16[288,1536]{1,0:T(8,128)(2,1)}, bf16[288,768]{1,0:T(8,128)(2,1)}, f32[32,1536]{1,0:T(8,128)}, f32[32,1536]{1,0:T(8,128)}, f32[32,1536]{1,0:T(8,128)}) custom-call(bf16[512,768]{1,0:T(8,128)(2,1)} %bitcast.12, bf16[768,2304]{1,0:T(8,128)(2,1)} %w_ref.5, f32[27,2,64]{2,1,0:T(2,128)} %bitcast.21), custom_call_target="tpu_custom_call" | custom-call | tf_op jit(solution)/shard_map/tap_sums/pallas_call | solution.py:95
  4.7 4.0 %collective-permute-start = (f32[32,1536]{1,0:T(8,128)}, f32[32,1536]{1,0:T(8,128)S(1)}, u32[]{:S(2)}, u32[]{:S(2)}) collective-permute-start(f32[32,1536]{1,0:T(8,128)} %get-tuple-element.38), channel_id=1, source_target_pairs={{0,1},{1,2},{2,3},{3,4},{4,5},{5,6},{6,7},{7,8},{8,9},{9,10},{10,1... | collective-permute-start | bytes 589832 | tf_op jit(solution)/shard_map/ppermute | solution.py:473
  8.8 1.3 collective-permute-start.1
  10.1 2.6 %collective-permute-done.low_ref = f32[32,1536]{1,0:T(8,128)S(1)} collective-permute-done((f32[32,1536]{1,0:T(8,128)}, f32[32,1536]{1,0:T(8,128)S(1)}, u32[]{:S(2)}, u32[]{:S(2)}) %collective-permute-start) | collective-permute-done | bytes 196640 | tf_op jit(solution)/shard_map/ppermute | solution.py:473
  12.6 3.7 %collective-permute-done.1.up_ref = f32[32,1536]{1,0:T(8,128)S(1)} collective-permute-done((f32[32,1536]{1,0:T(8,128)}, f32[32,1536]{1,0:T(8,128)S(1)}, u32[]{:S(2)}, u32[]{:S(2)}) %collective-permute-start.1) | collective-permute-done | bytes 196640 | tf_op jit(solution)/shard_map/ppermute | solution.py:477
  16.4 0.7 copy-done.16
  17.0 3.0 %norm_side.1 = (bf16[2,4,4,32,384]{4,3,2,1,0:T(8,128)(2,1)}, f32[32,1536]{1,0:T(8,128)}, f32[32,1536]{1,0:T(8,128)}) custom-call(f32[32,1536]{1,0:T(8,128)} %copy-done.15, f32[32,1536]{1,0:T(8,128)} %get-tuple-element.39.own_ref, f32[32,1536]{1,0:T(8,128)} %copy-done.16, f32[2,64]{1,0:T(2,128)} %gain_ref.3), custom_call_target="tpu_custom_call" | custom-call | tf_op jit(solution)/shard_map/norm_side/pallas_call | solution.py:172
  20.0 10.7 %all-to-all-start = ((bf16[32,32,384]{2,1,0:T(8,128)(2,1)}), bf16[32,32,384]{2,1,0:T(8,128)(2,1)S(1)}, u32[]{:S(2)}, u32[]{:S(2)}) async-start(bf16[32,32,384]{2,1,0:T(8,128)(2,1)} %bitcast.18), calls=%async_computation | async-start | bytes 1572864 | tf_op jit(solution)/shard_map/all_to_all | solution.py:469
  30.7 4.8 %query_side.1 = (bf16[512,384]{1,0:T(8,128)(2,1)}, bf16[512,384]{1,0:T(8,128)(2,1)}, bf16[512,384]{1,0:T(8,128)(2,1)}, bf16[512,384]{1,0:T(8,128)(2,1)}) custom-call(bf16[512,768]{1,0:T(8,128)(2,1)} %bitcast.13, bf16[768,2304]{1,0:T(8,128)(2,1)} %w_ref.5, bf16[512,768]{1,0:T(8,128)(2,1)} %bitcast.16, bf16[768,768]{1,0:T(8,128)(2,1)} %ow_ref.3), custom_call_target="tpu_custom_call" | custom-call | tf_op jit(solution)/shard_map/query_side/pallas_call | solution.py:137
  35.5 1.2 collective-permute-start.2
  36.7 2.4 %collective-permute-start.3 = (bf16[512,384]{1,0:T(8,128)(2,1)}, bf16[512,384]{1,0:T(8,128)(2,1)S(1)}, u32[]{:S(2)}, u32[]{:S(2)}) collective-permute-start(bf16[512,384]{1,0:T(8,128)(2,1)} %get-tuple-element.43), channel_id=1, source_target_pairs={{0,8},{4,12},{8,0},{12,4},{1,9},{5,13},{9,1},{13,5},{2,10},{6,14},... | collective-permute-start | bytes 1179656 | tf_op jit(solution)/shard_map/ppermute | solution.py:481
  39.1 1.2 collective-permute-start.4
  40.3 10.8 %collective-permute-done.2.q0_ref = bf16[512,384]{1,0:T(8,128)(2,1)S(1)} collective-permute-done((bf16[512,384]{1,0:T(8,128)(2,1)}, bf16[512,384]{1,0:T(8,128)(2,1)S(1)}, u32[]{:S(2)}, u32[]{:S(2)}) %collective-permute-start.2) | collective-permute-done | bytes 393248 | tf_op jit(solution)/shard_map/ppermute | solution.py:481
  51.2 6.4 %collective-permute-done.3.q1_ref = bf16[512,384]{1,0:T(8,128)(2,1)S(1)} collective-permute-done((bf16[512,384]{1,0:T(8,128)(2,1)}, bf16[512,384]{1,0:T(8,128)(2,1)S(1)}, u32[]{:S(2)}, u32[]{:S(2)}) %collective-permute-start.3) | collective-permute-done | bytes 393248 | tf_op jit(solution)/shard_map/ppermute | solution.py:481
  57.5 0.0 collective-permute-done.4.q2_ref
  57.6 0.7 copy-done.10
  58.3 0.1 copy-done.11
  58.4 0.2 copy-done
  58.7 18.9 %attend_others.1 = (bf16[512,384]{1,0:T(8,128)(2,1)}, bf16[512,384]{1,0:T(8,128)(2,1)}, bf16[512,384]{1,0:T(8,128)(2,1)}, f32[384,1024]{1,0:T(8,128)}) custom-call(bf16[512,384]{1,0:T(8,128)(2,1)} %copy-done.9, bf16[512,384]{1,0:T(8,128)(2,1)} %copy-done.10, bf16[512,384]{1,0:T(8,128)(2,1)} %copy-done.11, bf16[1024,384]{1,0:T(8,128)(2,1)} %bitcast.10), custom_call_target="tpu_custom_call" | custom-call | tf_op jit(solution)/shard_map/attend_others/pallas_call | solution.py:237
  77.6 3.2 %collective-permute-start.5 = (bf16[512,384]{1,0:T(8,128)(2,1)}, bf16[512,384]{1,0:T(8,128)(2,1)S(1)}, u32[]{:S(2)}, u32[]{:S(2)}) collective-permute-start(bf16[512,384]{1,0:T(8,128)(2,1)} %get-tuple-element.47), channel_id=1, source_target_pairs={{0,12},{4,0},{8,4},{12,8},{1,13},{5,1},{9,5},{13,9},{2,14},{6,2},{... | collective-permute-start | bytes 1179656 | tf_op jit(solution)/shard_map/ppermute | solution.py:481
  80.8 0.1 collective-permute-start.6
  80.8 0.5 collective-permute-start.7
  81.4 8.2 %attend_own.1 = (bf16[512,384]{1,0:T(8,128)(2,1)}, bf16[1024,384]{1,0:T(8,128)(2,1)}) custom-call(bf16[512,384]{1,0:T(8,128)(2,1)} %get-tuple-element.37.qd_ref, bf16[1024,384]{1,0:T(8,128)(2,1)} %bitcast.11, f32[384,1024]{1,0:T(8,128)} %get-tuple-element.45.start_ref), custom_call_target="tpu_custom_call" | custom-call | tf_op jit(solution)/shard_map/attend_own/pallas_call | solution.py:253
  89.6 7.8 %collective-permute-done.5.m1_ref = bf16[512,384]{1,0:T(8,128)(2,1)S(1)} collective-permute-done((bf16[512,384]{1,0:T(8,128)(2,1)}, bf16[512,384]{1,0:T(8,128)(2,1)S(1)}, u32[]{:S(2)}, u32[]{:S(2)}) %collective-permute-start.5) | collective-permute-done | bytes 393248 | tf_op jit(solution)/shard_map/ppermute | solution.py:481
  97.4 4.1 %collective-permute-done.7.m3_ref = bf16[512,384]{1,0:T(8,128)(2,1)S(1)} collective-permute-done((bf16[512,384]{1,0:T(8,128)(2,1)}, bf16[512,384]{1,0:T(8,128)(2,1)S(1)}, u32[]{:S(2)}, u32[]{:S(2)}) %collective-permute-start.7) | collective-permute-done | bytes 393248 | tf_op jit(solution)/shard_map/ppermute | solution.py:481
  101.5 0.7 copy-done.8
  102.3 6.3 %output_side.1 = (bf16[512,768]{1,0:T(8,128)(2,1)}, bf16[512,768]{1,0:T(8,128)(2,1)}, bf16[32,24,768]{2,1,0:T(8,128)(2,1)}, bf16[32,24,768]{2,1,0:T(8,128)(2,1)}) custom-call(bf16[512,384]{1,0:T(8,128)(2,1)} %get-tuple-element.46.m0_ref, bf16[512,384]{1,0:T(8,128)(2,1)} %copy-done.6, bf16[512,384]{1,0:T(8,128)(2,1)} %copy-done.7, ...), custom_call_target="tpu_custom_call" | custom-call | tf_op jit(solution)/shard_map/output_side/pallas_call | solution.py:387
  108.6 0.7 collective-permute-start.10
  109.2 18.5 %all_to_all.20 = bf16[32,32,384]{2,1,0:T(8,128)(2,1)} all-to-all(bf16[32,32,384]{2,1,0:T(8,128)(2,1)S(1)} %bitcast.19), channel_id=1, replica_groups=mesh['dp_0'=2,'dp_1'=2,'tm_0'=2,'tm_1'=4,'tm_2'=4] {'tm_0','tm_1','tm_2'}, dimensions={0} | all-to-all | bytes 1572864 | tf_op jit(solution)/shard_map/all_to_all | solution.py:469
  127.7 2.5 %norm_back.1 = (f32[32,1536]{1,0:T(8,128)}, f32[1,1536]{1,0:T(1,128)}) custom-call(bf16[2,4,4,32,384]{4,3,2,1,0:T(8,128)(2,1)} %bitcast.15, f32[32,1536]{1,0:T(8,128)} %get-tuple-element.53.normed_ref, f32[32,1536]{1,0:T(8,128)} %get-tuple-element.54.inv_ref, f32[2,64]{1,0:T(2,128)} %gain_ref.3), custom_call_target="tpu_custom_call" | custom-call | tf_op jit(solution)/shard_map/norm_back/pallas_call | solution.py:280
  130.3 3.1 %collective-permute-start.9 = (f32[32,1536]{1,0:T(8,128)}, f32[32,1536]{1,0:T(8,128)S(1)}, u32[]{:S(2)}, u32[]{:S(2)}) collective-permute-start(f32[32,1536]{1,0:T(8,128)} %get-tuple-element.55.own_ref), channel_id=1, source_target_pairs={{0,1},{1,2},{2,3},{3,4},{4,5},{5,6},{6,7},{7,8},{8,9},{9,10},{10,1... | collective-permute-start | bytes 589832 | tf_op jit(solution)/shard_map/ppermute | solution.py:473
  133.4 1.3 collective-permute-start.8
  134.7 1.8 collective-permute-done.9.low_ref
  136.5 3.5 %collective-permute-done.8.up_ref = f32[32,1536]{1,0:T(8,128)S(1)} collective-permute-done((f32[32,1536]{1,0:T(8,128)}, f32[32,1536]{1,0:T(8,128)S(1)}, u32[]{:S(2)}, u32[]{:S(2)}) %collective-permute-start.8) | collective-permute-done | bytes 196640 | tf_op jit(solution)/shard_map/ppermute | solution.py:477
  140.0 0.7 copy-done.14
  140.7 4.2 %pool_back.1 = (bf16[2,288,768]{2,1,0:T(8,128)(2,1)}, bf16[32,24,768]{2,1,0:T(8,128)(2,1)}, f32[24,256]{1,0:T(8,128)}) custom-call(f32[32,1536]{1,0:T(8,128)} %copy-done.14, f32[32,1536]{1,0:T(8,128)} %get-tuple-element.55.own_ref, f32[32,1536]{1,0:T(8,128)} %copy-done.13, bf16[288,1536]{1,0:T(8,128)(2,1)} %get-tuple-element.56.taps_ref, ...), custom_call_target="tpu_custom_call" | custom-call | tf_op jit(solution)/shard_map/pool_back/pallas_call | solution.py:331
  144.9 2.8 %collective-permute-start.14 = (bf16[32,24,768]{2,1,0:T(8,128)(2,1)}, bf16[32,24,768]{2,1,0:T(8,128)(2,1)S(1)}, u32[]{:S(2)}, u32[]{:S(2)}) collective-permute-start(bf16[32,24,768]{2,1,0:T(8,128)(2,1)} %get-tuple-element.62), channel_id=1, source_target_pairs={{0,32},{32,0},{1,33},{33,1},{2,34},{34,2},{3,35},{35,3},{4,36},{36... | collective-permute-start | bytes 3538952 | tf_op jit(solution)/shard_map/ppermute | solution.py:485
  147.7 1.3 add_convert_fusion
  149.1 10.8 %all-to-all-start.2 = ((bf16[32,24,768]{2,1,0:T(8,128)(2,1)}), bf16[32,24,768]{2,1,0:T(8,128)(2,1)S(1)}, u32[]{:S(2)}, u32[]{:S(2)}) async-start(bf16[32,24,768]{2,1,0:T(8,128)(2,1)} %add_convert_fusion), calls=%async_computation.2 | async-start | bytes 2359296 | tf_op jit(solution)/shard_map/all_to_all | solution.py:469
  159.8 0.6 collective-permute-start.15
  160.4 0.9 collective-permute-done.15.other_small_ref
  161.3 0.6 copy-done.24
  161.9 0.4 copy-done.4
  162.4 3.7 %pay_b_rows.1 = bf16[32,24,1024]{2,1,0:T(8,128)(2,1)} custom-call(bf16[288,768]{1,0:T(8,128)(2,1)} %get-tuple-element.57.tt_ref, bf16[2,288,768]{2,1,0:T(8,128)(2,1)} %get-tuple-element.59.dv_ref, bf16[32,24,768]{2,1,0:T(8,128)(2,1)} %copy-done.4, f32[24,256]{1,0:T(8,128)} %get-tuple-element.63.small_ref, f32[24,256]{1,0:T(8,128)} %copy-done.24), custom_call_target="tpu_custom_call" | custom-call | tf_op jit(solution)/shard_map/pay_b_rows/pallas_call | solution.py:356
  166.1 11.7 %all-to-all-done.2.parts_ref = bf16[32,24,768]{2,1,0:T(8,128)(2,1)S(1)} async-done(((bf16[32,24,768]{2,1,0:T(8,128)(2,1)}), bf16[32,24,768]{2,1,0:T(8,128)(2,1)S(1)}, u32[]{:S(2)}, u32[]{:S(2)}) %all-to-all-start.2) | async-done | bytes 1179680 | tf_op jit(solution)/shard_map/all_to_all | solution.py:469
  177.7 1.0 copy-done.2
  178.8 4.6 %all-to-all-start.3 = ((bf16[32,24,1024]{2,1,0:T(8,128)(2,1)}), bf16[32,24,1024]{2,1,0:T(8,128)(2,1)S(1)}, u32[]{:S(2)}, u32[]{:S(2)}) async-start(bf16[32,24,1024]{2,1,0:T(8,128)(2,1)} %pay_b_rows.1), calls=%async_computation.3 | async-start | bytes 3145728 | tf_op jit(solution)/shard_map/all_to_all | solution.py:469
  183.4 2.1 fold.2.refs_0_
  185.4 4.5 %collective-permute-start.13 = (f32[24,768]{1,0:T(8,128)}, f32[24,768]{1,0:T(8,128)S(1)}, u32[]{:S(2)}, u32[]{:S(2)}) collective-permute-start(f32[24,768]{1,0:T(8,128)} %fold.2.refs_0_), channel_id=1, source_target_pairs={{0,96},{32,64},{64,32},{96,0},{1,97},{33,65},{65,33},{97,1},{2,98}... | collective-permute-start | bytes 221192 | tf_op jit(solution)/shard_map/ppermute | solution.py:493
  189.9 14.2 %all-to-all-done.3.parts_ref = bf16[32,24,1024]{2,1,0:T(8,128)(2,1)S(1)} async-done(((bf16[32,24,1024]{2,1,0:T(8,128)(2,1)}), bf16[32,24,1024]{2,1,0:T(8,128)(2,1)S(1)}, u32[]{:S(2)}, u32[]{:S(2)}) %all-to-all-start.3) | async-done | bytes 1572896 | tf_op jit(solution)/shard_map/all_to_all | solution.py:469
  204.2 1.2 copy-done.1
  205.3 2.3 %fold.3.refs_4_ = f32[24,1024]{1,0:T(8,128)} custom-call(bf16[32,24,1024]{2,1,0:T(8,128)(2,1)} %copy-done.1), custom_call_target="tpu_custom_call" | custom-call | tf_op jit(solution)/shard_map/fold/pallas_call | solution.py:425
  207.6 5.9 %collective-permute-start.18 = (f32[24,1024]{1,0:T(8,128)}, f32[24,1024]{1,0:T(8,128)S(1)}, u32[]{:S(2)}, u32[]{:S(2)}) collective-permute-start(f32[24,1024]{1,0:T(8,128)} %fold.3.refs_4_), channel_id=1, source_target_pairs={{0,96},{32,64},{64,32},{96,0},{1,97},{33,65},{65,33},{97,1},{2,98}... | collective-permute-start | bytes 294920 | tf_op jit(solution)/shard_map/ppermute | solution.py:493
  213.5 0.4 collective-permute-start.16
  213.9 2.6 %collective-permute-start.12 = (f32[24,768]{1,0:T(8,128)S(1)}, f32[24,768]{1,0:T(8,128)S(1)}, u32[]{:S(2)}, u32[]{:S(2)}) collective-permute-start(f32[24,768]{1,0:T(8,128)S(1)} %copy-done.12), channel_id=1, source_target_pairs={{0,64},{32,96},{64,0},{96,32},{1,65},{33,97},{65,1},{97,33},{2,66}... | collective-permute-start | bytes 221192 | tf_op jit(solution)/shard_map/ppermute | solution.py:493
  216.5 0.0 collective-permute-done.13.refs_3_
  216.5 0.8 collective-permute-start.11
  217.3 6.3 %token_grad.1 = bf16[512,768]{1,0:T(8,128)(2,1)} custom-call(bf16[512,768]{1,0:T(8,128)(2,1)} %get-tuple-element.51.dq_ref, bf16[2,288,768]{2,1,0:T(8,128)(2,1)} %get-tuple-element.59.dv_ref, bf16[768,2304]{1,0:T(8,128)(2,1)} %w_ref.5), custom_call_target="tpu_custom_call" | custom-call | tf_op jit(solution)/shard_map/token_grad/pallas_call | solution.py:409
  223.7 0.6 copy-done.21
  224.2 0.0 copy-done.22
  224.3 0.0 copy-done.17
  224.3 0.1 copy-done.18
  224.4 0.6 copy-done.19
  225.0 2.0 finish.1
  (45 shorter events, 0.1 us)
Async XLA Ops:
  4.7 7.9 %collective-permute-start = (f32[32,1536]{1,0:T(8,128)}, f32[32,1536]{1,0:T(8,128)S(1)}, u32[]{:S(2)}, u32[]{:S(2)}) collective-permute-start(f32[32,1536]{1,0:T(8,128)} %get-tuple-element.38), channel_id=1, source_target_pairs={{0,1},{1,2},{2,3},{3,4},{4,5},{5,6},{6,7},{7,8},{8,9},{9,10},{10,1... | collective-permute-start | bytes 589832 | tf_op jit(solution)/shard_map/ppermute | solution.py:473
  8.8 7.6 %collective-permute-start.1 = (f32[32,1536]{1,0:T(8,128)}, f32[32,1536]{1,0:T(8,128)S(1)}, u32[]{:S(2)}, u32[]{:S(2)}) collective-permute-start(f32[32,1536]{1,0:T(8,128)} %get-tuple-element.40), channel_id=1, source_target_pairs={{1,0},{2,1},{3,2},{4,3},{5,4},{6,5},{7,6},{8,7},{9,8},{10,9},{11,1... | collective-permute-start | bytes 589832 | tf_op jit(solution)/shard_map/ppermute | solution.py:477
  12.6 3.7 %copy-start.15 = (f32[32,1536]{1,0:T(8,128)}, f32[32,1536]{1,0:T(8,128)S(1)}, u32[]{:S(2)}) copy-start(f32[32,1536]{1,0:T(8,128)S(1)} %collective-permute-done.low_ref) | copy-start | bytes 589828
  16.4 0.7 copy-start.16
  20.0 37.6 %all-to-all-start = ((bf16[32,32,384]{2,1,0:T(8,128)(2,1)}), bf16[32,32,384]{2,1,0:T(8,128)(2,1)S(1)}, u32[]{:S(2)}, u32[]{:S(2)}) async-start(bf16[32,32,384]{2,1,0:T(8,128)(2,1)} %bitcast.18), calls=%async_computation | async-start | bytes 1572864 | tf_op jit(solution)/shard_map/all_to_all | solution.py:469
  35.5 15.6 %collective-permute-start.2 = (bf16[512,384]{1,0:T(8,128)(2,1)}, bf16[512,384]{1,0:T(8,128)(2,1)S(1)}, u32[]{:S(2)}, u32[]{:S(2)}) collective-permute-start(bf16[512,384]{1,0:T(8,128)(2,1)} %get-tuple-element.42), channel_id=1, source_target_pairs={{0,4},{4,8},{8,12},{12,0},{1,5},{5,9},{9,13},{13,1},{2,6},{6,10},{... | collective-permute-start | bytes 1179656 | tf_op jit(solution)/shard_map/ppermute | solution.py:481
  36.7 20.8 %collective-permute-start.3 = (bf16[512,384]{1,0:T(8,128)(2,1)}, bf16[512,384]{1,0:T(8,128)(2,1)S(1)}, u32[]{:S(2)}, u32[]{:S(2)}) collective-permute-start(bf16[512,384]{1,0:T(8,128)(2,1)} %get-tuple-element.43), channel_id=1, source_target_pairs={{0,8},{4,12},{8,0},{12,4},{1,9},{5,13},{9,1},{13,5},{2,10},{6,14},... | collective-permute-start | bytes 1179656 | tf_op jit(solution)/shard_map/ppermute | solution.py:481
  39.1 18.4 %collective-permute-start.4 = (bf16[512,384]{1,0:T(8,128)(2,1)}, bf16[512,384]{1,0:T(8,128)(2,1)S(1)}, u32[]{:S(2)}, u32[]{:S(2)}) collective-permute-start(bf16[512,384]{1,0:T(8,128)(2,1)} %get-tuple-element.44), channel_id=1, source_target_pairs={{0,12},{4,0},{8,4},{12,8},{1,13},{5,1},{9,5},{13,9},{2,14},{6,2},{... | collective-permute-start | bytes 1179656 | tf_op jit(solution)/shard_map/ppermute | solution.py:481
  51.2 6.4 %copy-start.9 = (bf16[512,384]{1,0:T(8,128)(2,1)}, bf16[512,384]{1,0:T(8,128)(2,1)S(1)}, u32[]{:S(2)}) copy-start(bf16[512,384]{1,0:T(8,128)(2,1)S(1)} %collective-permute-done.2.q0_ref) | copy-start | bytes 1179652
  57.5 0.8 copy-start.10
  57.6 0.9 copy-start.11
  57.6 1.1 copy-start
  77.6 19.8 %collective-permute-start.5 = (bf16[512,384]{1,0:T(8,128)(2,1)}, bf16[512,384]{1,0:T(8,128)(2,1)S(1)}, u32[]{:S(2)}, u32[]{:S(2)}) collective-permute-start(bf16[512,384]{1,0:T(8,128)(2,1)} %get-tuple-element.47), channel_id=1, source_target_pairs={{0,12},{4,0},{8,4},{12,8},{1,13},{5,1},{9,5},{13,9},{2,14},{6,2},{... | collective-permute-start | bytes 1179656 | tf_op jit(solution)/shard_map/ppermute | solution.py:481
  80.8 16.6 %collective-permute-start.6 = (bf16[512,384]{1,0:T(8,128)(2,1)}, bf16[512,384]{1,0:T(8,128)(2,1)S(1)}, u32[]{:S(2)}, u32[]{:S(2)}) collective-permute-start(bf16[512,384]{1,0:T(8,128)(2,1)} %get-tuple-element.48), channel_id=1, source_target_pairs={{0,8},{4,12},{8,0},{12,4},{1,9},{5,13},{9,1},{13,5},{2,10},{6,14},... | collective-permute-start | bytes 1179656 | tf_op jit(solution)/shard_map/ppermute | solution.py:481
  80.8 20.7 %collective-permute-start.7 = (bf16[512,384]{1,0:T(8,128)(2,1)}, bf16[512,384]{1,0:T(8,128)(2,1)S(1)}, u32[]{:S(2)}, u32[]{:S(2)}) collective-permute-start(bf16[512,384]{1,0:T(8,128)(2,1)} %get-tuple-element.49), channel_id=1, source_target_pairs={{0,4},{4,8},{8,12},{12,0},{1,5},{5,9},{9,13},{13,1},{2,6},{6,10},{... | collective-permute-start | bytes 1179656 | tf_op jit(solution)/shard_map/ppermute | solution.py:481
  97.4 4.1 %copy-start.6 = (bf16[512,384]{1,0:T(8,128)(2,1)}, bf16[512,384]{1,0:T(8,128)(2,1)S(1)}, u32[]{:S(2)}) copy-start(bf16[512,384]{1,0:T(8,128)(2,1)S(1)} %collective-permute-done.5.m1_ref) | copy-start | bytes 1179652
  97.4 4.1 %copy-start.7 = (bf16[512,384]{1,0:T(8,128)(2,1)}, bf16[512,384]{1,0:T(8,128)(2,1)S(1)}, u32[]{:S(2)}) copy-start(bf16[512,384]{1,0:T(8,128)(2,1)S(1)} %collective-permute-done.6.m2_ref) | copy-start | bytes 1179652
  101.5 0.8 copy-start.8
  102.3 7.0 %copy-start.5 = (bf16[1024,384]{1,0:T(8,128)(2,1)S(1)}, bf16[1024,384]{1,0:T(8,128)(2,1)}, u32[]{:S(2)}) copy-start(bf16[1024,384]{1,0:T(8,128)(2,1)} %get-tuple-element.52) | copy-start | bytes 2359300
  108.6 39.2 %collective-permute-start.10 = (bf16[32,24,768]{2,1,0:T(8,128)(2,1)}, bf16[32,24,768]{2,1,0:T(8,128)(2,1)S(1)}, u32[]{:S(2)}, u32[]{:S(2)}) collective-permute-start(bf16[32,24,768]{2,1,0:T(8,128)(2,1)} %get-tuple-element.61), channel_id=1, source_target_pairs={{0,32},{32,0},{1,33},{33,1},{2,34},{34,2},{3,35},{35,3},{4,36},{36... | collective-permute-start | bytes 3538952 | tf_op jit(solution)/shard_map/ppermute | solution.py:485
  130.3 17.4 %copy-start.3 = (bf16[32,24,768]{2,1,0:T(8,128)(2,1)S(1)}, bf16[32,24,768]{2,1,0:T(8,128)(2,1)}, u32[]{:S(2)}) copy-start(bf16[32,24,768]{2,1,0:T(8,128)(2,1)} %get-tuple-element.60) | copy-start | bytes 3538948
  130.3 6.2 %collective-permute-start.9 = (f32[32,1536]{1,0:T(8,128)}, f32[32,1536]{1,0:T(8,128)S(1)}, u32[]{:S(2)}, u32[]{:S(2)}) collective-permute-start(f32[32,1536]{1,0:T(8,128)} %get-tuple-element.55.own_ref), channel_id=1, source_target_pairs={{0,1},{1,2},{2,3},{3,4},{4,5},{5,6},{6,7},{7,8},{8,9},{9,10},{10,1... | collective-permute-start | bytes 589832 | tf_op jit(solution)/shard_map/ppermute | solution.py:473
  133.4 6.6 %collective-permute-start.8 = (f32[32,1536]{1,0:T(8,128)}, f32[32,1536]{1,0:T(8,128)S(1)}, u32[]{:S(2)}, u32[]{:S(2)}) collective-permute-start(f32[32,1536]{1,0:T(8,128)} %get-tuple-element.55.own_ref), channel_id=1, source_target_pairs={{1,0},{2,1},{3,2},{4,3},{5,4},{6,5},{7,6},{8,7},{9,8},{10,9},{11,1... | collective-permute-start | bytes 589832 | tf_op jit(solution)/shard_map/ppermute | solution.py:477
  136.5 3.5 %copy-start.13 = (f32[32,1536]{1,0:T(8,128)}, f32[32,1536]{1,0:T(8,128)S(1)}, u32[]{:S(2)}) copy-start(f32[32,1536]{1,0:T(8,128)S(1)} %collective-permute-done.9.low_ref) | copy-start | bytes 589828
  140.0 0.7 copy-start.14
  144.9 16.4 %collective-permute-start.14 = (bf16[32,24,768]{2,1,0:T(8,128)(2,1)}, bf16[32,24,768]{2,1,0:T(8,128)(2,1)S(1)}, u32[]{:S(2)}, u32[]{:S(2)}) collective-permute-start(bf16[32,24,768]{2,1,0:T(8,128)(2,1)} %get-tuple-element.62), channel_id=1, source_target_pairs={{0,32},{32,0},{1,33},{33,1},{2,34},{34,2},{3,35},{35,3},{4,36},{36... | collective-permute-start | bytes 3538952 | tf_op jit(solution)/shard_map/ppermute | solution.py:485
  149.1 10.8 %copy-start.23 = (f32[24,256]{1,0:T(8,128)S(1)}, f32[24,256]{1,0:T(8,128)}, u32[]{:S(2)}) copy-start(f32[24,256]{1,0:T(8,128)} %get-tuple-element.63.small_ref) | copy-start | bytes 73732
  149.1 28.7 %all-to-all-start.2 = ((bf16[32,24,768]{2,1,0:T(8,128)(2,1)}), bf16[32,24,768]{2,1,0:T(8,128)(2,1)S(1)}, u32[]{:S(2)}, u32[]{:S(2)}) async-start(bf16[32,24,768]{2,1,0:T(8,128)(2,1)} %add_convert_fusion), calls=%async_computation.2 | async-start | bytes 2359296 | tf_op jit(solution)/shard_map/all_to_all | solution.py:469
  159.8 1.5 collective-permute-start.15
  161.3 0.6 copy-start.24
  161.3 1.0 copy-start.4
  177.7 1.0 copy-start.2
  178.8 25.4 %all-to-all-start.3 = ((bf16[32,24,1024]{2,1,0:T(8,128)(2,1)}), bf16[32,24,1024]{2,1,0:T(8,128)(2,1)S(1)}, u32[]{:S(2)}, u32[]{:S(2)}) async-start(bf16[32,24,1024]{2,1,0:T(8,128)(2,1)} %pay_b_rows.1), calls=%async_computation.3 | async-start | bytes 3145728 | tf_op jit(solution)/shard_map/all_to_all | solution.py:469
  185.4 28.5 %copy-start.12 = (f32[24,768]{1,0:T(8,128)S(1)}, f32[24,768]{1,0:T(8,128)}, u32[]{:S(2)}) copy-start(f32[24,768]{1,0:T(8,128)} %fold.2.refs_0_) | copy-start | bytes 221188
  185.4 31.0 %collective-permute-start.13 = (f32[24,768]{1,0:T(8,128)}, f32[24,768]{1,0:T(8,128)S(1)}, u32[]{:S(2)}, u32[]{:S(2)}) collective-permute-start(f32[24,768]{1,0:T(8,128)} %fold.2.refs_0_), channel_id=1, source_target_pairs={{0,96},{32,64},{64,32},{96,0},{1,97},{33,65},{65,33},{97,1},{2,98}... | collective-permute-start | bytes 221192 | tf_op jit(solution)/shard_map/ppermute | solution.py:493
  204.2 1.2 copy-start.1
  207.6 16.0 %collective-permute-start.18 = (f32[24,1024]{1,0:T(8,128)}, f32[24,1024]{1,0:T(8,128)S(1)}, u32[]{:S(2)}, u32[]{:S(2)}) collective-permute-start(f32[24,1024]{1,0:T(8,128)} %fold.3.refs_4_), channel_id=1, source_target_pairs={{0,96},{32,64},{64,32},{96,0},{1,97},{33,65},{65,33},{97,1},{2,98}... | collective-permute-start | bytes 294920 | tf_op jit(solution)/shard_map/ppermute | solution.py:493
  213.5 10.2 %collective-permute-start.17 = (f32[24,1024]{1,0:T(8,128)}, f32[24,1024]{1,0:T(8,128)S(1)}, u32[]{:S(2)}, u32[]{:S(2)}) collective-permute-start(f32[24,1024]{1,0:T(8,128)} %fold.3.refs_4_), channel_id=1, source_target_pairs={{0,64},{32,96},{64,0},{96,32},{1,65},{33,97},{65,1},{97,33},{2,66}... | collective-permute-start | bytes 294920 | tf_op jit(solution)/shard_map/ppermute | solution.py:493
  213.5 10.2 %collective-permute-start.16 = (f32[24,1024]{1,0:T(8,128)}, f32[24,1024]{1,0:T(8,128)S(1)}, u32[]{:S(2)}, u32[]{:S(2)}) collective-permute-start(f32[24,1024]{1,0:T(8,128)} %fold.3.refs_4_), channel_id=1, source_target_pairs={{0,32},{32,0},{64,96},{96,64},{1,33},{33,1},{65,97},{97,65},{2,34}... | collective-permute-start | bytes 294920 | tf_op jit(solution)/shard_map/ppermute | solution.py:493
  213.9 9.7 %collective-permute-start.12 = (f32[24,768]{1,0:T(8,128)S(1)}, f32[24,768]{1,0:T(8,128)S(1)}, u32[]{:S(2)}, u32[]{:S(2)}) collective-permute-start(f32[24,768]{1,0:T(8,128)S(1)} %copy-done.12), channel_id=1, source_target_pairs={{0,64},{32,96},{64,0},{96,32},{1,65},{33,97},{65,1},{97,33},{2,66}... | collective-permute-start | bytes 221192 | tf_op jit(solution)/shard_map/ppermute | solution.py:493
  216.5 7.1 %copy-start.20 = (f32[24,768]{1,0:T(8,128)}, f32[24,768]{1,0:T(8,128)S(1)}, u32[]{:S(2)}) copy-start(f32[24,768]{1,0:T(8,128)S(1)} %collective-permute-done.13.refs_3_) | copy-start | bytes 221188
  216.5 7.1 %collective-permute-start.11 = (f32[24,768]{1,0:T(8,128)S(1)}, f32[24,768]{1,0:T(8,128)S(1)}, u32[]{:S(2)}, u32[]{:S(2)}) collective-permute-start(f32[24,768]{1,0:T(8,128)S(1)} %copy-done.12), channel_id=1, source_target_pairs={{0,32},{32,0},{64,96},{96,64},{1,33},{33,1},{65,97},{97,65},{2,34}... | collective-permute-start | bytes 221192 | tf_op jit(solution)/shard_map/ppermute | solution.py:493
  223.6 0.6 copy-start.21
  223.6 0.7 copy-start.22
  223.6 0.7 copy-start.17
  223.7 0.7 copy-start.18
  224.4 0.7 copy-start.19

commit v4 on v3

--- a/solution.py
+++ b/solution.py
@@ -27,9 +27,9 @@
     return lax.dot_general(a, b, (((ca,), (cb,)), ((), ())), preferred_element_type=F32)
 
 
-def params(*semantics):
+def params(mib, *semantics):
     return pltpu.CompilerParams(
-        dimension_semantics=semantics or None, vmem_limit_bytes=56 * 1024 * 1024
+        dimension_semantics=semantics or None, vmem_limit_bytes=mib * 1024 * 1024
     )
 
 
@@ -114,7 +114,7 @@
             part,
             part,
         ],
-        compiler_params=params("arbitrary"),
+        compiler_params=params(56, "arbitrary"),
         name="tap_sums",
     )(tokens, qkv_weight, pool_kernel)
 
@@ -141,7 +141,7 @@
         out_specs=[pl.BlockSpec((HW, 2 * SPAN), lambda i: (0, 0))] * GROUPS,
         out_shape=[jax.ShapeDtypeStruct((HW, 2 * SPAN), BF)] * GROUPS,
         scratch_shapes=[pltpu.VMEM((GROUPS, HW, 2 * SPAN), BF)],
-        compiler_params=params("arbitrary"),
+        compiler_params=params(56, "arbitrary"),
         name="query_side",
     )(tokens, qkv_weight, cotangent, out_weight)
 
@@ -172,7 +172,7 @@
     return pl.pallas_call(
         norm_kernel,
         out_shape=[jax.ShapeDtypeStruct((2, GROUPS, 4, POS, 2 * SPAN), BF), flat, flat],
-        compiler_params=params(),
+        compiler_params=params(8),
         name="norm_side",
     )(low, own, up, gain)
 
@@ -238,7 +238,7 @@
         others_kernel,
         out_shape=[block, block, block, jax.ShapeDtypeStruct((kv.shape[1], kv.shape[0]), F32)],
         scratch_shapes=[pltpu.VMEM((3,) + block.shape, BF)],
-        compiler_params=params(),
+        compiler_params=params(20),
         name="attend_others",
     )(*qds, kv)
 
@@ -254,7 +254,7 @@
         own_kernel,
         out_shape=[jax.ShapeDtypeStruct(qd.shape, BF), jax.ShapeDtypeStruct(kv.shape, BF)],
         scratch_shapes=[pltpu.VMEM(start.shape, F32)],
-        compiler_params=params(),
+        compiler_params=params(20),
         name="attend_own",
     )(qd, kv, start)
 
@@ -283,7 +283,7 @@
             jax.ShapeDtypeStruct((POS, 2 * WIDTH), F32),
             jax.ShapeDtypeStruct((1, 2 * WIDTH), F32),
         ],
-        compiler_params=params(),
+        compiler_params=params(56),
         name="norm_back",
     )(parts, normed, inv, gain)
 
@@ -335,7 +335,7 @@
             jax.ShapeDtypeStruct((32, 24, WIDTH), BF),
             jax.ShapeDtypeStruct((24, 256), F32),
         ],
-        compiler_params=params(),
+        compiler_params=params(56),
         name="pool_back",
     )(up, own, low, taps, tap_tokens, pool_kernel, gain_sum)
 
@@ -356,7 +356,7 @@
     return pl.pallas_call(
         pay_b_kernel,
         out_shape=jax.ShapeDtypeStruct((32, 24, PAY_B), BF),
-        compiler_params=params(),
+        compiler_params=params(16),
         name="pay_b_rows",
     )(tap_tokens, dv, other, small, other_small)
 
@@ -391,7 +391,7 @@
             pltpu.VMEM((GROUPS, HW, 2 * SPAN), BF),
             pltpu.VMEM((2, 32, 24, WIDTH), BF),
         ],
-        compiler_params=params(),
+        compiler_params=params(56),
         name="output_side",
     )(*mds, tokens, cotangent, out_weight)
 
@@ -409,7 +409,7 @@
     return pl.pallas_call(
         token_grad_kernel,
         out_shape=jax.ShapeDtypeStruct((HW, WIDTH), BF),
-        compiler_params=params(),
+        compiler_params=params(56),
         name="token_grad",
     )(dq, dv, qkv_weight)
 
@@ -425,7 +425,7 @@
     return pl.pallas_call(
         fold_kernel,
         out_shape=jax.ShapeDtypeStruct(parts.shape[1:], F32),
-        compiler_params=params(),
+        compiler_params=params(8),
         name="fold",
     )(parts)
 
@@ -460,7 +460,7 @@
             jax.ShapeDtypeStruct((2, HEAD), F32),
         ],
         scratch_shapes=[pltpu.VMEM((2, 24, WIDTH), F32), pltpu.VMEM((2, 24, PAY_B), F32)],
-        compiler_params=params(),
+        compiler_params=params(56),
         name="finish",
     )(*a, *b)
 

time: 228 us -> 220 us (0.965)
  Pallas kernels: 68.4 us -> 57.5 us
  waiting for transfers between devices: 67.6 us -> 72.4 us
    pallas_call x2, Pallas kernels: 4.33 us -> 0.39 us  [fold(): pl.pallas_call(fold_kernel, out_shape=jax.ShapeDtypeStruct(parts.shape[1:...]
    all_to_all x3, waiting for transfers between devices: 25.9 us -> 29.1 us  [exchange(): return lax.all_to_all(array, axis, split_axis=0, concat_axis=0, tiled=True)]
    pallas_call x1, Pallas kernels: 18.9 us -> 16.1 us  [others(): pl.pallas_call(others_kernel, out_shape=[block, block, block, jax.ShapeDt...]
    pallas_call x1, Pallas kernels: 8.2 us -> 5.76 us  [own(): pl.pallas_call(own_kernel, out_shape=[jax.ShapeDtypeStruct(qd.shape, BF),...]
    unnamed x50 -> x46, local copies, waits for them, and re-layouts: 7.82 us -> 5.81 us
  transfers between devices with their start and end apart: 22 -> 22, of which waited for: 11 -> 11; matrix products, arithmetic and copies ran while one was open for 1% -> 1% of each run, Pallas kernels for 15% -> 12%
where the time goes in v4:
time: 220 us; the launch traced here: 219 us
  waiting for transfers between devices  72.4 us (33%)
  starting transfers between devices  62.9 us (29%)
  Pallas kernels  57.5 us (26%)
  blocking collectives  18.4 us (8%)
  local copies, waits for them, and re-layouts  5.81 us (3%)
    ppermute x6, waiting for transfers between devices, rotate(): lax.ppermute(array, 'tm_1', [(i, (i + steps) % GROUPS) for i in range(GRO...  30.7 us
    all_to_all x3, waiting for transfers between devices, exchange(): return lax.all_to_all(array, axis, split_axis=0, concat_axis=0, tiled=True)  29.1 us
    all_to_all x3, starting transfers between devices, exchange(): return lax.all_to_all(array, axis, split_axis=0, concat_axis=0, tiled=True)  26 us
    all_to_all x1, blocking collectives, exchange(): return lax.all_to_all(array, axis, split_axis=0, concat_axis=0, tiled=True)  18.4 us
    pallas_call x1, Pallas kernels, others(): pl.pallas_call(others_kernel, out_shape=[block, block, block, jax.ShapeDt...  16.1 us
    ppermute x6, starting transfers between devices, copies(): lax.ppermute(array, DP, [(i, i ^ k) for i in range(4)])  14.3 us
    ppermute x6, starting transfers between devices, rotate(): lax.ppermute(array, 'tm_1', [(i, (i + steps) % GROUPS) for i in range(GRO...  8.83 us
    ppermute x2, waiting for transfers between devices, to_previous(): lax.ppermute(array, TM, [(i + 1, i) for i in range(lax.axis_size(TM) - 1)])  7.22 us
  transfers between devices with their start and end apart: 22, of which 11 were waited for; matrix products, arithmetic and copies ran while one was open for 1% of the time, Pallas kernels for 12%

profile of v4, /device:TPU:1, one launch (start us, length us, event | category | flops | bytes accessed | tf_op | source)
XLA Modules:
  0.0 219.2 jit_solution(8691971225671405837)
XLA Ops:
  0.6 0.0 copy-start.10
  0.6 4.1 %tap_sums.1 = (bf16[288,1536]{1,0:T(8,128)(2,1)}, bf16[288,768]{1,0:T(8,128)(2,1)}, f32[32,1536]{1,0:T(8,128)}, f32[32,1536]{1,0:T(8,128)}, f32[32,1536]{1,0:T(8,128)}) custom-call(bf16[512,768]{1,0:T(8,128)(2,1)} %bitcast.13, bf16[768,2304]{1,0:T(8,128)(2,1)} %w_ref.5, f32[27,2,64]{2,1,0:T(2,128)} %bitcast.20), custom_call_target="tpu_custom_call" | custom-call | tf_op jit(solution)/shard_map/tap_sums/pallas_call | solution.py:95
  4.7 4.0 %collective-permute-start = (f32[32,1536]{1,0:T(8,128)}, f32[32,1536]{1,0:T(8,128)S(1)}, u32[]{:S(2)}, u32[]{:S(2)}) collective-permute-start(f32[32,1536]{1,0:T(8,128)} %get-tuple-element.38), channel_id=1, source_target_pairs={{0,1},{1,2},{2,3},{3,4},{4,5},{5,6},{6,7},{7,8},{8,9},{9,10},{10,1... | collective-permute-start | bytes 589832 | tf_op jit(solution)/shard_map/ppermute | solution.py:473
  8.8 1.3 collective-permute-start.1
  10.1 2.6 %collective-permute-done.low_ref = f32[32,1536]{1,0:T(8,128)S(1)} collective-permute-done((f32[32,1536]{1,0:T(8,128)}, f32[32,1536]{1,0:T(8,128)S(1)}, u32[]{:S(2)}, u32[]{:S(2)}) %collective-permute-start) | collective-permute-done | bytes 196640 | tf_op jit(solution)/shard_map/ppermute | solution.py:473
  12.6 3.7 %collective-permute-done.1.up_ref = f32[32,1536]{1,0:T(8,128)S(1)} collective-permute-done((f32[32,1536]{1,0:T(8,128)}, f32[32,1536]{1,0:T(8,128)S(1)}, u32[]{:S(2)}, u32[]{:S(2)}) %collective-permute-start.1) | collective-permute-done | bytes 196640 | tf_op jit(solution)/shard_map/ppermute | solution.py:477
  16.4 0.9 copy-done.6
  17.3 1.8 norm_side.1
  19.1 0.7 copy-done.7
  19.8 0.7 copy-done.8
  20.5 10.7 %all-to-all-start = ((bf16[32,32,384]{2,1,0:T(8,128)(2,1)}), bf16[32,32,384]{2,1,0:T(8,128)(2,1)S(1)}, u32[]{:S(2)}, u32[]{:S(2)}) async-start(bf16[32,32,384]{2,1,0:T(8,128)(2,1)} %bitcast.3), calls=%async_computation | async-start | bytes 1572864 | tf_op jit(solution)/shard_map/all_to_all | solution.py:469
  31.2 4.8 %query_side.1 = (bf16[512,384]{1,0:T(8,128)(2,1)}, bf16[512,384]{1,0:T(8,128)(2,1)}, bf16[512,384]{1,0:T(8,128)(2,1)}, bf16[512,384]{1,0:T(8,128)(2,1)}) custom-call(bf16[512,768]{1,0:T(8,128)(2,1)} %bitcast.14, bf16[768,2304]{1,0:T(8,128)(2,1)} %w_ref.5, bf16[512,768]{1,0:T(8,128)(2,1)} %bitcast.17, bf16[768,768]{1,0:T(8,128)(2,1)} %ow_ref.3), custom_call_target="tpu_custom_call" | custom-call | tf_op jit(solution)/shard_map/query_side/pallas_call | solution.py:137
  36.0 1.2 collective-permute-start.2
  37.2 2.4 %collective-permute-start.3 = (bf16[512,384]{1,0:T(8,128)(2,1)}, bf16[512,384]{1,0:T(8,128)(2,1)S(1)}, u32[]{:S(2)}, u32[]{:S(2)}) collective-permute-start(bf16[512,384]{1,0:T(8,128)(2,1)} %get-tuple-element.43), channel_id=1, source_target_pairs={{0,8},{4,12},{8,0},{12,4},{1,9},{5,13},{9,1},{13,5},{2,10},{6,14},... | collective-permute-start | bytes 1179656 | tf_op jit(solution)/shard_map/ppermute | solution.py:481
  39.6 1.2 collective-permute-start.4
  40.8 10.8 %collective-permute-done.2.q0_ref = bf16[512,384]{1,0:T(8,128)(2,1)S(1)} collective-permute-done((bf16[512,384]{1,0:T(8,128)(2,1)}, bf16[512,384]{1,0:T(8,128)(2,1)S(1)}, u32[]{:S(2)}, u32[]{:S(2)}) %collective-permute-start.2) | collective-permute-done | bytes 393248 | tf_op jit(solution)/shard_map/ppermute | solution.py:481
  51.6 6.4 %collective-permute-done.3.q1_ref = bf16[512,384]{1,0:T(8,128)(2,1)S(1)} collective-permute-done((bf16[512,384]{1,0:T(8,128)(2,1)}, bf16[512,384]{1,0:T(8,128)(2,1)S(1)}, u32[]{:S(2)}, u32[]{:S(2)}) %collective-permute-start.3) | collective-permute-done | bytes 393248 | tf_op jit(solution)/shard_map/ppermute | solution.py:481
  58.0 16.1 %attend_others.1 = (bf16[512,384]{1,0:T(8,128)(2,1)S(1)}, bf16[512,384]{1,0:T(8,128)(2,1)S(1)}, bf16[512,384]{1,0:T(8,128)(2,1)S(1)}, f32[384,1024]{1,0:T(8,128)S(1)}) custom-call(bf16[512,384]{1,0:T(8,128)(2,1)S(1)} %collective-permute-done.2.q0_ref, bf16[512,384]{1,0:T(8,128)(2,1)S(1)} %collective-permute-done.3.q1_ref, ...), custom_call_target="tpu_custom_call" | custom-call | tf_op jit(solution)/shard_map/attend_others/pallas_call | solution.py:237
  74.1 3.3 %collective-permute-start.5 = (bf16[512,384]{1,0:T(8,128)(2,1)S(1)}, bf16[512,384]{1,0:T(8,128)(2,1)S(1)}, u32[]{:S(2)}, u32[]{:S(2)}) collective-permute-start(bf16[512,384]{1,0:T(8,128)(2,1)S(1)} %get-tuple-element.47), channel_id=1, source_target_pairs={{0,12},{4,0},{8,4},{12,8},{1,13},{5,1},{9,5},{13,9},{2,14},{6,2},{... | collective-permute-start | bytes 1179656 | tf_op jit(solution)/shard_map/ppermute | solution.py:481
  77.4 0.1 collective-permute-start.6
  77.5 0.5 collective-permute-start.7
  78.1 5.8 %attend_own.1 = (bf16[512,384]{1,0:T(8,128)(2,1)S(1)}, bf16[1024,384]{1,0:T(8,128)(2,1)S(1)}) custom-call(bf16[512,384]{1,0:T(8,128)(2,1)S(1)} %copy-done.4, bf16[1024,384]{1,0:T(8,128)(2,1)S(1)} %bitcast.11, f32[384,1024]{1,0:T(8,128)S(1)} %get-tuple-element.45.start_ref), custom_call_target="tpu_custom_call" | custom-call | tf_op jit(solution)/shard_map/attend_own/pallas_call | solution.py:253
  83.9 0.0 copy-start.2
  83.9 0.7 copy-done.2
  84.6 9.1 %collective-permute-done.5.m1_ref = bf16[512,384]{1,0:T(8,128)(2,1)S(1)} collective-permute-done((bf16[512,384]{1,0:T(8,128)(2,1)S(1)}, bf16[512,384]{1,0:T(8,128)(2,1)S(1)}, u32[]{:S(2)}, u32[]{:S(2)}) %collective-permute-start.5) | collective-permute-done | bytes 393248 | tf_op jit(solution)/shard_map/ppermute | solution.py:481
  93.7 4.3 %collective-permute-done.7.m3_ref = bf16[512,384]{1,0:T(8,128)(2,1)S(1)} collective-permute-done((bf16[512,384]{1,0:T(8,128)(2,1)S(1)}, bf16[512,384]{1,0:T(8,128)(2,1)S(1)}, u32[]{:S(2)}, u32[]{:S(2)}) %collective-permute-start.7) | collective-permute-done | bytes 393248 | tf_op jit(solution)/shard_map/ppermute | solution.py:481
  98.1 0.7 copy-done.14
  98.8 6.2 %output_side.1 = (bf16[512,768]{1,0:T(8,128)(2,1)}, bf16[512,768]{1,0:T(8,128)(2,1)}, bf16[32,24,768]{2,1,0:T(8,128)(2,1)}, bf16[32,24,768]{2,1,0:T(8,128)(2,1)}) custom-call(bf16[512,384]{1,0:T(8,128)(2,1)} %copy-done.2, bf16[512,384]{1,0:T(8,128)(2,1)} %copy-done.12, bf16[512,384]{1,0:T(8,128)(2,1)} %copy-done.13, bf16[512,384]{1,0:T(8,128)(2,1)} %copy-done.14, ...), custom_call_target="tpu_custom_call" | custom-call | tf_op jit(solution)/shard_map/output_side/pallas_call | solution.py:387
  105.1 0.6 collective-permute-start.10
  105.7 18.4 %all_to_all.20 = bf16[32,32,384]{2,1,0:T(8,128)(2,1)} all-to-all(bf16[32,32,384]{2,1,0:T(8,128)(2,1)S(1)} %bitcast.12), channel_id=1, replica_groups=mesh['dp_0'=2,'dp_1'=2,'tm_0'=2,'tm_1'=4,'tm_2'=4] {'tm_0','tm_1','tm_2'}, dimensions={0} | all-to-all | bytes 1572864 | tf_op jit(solution)/shard_map/all_to_all | solution.py:469
  124.1 2.5 %norm_back.1 = (f32[32,1536]{1,0:T(8,128)}, f32[1,1536]{1,0:T(1,128)}) custom-call(bf16[2,4,4,32,384]{4,3,2,1,0:T(8,128)(2,1)} %bitcast.16, f32[32,1536]{1,0:T(8,128)} %copy-done.7, f32[32,1536]{1,0:T(8,128)} %copy-done.8, f32[2,64]{1,0:T(2,128)} %gain_ref.3), custom_call_target="tpu_custom_call" | custom-call | tf_op jit(solution)/shard_map/norm_back/pallas_call | solution.py:280
  126.7 3.1 %collective-permute-start.9 = (f32[32,1536]{1,0:T(8,128)}, f32[32,1536]{1,0:T(8,128)S(1)}, u32[]{:S(2)}, u32[]{:S(2)}) collective-permute-start(f32[32,1536]{1,0:T(8,128)} %get-tuple-element.55.own_ref), channel_id=1, source_target_pairs={{0,1},{1,2},{2,3},{3,4},{4,5},{5,6},{6,7},{7,8},{8,9},{9,10},{10,1... | collective-permute-start | bytes 589832 | tf_op jit(solution)/shard_map/ppermute | solution.py:473
  129.8 1.3 collective-permute-start.8
  131.1 1.8 collective-permute-done.9.low_ref
  132.9 3.5 %collective-permute-done.8.up_ref = f32[32,1536]{1,0:T(8,128)S(1)} collective-permute-done((f32[32,1536]{1,0:T(8,128)}, f32[32,1536]{1,0:T(8,128)S(1)}, u32[]{:S(2)}, u32[]{:S(2)}) %collective-permute-start.8) | collective-permute-done | bytes 196640 | tf_op jit(solution)/shard_map/ppermute | solution.py:477
  136.4 0.7 copy-done.16
  137.1 4.2 %pool_back.1 = (bf16[2,288,768]{2,1,0:T(8,128)(2,1)}, bf16[32,24,768]{2,1,0:T(8,128)(2,1)}, f32[24,256]{1,0:T(8,128)}) custom-call(f32[32,1536]{1,0:T(8,128)} %copy-done.16, f32[32,1536]{1,0:T(8,128)} %get-tuple-element.55.own_ref, f32[32,1536]{1,0:T(8,128)} %copy-done.15, bf16[288,1536]{1,0:T(8,128)(2,1)} %get-tuple-element.56.taps_ref, ...), custom_call_target="tpu_custom_call" | custom-call | tf_op jit(solution)/shard_map/pool_back/pallas_call | solution.py:331
  141.3 2.8 %collective-permute-start.14 = (bf16[32,24,768]{2,1,0:T(8,128)(2,1)}, bf16[32,24,768]{2,1,0:T(8,128)(2,1)}, u32[]{:S(2)}, u32[]{:S(2)}) collective-permute-start(bf16[32,24,768]{2,1,0:T(8,128)(2,1)} %get-tuple-element.62), channel_id=1, source_target_pairs={{0,32},{32,0},{1,33},{33,1},{2,34},{34,2},{3,35},{35,3},{4,36},{36... | collective-permute-start | bytes 3538952 | tf_op jit(solution)/shard_map/ppermute | solution.py:485
  144.1 1.3 add_convert_fusion
  145.5 10.7 %all-to-all-start.2 = ((bf16[32,24,768]{2,1,0:T(8,128)(2,1)}), bf16[32,24,768]{2,1,0:T(8,128)(2,1)S(1)}, u32[]{:S(2)}, u32[]{:S(2)}) async-start(bf16[32,24,768]{2,1,0:T(8,128)(2,1)} %add_convert_fusion), calls=%async_computation.2 | async-start | bytes 2359296 | tf_op jit(solution)/shard_map/all_to_all | solution.py:469
  156.2 0.6 collective-permute-start.15
  156.8 0.9 collective-permute-done.15.other_small_ref
  157.7 0.0 collective-permute-done.14.other_ref
  157.7 3.3 %pay_b_rows.1 = bf16[32,24,1024]{2,1,0:T(8,128)(2,1)} custom-call(bf16[288,768]{1,0:T(8,128)(2,1)S(1)} %copy-done.1, bf16[2,288,768]{2,1,0:T(8,128)(2,1)S(1)} %copy-done, bf16[32,24,768]{2,1,0:T(8,128)(2,1)} %collective-permute-done.14.other_ref, f32[24,256]{1,0:T(8,128)S(1)} %copy-done.9, f32[24,256]{1,0:T(8,128)S(1)} %collective-permute-done.15.other_small_ref), custom_call_target="tpu_custom_call" | custom-call | tf_op jit(solution)/shard_map/pay_b_rows/pallas_call | solution.py:356
  161.0 13.1 %all-to-all-done.2.parts_ref = bf16[32,24,768]{2,1,0:T(8,128)(2,1)S(1)} async-done(((bf16[32,24,768]{2,1,0:T(8,128)(2,1)}), bf16[32,24,768]{2,1,0:T(8,128)(2,1)S(1)}, u32[]{:S(2)}, u32[]{:S(2)}) %all-to-all-start.2) | async-done | bytes 1179680 | tf_op jit(solution)/shard_map/all_to_all | solution.py:469
  174.1 4.6 %all-to-all-start.3 = ((bf16[32,24,1024]{2,1,0:T(8,128)(2,1)}), bf16[32,24,1024]{2,1,0:T(8,128)(2,1)S(1)}, u32[]{:S(2)}, u32[]{:S(2)}) async-start(bf16[32,24,1024]{2,1,0:T(8,128)(2,1)} %pay_b_rows.1), calls=%async_computation.3 | async-start | bytes 3145728 | tf_op jit(solution)/shard_map/all_to_all | solution.py:469
  178.7 0.2 fold.2.refs_0_
  178.9 4.6 %collective-permute-start.13 = (f32[24,768]{1,0:T(8,128)S(1)}, f32[24,768]{1,0:T(8,128)S(1)}, u32[]{:S(2)}, u32[]{:S(2)}) collective-permute-start(f32[24,768]{1,0:T(8,128)S(1)} %fold.2.refs_0_), channel_id=1, source_target_pairs={{0,96},{32,64},{64,32},{96,0},{1,97},{33,65},{65,33},{97,1},{2,98}... | collective-permute-start | bytes 221192 | tf_op jit(solution)/shard_map/ppermute | solution.py:493
  183.5 16.0 %all-to-all-done.3.parts_ref = bf16[32,24,1024]{2,1,0:T(8,128)(2,1)S(1)} async-done(((bf16[32,24,1024]{2,1,0:T(8,128)(2,1)}), bf16[32,24,1024]{2,1,0:T(8,128)(2,1)S(1)}, u32[]{:S(2)}, u32[]{:S(2)}) %all-to-all-start.3) | async-done | bytes 1572896 | tf_op jit(solution)/shard_map/all_to_all | solution.py:469
  199.5 0.2 fold.3.refs_4_
  199.7 6.0 %collective-permute-start.18 = (f32[24,1024]{1,0:T(8,128)S(1)}, f32[24,1024]{1,0:T(8,128)S(1)}, u32[]{:S(2)}, u32[]{:S(2)}) collective-permute-start(f32[24,1024]{1,0:T(8,128)S(1)} %fold.3.refs_4_), channel_id=1, source_target_pairs={{0,96},{32,64},{64,32},{96,0},{1,97},{33,65},{65,33},{97,1},{2,98}... | collective-permute-start | bytes 294920 | tf_op jit(solution)/shard_map/ppermute | solution.py:493
  205.7 0.0 collective-permute-start.17
  205.7 0.5 collective-permute-start.16
  206.2 2.5 %collective-permute-start.12 = (f32[24,768]{1,0:T(8,128)S(1)}, f32[24,768]{1,0:T(8,128)S(1)}, u32[]{:S(2)}, u32[]{:S(2)}) collective-permute-start(f32[24,768]{1,0:T(8,128)S(1)} %fold.2.refs_0_), channel_id=1, source_target_pairs={{0,64},{32,96},{64,0},{96,32},{1,65},{33,97},{65,1},{97,33},{2,66}... | collective-permute-start | bytes 221192 | tf_op jit(solution)/shard_map/ppermute | solution.py:493
  208.7 0.8 collective-permute-start.11
  209.5 6.3 %token_grad.1 = bf16[512,768]{1,0:T(8,128)(2,1)} custom-call(bf16[512,768]{1,0:T(8,128)(2,1)} %get-tuple-element.51.dq_ref, bf16[2,288,768]{2,1,0:T(8,128)(2,1)} %get-tuple-element.59.dv_ref, bf16[768,2304]{1,0:T(8,128)(2,1)} %w_ref.5), custom_call_target="tpu_custom_call" | custom-call | tf_op jit(solution)/shard_map/token_grad/pallas_call | solution.py:409
  215.8 0.0 collective-permute-done.12.refs_2_
  215.8 0.0 collective-permute-done.11.refs_1_
  215.9 0.5 copy-done.21
  216.5 0.0 copy-done.22
  216.5 0.0 copy-done.17
  216.5 0.0 copy-done.18
  216.6 0.6 copy-done.19
  217.2 2.0 finish.1
  (41 shorter events, 0.1 us)
Async XLA Ops:
  0.6 15.8 %copy-start.10 = (f32[2,64]{1,0:T(2,128)S(1)}, f32[2,64]{1,0:T(2,128)}, u32[]{:S(2)}) copy-start(f32[2,64]{1,0:T(2,128)} %gain_ref.3) | copy-start | bytes 1540
  4.7 7.9 %collective-permute-start = (f32[32,1536]{1,0:T(8,128)}, f32[32,1536]{1,0:T(8,128)S(1)}, u32[]{:S(2)}, u32[]{:S(2)}) collective-permute-start(f32[32,1536]{1,0:T(8,128)} %get-tuple-element.38), channel_id=1, source_target_pairs={{0,1},{1,2},{2,3},{3,4},{4,5},{5,6},{6,7},{7,8},{8,9},{9,10},{10,1... | collective-permute-start | bytes 589832 | tf_op jit(solution)/shard_map/ppermute | solution.py:473
  8.8 7.6 %collective-permute-start.1 = (f32[32,1536]{1,0:T(8,128)}, f32[32,1536]{1,0:T(8,128)S(1)}, u32[]{:S(2)}, u32[]{:S(2)}) collective-permute-start(f32[32,1536]{1,0:T(8,128)} %get-tuple-element.40), channel_id=1, source_target_pairs={{1,0},{2,1},{3,2},{4,3},{5,4},{6,5},{7,6},{8,7},{9,8},{10,9},{11,1... | collective-permute-start | bytes 589832 | tf_op jit(solution)/shard_map/ppermute | solution.py:477
  16.4 0.9 copy-start.6
  19.1 0.7 copy-start.7
  19.8 0.7 copy-start.8
  20.5 37.5 %all-to-all-start = ((bf16[32,32,384]{2,1,0:T(8,128)(2,1)}), bf16[32,32,384]{2,1,0:T(8,128)(2,1)S(1)}, u32[]{:S(2)}, u32[]{:S(2)}) async-start(bf16[32,32,384]{2,1,0:T(8,128)(2,1)} %bitcast.3), calls=%async_computation | async-start | bytes 1572864 | tf_op jit(solution)/shard_map/all_to_all | solution.py:469
  36.0 42.1 %copy-start.4 = (bf16[512,384]{1,0:T(8,128)(2,1)S(1)}, bf16[512,384]{1,0:T(8,128)(2,1)}, u32[]{:S(2)}) copy-start(bf16[512,384]{1,0:T(8,128)(2,1)} %get-tuple-element.37.qd_ref) | copy-start | bytes 1179652
  36.0 15.7 %collective-permute-start.2 = (bf16[512,384]{1,0:T(8,128)(2,1)}, bf16[512,384]{1,0:T(8,128)(2,1)S(1)}, u32[]{:S(2)}, u32[]{:S(2)}) collective-permute-start(bf16[512,384]{1,0:T(8,128)(2,1)} %get-tuple-element.42), channel_id=1, source_target_pairs={{0,4},{4,8},{8,12},{12,0},{1,5},{5,9},{9,13},{13,1},{2,6},{6,10},{... | collective-permute-start | bytes 1179656 | tf_op jit(solution)/shard_map/ppermute | solution.py:481
  37.2 20.8 %collective-permute-start.3 = (bf16[512,384]{1,0:T(8,128)(2,1)}, bf16[512,384]{1,0:T(8,128)(2,1)S(1)}, u32[]{:S(2)}, u32[]{:S(2)}) collective-permute-start(bf16[512,384]{1,0:T(8,128)(2,1)} %get-tuple-element.43), channel_id=1, source_target_pairs={{0,8},{4,12},{8,0},{12,4},{1,9},{5,13},{9,1},{13,5},{2,10},{6,14},... | collective-permute-start | bytes 1179656 | tf_op jit(solution)/shard_map/ppermute | solution.py:481
  39.6 18.4 %collective-permute-start.4 = (bf16[512,384]{1,0:T(8,128)(2,1)}, bf16[512,384]{1,0:T(8,128)(2,1)S(1)}, u32[]{:S(2)}, u32[]{:S(2)}) collective-permute-start(bf16[512,384]{1,0:T(8,128)(2,1)} %get-tuple-element.44), channel_id=1, source_target_pairs={{0,12},{4,0},{8,4},{12,8},{1,13},{5,1},{9,5},{13,9},{2,14},{6,2},{... | collective-permute-start | bytes 1179656 | tf_op jit(solution)/shard_map/ppermute | solution.py:481
  74.1 19.6 %collective-permute-start.5 = (bf16[512,384]{1,0:T(8,128)(2,1)S(1)}, bf16[512,384]{1,0:T(8,128)(2,1)S(1)}, u32[]{:S(2)}, u32[]{:S(2)}) collective-permute-start(bf16[512,384]{1,0:T(8,128)(2,1)S(1)} %get-tuple-element.47), channel_id=1, source_target_pairs={{0,12},{4,0},{8,4},{12,8},{1,13},{5,1},{9,5},{13,9},{2,14},{6,2},{... | collective-permute-start | bytes 1179656 | tf_op jit(solution)/shard_map/ppermute | solution.py:481
  77.4 16.3 %collective-permute-start.6 = (bf16[512,384]{1,0:T(8,128)(2,1)S(1)}, bf16[512,384]{1,0:T(8,128)(2,1)S(1)}, u32[]{:S(2)}, u32[]{:S(2)}) collective-permute-start(bf16[512,384]{1,0:T(8,128)(2,1)S(1)} %get-tuple-element.48), channel_id=1, source_target_pairs={{0,8},{4,12},{8,0},{12,4},{1,9},{5,13},{9,1},{13,5},{2,10},{6,14},... | collective-permute-start | bytes 1179656 | tf_op jit(solution)/shard_map/ppermute | solution.py:481
  77.5 20.5 %collective-permute-start.7 = (bf16[512,384]{1,0:T(8,128)(2,1)S(1)}, bf16[512,384]{1,0:T(8,128)(2,1)S(1)}, u32[]{:S(2)}, u32[]{:S(2)}) collective-permute-start(bf16[512,384]{1,0:T(8,128)(2,1)S(1)} %get-tuple-element.49), channel_id=1, source_target_pairs={{0,4},{4,8},{8,12},{12,0},{1,5},{5,9},{9,13},{13,1},{2,6},{6,10},{... | collective-permute-start | bytes 1179656 | tf_op jit(solution)/shard_map/ppermute | solution.py:481
  83.9 0.7 copy-start.2
  93.7 4.4 %copy-start.12 = (bf16[512,384]{1,0:T(8,128)(2,1)}, bf16[512,384]{1,0:T(8,128)(2,1)S(1)}, u32[]{:S(2)}) copy-start(bf16[512,384]{1,0:T(8,128)(2,1)S(1)} %collective-permute-done.5.m1_ref) | copy-start | bytes 1179652
  93.7 4.4 %copy-start.13 = (bf16[512,384]{1,0:T(8,128)(2,1)}, bf16[512,384]{1,0:T(8,128)(2,1)S(1)}, u32[]{:S(2)}) copy-start(bf16[512,384]{1,0:T(8,128)(2,1)S(1)} %collective-permute-done.6.m2_ref) | copy-start | bytes 1179652
  98.1 0.8 copy-start.14
  105.1 39.1 %collective-permute-start.10 = (bf16[32,24,768]{2,1,0:T(8,128)(2,1)}, bf16[32,24,768]{2,1,0:T(8,128)(2,1)S(1)}, u32[]{:S(2)}, u32[]{:S(2)}) collective-permute-start(bf16[32,24,768]{2,1,0:T(8,128)(2,1)} %get-tuple-element.61), channel_id=1, source_target_pairs={{0,32},{32,0},{1,33},{33,1},{2,34},{34,2},{3,35},{35,3},{4,36},{36... | collective-permute-start | bytes 3538952 | tf_op jit(solution)/shard_map/ppermute | solution.py:485
  126.7 17.4 %copy-start.11 = (bf16[32,24,768]{2,1,0:T(8,128)(2,1)S(1)}, bf16[32,24,768]{2,1,0:T(8,128)(2,1)}, u32[]{:S(2)}) copy-start(bf16[32,24,768]{2,1,0:T(8,128)(2,1)} %get-tuple-element.60) | copy-start | bytes 3538948
  126.7 6.2 %collective-permute-start.9 = (f32[32,1536]{1,0:T(8,128)}, f32[32,1536]{1,0:T(8,128)S(1)}, u32[]{:S(2)}, u32[]{:S(2)}) collective-permute-start(f32[32,1536]{1,0:T(8,128)} %get-tuple-element.55.own_ref), channel_id=1, source_target_pairs={{0,1},{1,2},{2,3},{3,4},{4,5},{5,6},{6,7},{7,8},{8,9},{9,10},{10,1... | collective-permute-start | bytes 589832 | tf_op jit(solution)/shard_map/ppermute | solution.py:473
  129.8 6.6 %collective-permute-start.8 = (f32[32,1536]{1,0:T(8,128)}, f32[32,1536]{1,0:T(8,128)S(1)}, u32[]{:S(2)}, u32[]{:S(2)}) collective-permute-start(f32[32,1536]{1,0:T(8,128)} %get-tuple-element.55.own_ref), channel_id=1, source_target_pairs={{1,0},{2,1},{3,2},{4,3},{5,4},{6,5},{7,6},{8,7},{9,8},{10,9},{11,1... | collective-permute-start | bytes 589832 | tf_op jit(solution)/shard_map/ppermute | solution.py:477
  132.9 3.5 %copy-start.15 = (f32[32,1536]{1,0:T(8,128)}, f32[32,1536]{1,0:T(8,128)S(1)}, u32[]{:S(2)}) copy-start(f32[32,1536]{1,0:T(8,128)S(1)} %collective-permute-done.9.low_ref) | copy-start | bytes 589828
  136.4 0.7 copy-start.16
  141.3 16.4 %collective-permute-start.14 = (bf16[32,24,768]{2,1,0:T(8,128)(2,1)}, bf16[32,24,768]{2,1,0:T(8,128)(2,1)}, u32[]{:S(2)}, u32[]{:S(2)}) collective-permute-start(bf16[32,24,768]{2,1,0:T(8,128)(2,1)} %get-tuple-element.62), channel_id=1, source_target_pairs={{0,32},{32,0},{1,33},{33,1},{2,34},{34,2},{3,35},{35,3},{4,36},{36... | collective-permute-start | bytes 3538952 | tf_op jit(solution)/shard_map/ppermute | solution.py:485
  145.4 10.8 %copy-start.9 = (f32[24,256]{1,0:T(8,128)S(1)}, f32[24,256]{1,0:T(8,128)}, u32[]{:S(2)}) copy-start(f32[24,256]{1,0:T(8,128)} %get-tuple-element.63.small_ref) | copy-start | bytes 73732
  145.5 12.3 %copy-start = (bf16[2,288,768]{2,1,0:T(8,128)(2,1)S(1)}, bf16[2,288,768]{2,1,0:T(8,128)(2,1)}, u32[]{:S(2)}) copy-start(bf16[2,288,768]{2,1,0:T(8,128)(2,1)} %get-tuple-element.59.dv_ref) | copy-start | bytes 2654212
  145.5 12.3 %copy-start.1 = (bf16[288,768]{1,0:T(8,128)(2,1)S(1)}, bf16[288,768]{1,0:T(8,128)(2,1)}, u32[]{:S(2)}) copy-start(bf16[288,768]{1,0:T(8,128)(2,1)} %get-tuple-element.57.tt_ref) | copy-start | bytes 1327108
  145.5 28.7 %all-to-all-start.2 = ((bf16[32,24,768]{2,1,0:T(8,128)(2,1)}), bf16[32,24,768]{2,1,0:T(8,128)(2,1)S(1)}, u32[]{:S(2)}, u32[]{:S(2)}) async-start(bf16[32,24,768]{2,1,0:T(8,128)(2,1)} %add_convert_fusion), calls=%async_computation.2 | async-start | bytes 2359296 | tf_op jit(solution)/shard_map/all_to_all | solution.py:469
  156.2 1.5 collective-permute-start.15
  174.1 25.4 %all-to-all-start.3 = ((bf16[32,24,1024]{2,1,0:T(8,128)(2,1)}), bf16[32,24,1024]{2,1,0:T(8,128)(2,1)S(1)}, u32[]{:S(2)}, u32[]{:S(2)}) async-start(bf16[32,24,1024]{2,1,0:T(8,128)(2,1)} %pay_b_rows.1), calls=%async_computation.3 | async-start | bytes 3145728 | tf_op jit(solution)/shard_map/all_to_all | solution.py:469
  178.9 36.9 %copy-start.5 = (f32[24,768]{1,0:T(8,128)}, f32[24,768]{1,0:T(8,128)S(1)}, u32[]{:S(2)}) copy-start(f32[24,768]{1,0:T(8,128)S(1)} %fold.2.refs_0_) | copy-start | bytes 221188
  178.9 29.8 %collective-permute-start.13 = (f32[24,768]{1,0:T(8,128)S(1)}, f32[24,768]{1,0:T(8,128)S(1)}, u32[]{:S(2)}, u32[]{:S(2)}) collective-permute-start(f32[24,768]{1,0:T(8,128)S(1)} %fold.2.refs_0_), channel_id=1, source_target_pairs={{0,96},{32,64},{64,32},{96,0},{1,97},{33,65},{65,33},{97,1},{2,98}... | collective-permute-start | bytes 221192 | tf_op jit(solution)/shard_map/ppermute | solution.py:493
  199.7 16.1 %copy-start.3 = (f32[24,1024]{1,0:T(8,128)}, f32[24,1024]{1,0:T(8,128)S(1)}, u32[]{:S(2)}) copy-start(f32[24,1024]{1,0:T(8,128)S(1)} %fold.3.refs_4_) | copy-start | bytes 294916
  199.7 16.1 %collective-permute-start.18 = (f32[24,1024]{1,0:T(8,128)S(1)}, f32[24,1024]{1,0:T(8,128)S(1)}, u32[]{:S(2)}, u32[]{:S(2)}) collective-permute-start(f32[24,1024]{1,0:T(8,128)S(1)} %fold.3.refs_4_), channel_id=1, source_target_pairs={{0,96},{32,64},{64,32},{96,0},{1,97},{33,65},{65,33},{97,1},{2,98}... | collective-permute-start | bytes 294920 | tf_op jit(solution)/shard_map/ppermute | solution.py:493
  205.7 10.2 %collective-permute-start.17 = (f32[24,1024]{1,0:T(8,128)S(1)}, f32[24,1024]{1,0:T(8,128)S(1)}, u32[]{:S(2)}, u32[]{:S(2)}) collective-permute-start(f32[24,1024]{1,0:T(8,128)S(1)} %fold.3.refs_4_), channel_id=1, source_target_pairs={{0,64},{32,96},{64,0},{96,32},{1,65},{33,97},{65,1},{97,33},{2,66}... | collective-permute-start | bytes 294920 | tf_op jit(solution)/shard_map/ppermute | solution.py:493
  205.7 10.2 %collective-permute-start.16 = (f32[24,1024]{1,0:T(8,128)S(1)}, f32[24,1024]{1,0:T(8,128)S(1)}, u32[]{:S(2)}, u32[]{:S(2)}) collective-permute-start(f32[24,1024]{1,0:T(8,128)S(1)} %fold.3.refs_4_), channel_id=1, source_target_pairs={{0,32},{32,0},{64,96},{96,64},{1,33},{33,1},{65,97},{97,65},{2,34}... | collective-permute-start | bytes 294920 | tf_op jit(solution)/shard_map/ppermute | solution.py:493
  206.2 9.6 %collective-permute-start.12 = (f32[24,768]{1,0:T(8,128)S(1)}, f32[24,768]{1,0:T(8,128)S(1)}, u32[]{:S(2)}, u32[]{:S(2)}) collective-permute-start(f32[24,768]{1,0:T(8,128)S(1)} %fold.2.refs_0_), channel_id=1, source_target_pairs={{0,64},{32,96},{64,0},{96,32},{1,65},{33,97},{65,1},{97,33},{2,66}... | collective-permute-start | bytes 221192 | tf_op jit(solution)/shard_map/ppermute | solution.py:493
  208.7 7.1 %copy-start.20 = (f32[24,768]{1,0:T(8,128)}, f32[24,768]{1,0:T(8,128)S(1)}, u32[]{:S(2)}) copy-start(f32[24,768]{1,0:T(8,128)S(1)} %collective-permute-done.13.refs_3_) | copy-start | bytes 221188
  208.7 7.2 %collective-permute-start.11 = (f32[24,768]{1,0:T(8,128)S(1)}, f32[24,768]{1,0:T(8,128)S(1)}, u32[]{:S(2)}, u32[]{:S(2)}) collective-permute-start(f32[24,768]{1,0:T(8,128)S(1)} %fold.2.refs_0_), channel_id=1, source_target_pairs={{0,32},{32,0},{64,96},{96,64},{1,33},{33,1},{65,97},{97,65},{2,34}... | collective-permute-start | bytes 221192 | tf_op jit(solution)/shard_map/ppermute | solution.py:493
  215.8 0.6 copy-start.21
  215.8 0.6 copy-start.22
  215.9 0.7 copy-start.17
  215.9 0.7 copy-start.18
  216.6 0.6 copy-start.19

commit v5 on v4

--- a/solution.py
+++ b/solution.py
@@ -283,7 +283,7 @@
             jax.ShapeDtypeStruct((POS, 2 * WIDTH), F32),
             jax.ShapeDtypeStruct((1, 2 * WIDTH), F32),
         ],
-        compiler_params=params(56),
+        compiler_params=params(40),
         name="norm_back",
     )(parts, normed, inv, gain)
 
@@ -335,7 +335,7 @@
             jax.ShapeDtypeStruct((32, 24, WIDTH), BF),
             jax.ShapeDtypeStruct((24, 256), F32),
         ],
-        compiler_params=params(56),
+        compiler_params=params(40),
         name="pool_back",
     )(up, own, low, taps, tap_tokens, pool_kernel, gain_sum)
 
@@ -460,7 +460,7 @@
             jax.ShapeDtypeStruct((2, HEAD), F32),
         ],
         scratch_shapes=[pltpu.VMEM((2, 24, WIDTH), F32), pltpu.VMEM((2, 24, PAY_B), F32)],
-        compiler_params=params(56),
+        compiler_params=params(8),
         name="finish",
     )(*a, *b)
 

time: 220 us -> 212 us (0.964)
  Pallas kernels: 57.5 us -> 53 us
  local copies, waits for them, and re-layouts: 5.81 us -> 2.45 us
    unnamed x46 -> x24, local copies, waits for them, and re-layouts: 5.81 us -> 2.45 us
  transfers between devices with their start and end apart: 22 -> 22, of which waited for: 11 -> 11; matrix products, arithmetic and copies ran while one was open for 1% -> 1% of each run, Pallas kernels for 12% -> 11%
where the time goes in v5:
time: 212 us; the launch traced here: 211 us
  waiting for transfers between devices  72 us (34%)
  starting transfers between devices  62.9 us (30%)
  Pallas kernels  53 us (25%)
  blocking collectives  18.6 us (9%)
  local copies, waits for them, and re-layouts  2.45 us (1%)
    ppermute x6, waiting for transfers between devices, rotate(): lax.ppermute(array, 'tm_1', [(i, (i + steps) % GROUPS) for i in range(GRO...  30.5 us
    all_to_all x3, waiting for transfers between devices, exchange(): return lax.all_to_all(array, axis, split_axis=0, concat_axis=0, tiled=True)  29.2 us
    all_to_all x3, starting transfers between devices, exchange(): return lax.all_to_all(array, axis, split_axis=0, concat_axis=0, tiled=True)  25.9 us
    all_to_all x1, blocking collectives, exchange(): return lax.all_to_all(array, axis, split_axis=0, concat_axis=0, tiled=True)  18.6 us
    pallas_call x1, Pallas kernels, others(): pl.pallas_call(others_kernel, out_shape=[block, block, block, jax.ShapeDt...  16 us
    ppermute x6, starting transfers between devices, copies(): lax.ppermute(array, DP, [(i, i ^ k) for i in range(4)])  14.3 us
    ppermute x6, starting transfers between devices, rotate(): lax.ppermute(array, 'tm_1', [(i, (i + steps) % GROUPS) for i in range(GRO...  8.87 us
    ppermute x2, waiting for transfers between devices, to_previous(): lax.ppermute(array, TM, [(i + 1, i) for i in range(lax.axis_size(TM) - 1)])  7.32 us
  transfers between devices with their start and end apart: 22, of which 11 were waited for; matrix products, arithmetic and copies ran while one was open for 1% of the time, Pallas kernels for 11%

profile of v5, /device:TPU:1, one launch (start us, length us, event | category | flops | bytes accessed | tf_op | source)
XLA Modules:
  0.0 211.1 jit_solution(3029194362142985095)
XLA Ops:
  0.6 0.0 copy-start.7
  0.6 4.1 %tap_sums.1 = (bf16[288,1536]{1,0:T(8,128)(2,1)}, bf16[288,768]{1,0:T(8,128)(2,1)}, f32[32,1536]{1,0:T(8,128)}, f32[32,1536]{1,0:T(8,128)}, f32[32,1536]{1,0:T(8,128)}) custom-call(bf16[512,768]{1,0:T(8,128)(2,1)} %bitcast.16, bf16[768,2304]{1,0:T(8,128)(2,1)} %w_ref.5, f32[27,2,64]{2,1,0:T(2,128)} %bitcast.14), custom_call_target="tpu_custom_call" | custom-call | tf_op jit(solution)/shard_map/tap_sums/pallas_call | solution.py:95
  4.7 4.0 %collective-permute-start = (f32[32,1536]{1,0:T(8,128)}, f32[32,1536]{1,0:T(8,128)S(1)}, u32[]{:S(2)}, u32[]{:S(2)}) collective-permute-start(f32[32,1536]{1,0:T(8,128)} %get-tuple-element.38), channel_id=1, source_target_pairs={{0,1},{1,2},{2,3},{3,4},{4,5},{5,6},{6,7},{7,8},{8,9},{9,10},{10,1... | collective-permute-start | bytes 589832 | tf_op jit(solution)/shard_map/ppermute | solution.py:473
  8.8 1.3 collective-permute-start.1
  10.1 2.6 %collective-permute-done.low_ref = f32[32,1536]{1,0:T(8,128)S(1)} collective-permute-done((f32[32,1536]{1,0:T(8,128)}, f32[32,1536]{1,0:T(8,128)S(1)}, u32[]{:S(2)}, u32[]{:S(2)}) %collective-permute-start) | collective-permute-done | bytes 196640 | tf_op jit(solution)/shard_map/ppermute | solution.py:473
  12.6 3.7 %collective-permute-done.1.up_ref = f32[32,1536]{1,0:T(8,128)S(1)} collective-permute-done((f32[32,1536]{1,0:T(8,128)}, f32[32,1536]{1,0:T(8,128)S(1)}, u32[]{:S(2)}, u32[]{:S(2)}) %collective-permute-start.1) | collective-permute-done | bytes 196640 | tf_op jit(solution)/shard_map/ppermute | solution.py:477
  16.4 0.9 copy-done.5
  17.3 1.8 norm_side.1
  19.1 10.7 %all-to-all-start = ((bf16[32,32,384]{2,1,0:T(8,128)(2,1)}), bf16[32,32,384]{2,1,0:T(8,128)(2,1)S(1)}, u32[]{:S(2)}, u32[]{:S(2)}) async-start(bf16[32,32,384]{2,1,0:T(8,128)(2,1)} %bitcast.3), calls=%async_computation | async-start | bytes 1572864 | tf_op jit(solution)/shard_map/all_to_all | solution.py:469
  29.8 4.8 %query_side.1 = (bf16[512,384]{1,0:T(8,128)(2,1)}, bf16[512,384]{1,0:T(8,128)(2,1)}, bf16[512,384]{1,0:T(8,128)(2,1)}, bf16[512,384]{1,0:T(8,128)(2,1)}) custom-call(bf16[512,768]{1,0:T(8,128)(2,1)} %bitcast.17, bf16[768,2304]{1,0:T(8,128)(2,1)} %w_ref.5, bf16[512,768]{1,0:T(8,128)(2,1)} %bitcast.19, bf16[768,768]{1,0:T(8,128)(2,1)} %ow_ref.3), custom_call_target="tpu_custom_call" | custom-call | tf_op jit(solution)/shard_map/query_side/pallas_call | solution.py:137
  34.6 1.2 collective-permute-start.2
  35.9 2.4 %collective-permute-start.3 = (bf16[512,384]{1,0:T(8,128)(2,1)}, bf16[512,384]{1,0:T(8,128)(2,1)S(1)}, u32[]{:S(2)}, u32[]{:S(2)}) collective-permute-start(bf16[512,384]{1,0:T(8,128)(2,1)} %get-tuple-element.43), channel_id=1, source_target_pairs={{0,8},{4,12},{8,0},{12,4},{1,9},{5,13},{9,1},{13,5},{2,10},{6,14},... | collective-permute-start | bytes 1179656 | tf_op jit(solution)/shard_map/ppermute | solution.py:481
  38.3 1.2 collective-permute-start.4
  39.4 10.8 %collective-permute-done.2.q0_ref = bf16[512,384]{1,0:T(8,128)(2,1)S(1)} collective-permute-done((bf16[512,384]{1,0:T(8,128)(2,1)}, bf16[512,384]{1,0:T(8,128)(2,1)S(1)}, u32[]{:S(2)}, u32[]{:S(2)}) %collective-permute-start.2) | collective-permute-done | bytes 393248 | tf_op jit(solution)/shard_map/ppermute | solution.py:481
  50.3 6.4 %collective-permute-done.3.q1_ref = bf16[512,384]{1,0:T(8,128)(2,1)S(1)} collective-permute-done((bf16[512,384]{1,0:T(8,128)(2,1)}, bf16[512,384]{1,0:T(8,128)(2,1)S(1)}, u32[]{:S(2)}, u32[]{:S(2)}) %collective-permute-start.3) | collective-permute-done | bytes 393248 | tf_op jit(solution)/shard_map/ppermute | solution.py:481
  56.6 0.0 collective-permute-done.4.q2_ref
  56.7 0.0 all-to-all-done
  56.7 16.0 %attend_others.1 = (bf16[512,384]{1,0:T(8,128)(2,1)S(1)}, bf16[512,384]{1,0:T(8,128)(2,1)S(1)}, bf16[512,384]{1,0:T(8,128)(2,1)S(1)}, f32[384,1024]{1,0:T(8,128)S(1)}) custom-call(bf16[512,384]{1,0:T(8,128)(2,1)S(1)} %collective-permute-done.2.q0_ref, bf16[512,384]{1,0:T(8,128)(2,1)S(1)} %collective-permute-done.3.q1_ref, ...), custom_call_target="tpu_custom_call" | custom-call | tf_op jit(solution)/shard_map/attend_others/pallas_call | solution.py:237
  72.7 3.4 %collective-permute-start.5 = (bf16[512,384]{1,0:T(8,128)(2,1)S(1)}, bf16[512,384]{1,0:T(8,128)(2,1)S(1)}, u32[]{:S(2)}, u32[]{:S(2)}) collective-permute-start(bf16[512,384]{1,0:T(8,128)(2,1)S(1)} %get-tuple-element.47), channel_id=1, source_target_pairs={{0,12},{4,0},{8,4},{12,8},{1,13},{5,1},{9,5},{13,9},{2,14},{6,2},{... | collective-permute-start | bytes 1179656 | tf_op jit(solution)/shard_map/ppermute | solution.py:481
  76.1 0.0 collective-permute-start.6
  76.2 0.6 collective-permute-start.7
  76.8 5.8 %attend_own.1 = (bf16[512,384]{1,0:T(8,128)(2,1)S(1)}, bf16[1024,384]{1,0:T(8,128)(2,1)S(1)}) custom-call(bf16[512,384]{1,0:T(8,128)(2,1)S(1)} %copy-done.4, bf16[1024,384]{1,0:T(8,128)(2,1)S(1)} %bitcast.11, f32[384,1024]{1,0:T(8,128)S(1)} %get-tuple-element.45.start_ref), custom_call_target="tpu_custom_call" | custom-call | tf_op jit(solution)/shard_map/attend_own/pallas_call | solution.py:253
  82.6 0.0 copy-start.3
  82.6 0.7 copy-done.3
  83.3 9.1 %collective-permute-done.5.m1_ref = bf16[512,384]{1,0:T(8,128)(2,1)S(1)} collective-permute-done((bf16[512,384]{1,0:T(8,128)(2,1)S(1)}, bf16[512,384]{1,0:T(8,128)(2,1)S(1)}, u32[]{:S(2)}, u32[]{:S(2)}) %collective-permute-start.5) | collective-permute-done | bytes 393248 | tf_op jit(solution)/shard_map/ppermute | solution.py:481
  92.5 0.0 collective-permute-done.6.m2_ref
  92.5 4.1 %collective-permute-done.7.m3_ref = bf16[512,384]{1,0:T(8,128)(2,1)S(1)} collective-permute-done((bf16[512,384]{1,0:T(8,128)(2,1)S(1)}, bf16[512,384]{1,0:T(8,128)(2,1)S(1)}, u32[]{:S(2)}, u32[]{:S(2)}) %collective-permute-start.7) | collective-permute-done | bytes 393248 | tf_op jit(solution)/shard_map/ppermute | solution.py:481
  96.6 0.7 copy-done.11
  97.3 6.3 %output_side.1 = (bf16[512,768]{1,0:T(8,128)(2,1)}, bf16[512,768]{1,0:T(8,128)(2,1)}, bf16[32,24,768]{2,1,0:T(8,128)(2,1)}, bf16[32,24,768]{2,1,0:T(8,128)(2,1)}) custom-call(bf16[512,384]{1,0:T(8,128)(2,1)} %copy-done.3, bf16[512,384]{1,0:T(8,128)(2,1)} %copy-done.9, bf16[512,384]{1,0:T(8,128)(2,1)} %copy-done.10, bf16[512,384]{1,0:T(8,128)(2,1)} %copy-done.11, ...), custom_call_target="tpu_custom_call" | custom-call | tf_op jit(solution)/shard_map/output_side/pallas_call | solution.py:387
  103.6 0.7 collective-permute-start.10
  104.4 18.6 %all_to_all.20 = bf16[32,32,384]{2,1,0:T(8,128)(2,1)S(1)} all-to-all(bf16[32,32,384]{2,1,0:T(8,128)(2,1)S(1)} %bitcast.13), channel_id=1, replica_groups=mesh['dp_0'=2,'dp_1'=2,'tm_0'=2,'tm_1'=4,'tm_2'=4] {'tm_0','tm_1','tm_2'}, dimensions={0} | all-to-all | bytes 1572864 | tf_op jit(solution)/shard_map/all_to_all | solution.py:469
  122.9 0.6 norm_back.1
  123.5 3.1 %collective-permute-start.9 = (f32[32,1536]{1,0:T(8,128)S(1)}, f32[32,1536]{1,0:T(8,128)S(1)}, u32[]{:S(2)}, u32[]{:S(2)}) collective-permute-start(f32[32,1536]{1,0:T(8,128)S(1)} %get-tuple-element.55.own_ref), channel_id=1, source_target_pairs={{0,1},{1,2},{2,3},{3,4},{4,5},{5,6},{6,7},{7,8},{8,9},{9,10},{10,1... | collective-permute-start | bytes 589832 | tf_op jit(solution)/shard_map/ppermute | solution.py:473
  126.6 1.3 collective-permute-start.8
  127.9 1.5 collective-permute-done.9.low_ref
  129.5 3.6 %collective-permute-done.8.up_ref = f32[32,1536]{1,0:T(8,128)S(1)} collective-permute-done((f32[32,1536]{1,0:T(8,128)S(1)}, f32[32,1536]{1,0:T(8,128)S(1)}, u32[]{:S(2)}, u32[]{:S(2)}) %collective-permute-start.8) | collective-permute-done | bytes 196640 | tf_op jit(solution)/shard_map/ppermute | solution.py:477
  133.1 2.8 %pool_back.1 = (bf16[2,288,768]{2,1,0:T(8,128)(2,1)S(1)}, bf16[32,24,768]{2,1,0:T(8,128)(2,1)}, f32[24,256]{1,0:T(8,128)S(1)}) custom-call(f32[32,1536]{1,0:T(8,128)S(1)} %collective-permute-done.8.up_ref, f32[32,1536]{1,0:T(8,128)S(1)} %get-tuple-element.55.own_ref, f32[32,1536]{1,0:T(8,128)S(1)} %collective-permute-done.9.low_ref, ...), custom_call_target="tpu_custom_call" | custom-call | tf_op jit(solution)/shard_map/pool_back/pallas_call | solution.py:331
  135.8 2.8 %collective-permute-start.14 = (bf16[32,24,768]{2,1,0:T(8,128)(2,1)}, bf16[32,24,768]{2,1,0:T(8,128)(2,1)}, u32[]{:S(2)}, u32[]{:S(2)}) collective-permute-start(bf16[32,24,768]{2,1,0:T(8,128)(2,1)} %get-tuple-element.62), channel_id=1, source_target_pairs={{0,32},{32,0},{1,33},{33,1},{2,34},{34,2},{3,35},{35,3},{4,36},{36... | collective-permute-start | bytes 3538952 | tf_op jit(solution)/shard_map/ppermute | solution.py:485
  138.7 0.0 collective-permute-done.10
  138.7 1.4 add_convert_fusion
  140.0 10.6 %all-to-all-start.2 = ((bf16[32,24,768]{2,1,0:T(8,128)(2,1)}), bf16[32,24,768]{2,1,0:T(8,128)(2,1)S(1)}, u32[]{:S(2)}, u32[]{:S(2)}) async-start(bf16[32,24,768]{2,1,0:T(8,128)(2,1)} %add_convert_fusion), calls=%async_computation.2 | async-start | bytes 2359296 | tf_op jit(solution)/shard_map/all_to_all | solution.py:469
  150.7 0.6 collective-permute-start.15
  151.3 0.9 collective-permute-done.15.other_small_ref
  152.2 0.0 collective-permute-done.14.other_ref
  152.2 3.3 %pay_b_rows.1 = bf16[32,24,1024]{2,1,0:T(8,128)(2,1)} custom-call(bf16[288,768]{1,0:T(8,128)(2,1)S(1)} %copy-done.1, bf16[2,288,768]{2,1,0:T(8,128)(2,1)S(1)} %get-tuple-element.59.dv_ref, bf16[32,24,768]{2,1,0:T(8,128)(2,1)} %collective-permute-done.14.other_ref, f32[24,256]{1,0:T(8,128)S(1)} %get-tuple-element.63.small_ref, ...), custom_call_target="tpu_custom_call" | custom-call | tf_op jit(solution)/shard_map/pay_b_rows/pallas_call | solution.py:356
  155.5 13.1 %all-to-all-done.2.parts_ref = bf16[32,24,768]{2,1,0:T(8,128)(2,1)S(1)} async-done(((bf16[32,24,768]{2,1,0:T(8,128)(2,1)}), bf16[32,24,768]{2,1,0:T(8,128)(2,1)S(1)}, u32[]{:S(2)}, u32[]{:S(2)}) %all-to-all-start.2) | async-done | bytes 1179680 | tf_op jit(solution)/shard_map/all_to_all | solution.py:469
  168.6 4.6 %all-to-all-start.3 = ((bf16[32,24,1024]{2,1,0:T(8,128)(2,1)}), bf16[32,24,1024]{2,1,0:T(8,128)(2,1)S(1)}, u32[]{:S(2)}, u32[]{:S(2)}) async-start(bf16[32,24,1024]{2,1,0:T(8,128)(2,1)} %pay_b_rows.1), calls=%async_computation.3 | async-start | bytes 3145728 | tf_op jit(solution)/shard_map/all_to_all | solution.py:469
  173.2 0.2 fold.2.refs_0_
  173.4 4.6 %collective-permute-start.13 = (f32[24,768]{1,0:T(8,128)S(1)}, f32[24,768]{1,0:T(8,128)S(1)}, u32[]{:S(2)}, u32[]{:S(2)}) collective-permute-start(f32[24,768]{1,0:T(8,128)S(1)} %fold.2.refs_0_), channel_id=1, source_target_pairs={{0,96},{32,64},{64,32},{96,0},{1,97},{33,65},{65,33},{97,1},{2,98}... | collective-permute-start | bytes 221192 | tf_op jit(solution)/shard_map/ppermute | solution.py:493
  177.9 16.0 %all-to-all-done.3.parts_ref = bf16[32,24,1024]{2,1,0:T(8,128)(2,1)S(1)} async-done(((bf16[32,24,1024]{2,1,0:T(8,128)(2,1)}), bf16[32,24,1024]{2,1,0:T(8,128)(2,1)S(1)}, u32[]{:S(2)}, u32[]{:S(2)}) %all-to-all-start.3) | async-done | bytes 1572896 | tf_op jit(solution)/shard_map/all_to_all | solution.py:469
  194.0 0.2 fold.3.refs_4_
  194.2 5.9 %collective-permute-start.18 = (f32[24,1024]{1,0:T(8,128)S(1)}, f32[24,1024]{1,0:T(8,128)S(1)}, u32[]{:S(2)}, u32[]{:S(2)}) collective-permute-start(f32[24,1024]{1,0:T(8,128)S(1)} %fold.3.refs_4_), channel_id=1, source_target_pairs={{0,96},{32,64},{64,32},{96,0},{1,97},{33,65},{65,33},{97,1},{2,98}... | collective-permute-start | bytes 294920 | tf_op jit(solution)/shard_map/ppermute | solution.py:493
  200.1 0.0 collective-permute-start.17
  200.1 0.5 collective-permute-start.16
  200.6 2.5 %collective-permute-start.12 = (f32[24,768]{1,0:T(8,128)S(1)}, f32[24,768]{1,0:T(8,128)S(1)}, u32[]{:S(2)}, u32[]{:S(2)}) collective-permute-start(f32[24,768]{1,0:T(8,128)S(1)} %fold.2.refs_0_), channel_id=1, source_target_pairs={{0,64},{32,96},{64,0},{96,32},{1,65},{33,97},{65,1},{97,33},{2,66}... | collective-permute-start | bytes 221192 | tf_op jit(solution)/shard_map/ppermute | solution.py:493
  203.1 0.0 collective-permute-done.13.refs_3_
  203.1 0.8 collective-permute-start.11
  203.9 6.3 %token_grad.1 = bf16[512,768]{1,0:T(8,128)(2,1)} custom-call(bf16[512,768]{1,0:T(8,128)(2,1)} %get-tuple-element.51.dq_ref, bf16[2,288,768]{2,1,0:T(8,128)(2,1)} %copy-done, bf16[768,2304]{1,0:T(8,128)(2,1)} %w_ref.5), custom_call_target="tpu_custom_call" | custom-call | tf_op jit(solution)/shard_map/token_grad/pallas_call | solution.py:409
  210.2 0.0 collective-permute-done.12.refs_2_
  210.2 0.0 collective-permute-done.11.refs_1_
  210.2 0.0 collective-permute-done.18.refs_7_
  210.3 0.0 collective-permute-done.17.refs_6_
  210.3 0.0 collective-permute-done.16.refs_5_
  210.3 0.8 finish.1
  (19 shorter events, 0.0 us)
Async XLA Ops:
  0.6 15.8 %copy-start.7 = (f32[2,64]{1,0:T(2,128)S(1)}, f32[2,64]{1,0:T(2,128)}, u32[]{:S(2)}) copy-start(f32[2,64]{1,0:T(2,128)} %gain_ref.3) | copy-start | bytes 1540
  4.7 7.9 %collective-permute-start = (f32[32,1536]{1,0:T(8,128)}, f32[32,1536]{1,0:T(8,128)S(1)}, u32[]{:S(2)}, u32[]{:S(2)}) collective-permute-start(f32[32,1536]{1,0:T(8,128)} %get-tuple-element.38), channel_id=1, source_target_pairs={{0,1},{1,2},{2,3},{3,4},{4,5},{5,6},{6,7},{7,8},{8,9},{9,10},{10,1... | collective-permute-start | bytes 589832 | tf_op jit(solution)/shard_map/ppermute | solution.py:473
  8.8 7.6 %collective-permute-start.1 = (f32[32,1536]{1,0:T(8,128)}, f32[32,1536]{1,0:T(8,128)S(1)}, u32[]{:S(2)}, u32[]{:S(2)}) collective-permute-start(f32[32,1536]{1,0:T(8,128)} %get-tuple-element.40), channel_id=1, source_target_pairs={{1,0},{2,1},{3,2},{4,3},{5,4},{6,5},{7,6},{8,7},{9,8},{10,9},{11,1... | collective-permute-start | bytes 589832 | tf_op jit(solution)/shard_map/ppermute | solution.py:477
  16.4 0.9 copy-start.5
  19.1 37.6 %all-to-all-start = ((bf16[32,32,384]{2,1,0:T(8,128)(2,1)}), bf16[32,32,384]{2,1,0:T(8,128)(2,1)S(1)}, u32[]{:S(2)}, u32[]{:S(2)}) async-start(bf16[32,32,384]{2,1,0:T(8,128)(2,1)} %bitcast.3), calls=%async_computation | async-start | bytes 1572864 | tf_op jit(solution)/shard_map/all_to_all | solution.py:469
  34.6 42.2 %copy-start.4 = (bf16[512,384]{1,0:T(8,128)(2,1)S(1)}, bf16[512,384]{1,0:T(8,128)(2,1)}, u32[]{:S(2)}) copy-start(bf16[512,384]{1,0:T(8,128)(2,1)} %get-tuple-element.37.qd_ref) | copy-start | bytes 1179652
  34.6 15.6 %collective-permute-start.2 = (bf16[512,384]{1,0:T(8,128)(2,1)}, bf16[512,384]{1,0:T(8,128)(2,1)S(1)}, u32[]{:S(2)}, u32[]{:S(2)}) collective-permute-start(bf16[512,384]{1,0:T(8,128)(2,1)} %get-tuple-element.42), channel_id=1, source_target_pairs={{0,4},{4,8},{8,12},{12,0},{1,5},{5,9},{9,13},{13,1},{2,6},{6,10},{... | collective-permute-start | bytes 1179656 | tf_op jit(solution)/shard_map/ppermute | solution.py:481
  35.9 20.8 %collective-permute-start.3 = (bf16[512,384]{1,0:T(8,128)(2,1)}, bf16[512,384]{1,0:T(8,128)(2,1)S(1)}, u32[]{:S(2)}, u32[]{:S(2)}) collective-permute-start(bf16[512,384]{1,0:T(8,128)(2,1)} %get-tuple-element.43), channel_id=1, source_target_pairs={{0,8},{4,12},{8,0},{12,4},{1,9},{5,13},{9,1},{13,5},{2,10},{6,14},... | collective-permute-start | bytes 1179656 | tf_op jit(solution)/shard_map/ppermute | solution.py:481
  38.3 18.4 %collective-permute-start.4 = (bf16[512,384]{1,0:T(8,128)(2,1)}, bf16[512,384]{1,0:T(8,128)(2,1)S(1)}, u32[]{:S(2)}, u32[]{:S(2)}) collective-permute-start(bf16[512,384]{1,0:T(8,128)(2,1)} %get-tuple-element.44), channel_id=1, source_target_pairs={{0,12},{4,0},{8,4},{12,8},{1,13},{5,1},{9,5},{13,9},{2,14},{6,2},{... | collective-permute-start | bytes 1179656 | tf_op jit(solution)/shard_map/ppermute | solution.py:481
  72.7 19.7 %collective-permute-start.5 = (bf16[512,384]{1,0:T(8,128)(2,1)S(1)}, bf16[512,384]{1,0:T(8,128)(2,1)S(1)}, u32[]{:S(2)}, u32[]{:S(2)}) collective-permute-start(bf16[512,384]{1,0:T(8,128)(2,1)S(1)} %get-tuple-element.47), channel_id=1, source_target_pairs={{0,12},{4,0},{8,4},{12,8},{1,13},{5,1},{9,5},{13,9},{2,14},{6,2},{... | collective-permute-start | bytes 1179656 | tf_op jit(solution)/shard_map/ppermute | solution.py:481
  76.1 16.3 %collective-permute-start.6 = (bf16[512,384]{1,0:T(8,128)(2,1)S(1)}, bf16[512,384]{1,0:T(8,128)(2,1)S(1)}, u32[]{:S(2)}, u32[]{:S(2)}) collective-permute-start(bf16[512,384]{1,0:T(8,128)(2,1)S(1)} %get-tuple-element.48), channel_id=1, source_target_pairs={{0,8},{4,12},{8,0},{12,4},{1,9},{5,13},{9,1},{13,5},{2,10},{6,14},... | collective-permute-start | bytes 1179656 | tf_op jit(solution)/shard_map/ppermute | solution.py:481
  76.2 20.4 %collective-permute-start.7 = (bf16[512,384]{1,0:T(8,128)(2,1)S(1)}, bf16[512,384]{1,0:T(8,128)(2,1)S(1)}, u32[]{:S(2)}, u32[]{:S(2)}) collective-permute-start(bf16[512,384]{1,0:T(8,128)(2,1)S(1)} %get-tuple-element.49), channel_id=1, source_target_pairs={{0,4},{4,8},{8,12},{12,0},{1,5},{5,9},{9,13},{13,1},{2,6},{6,10},{... | collective-permute-start | bytes 1179656 | tf_op jit(solution)/shard_map/ppermute | solution.py:481
  82.6 0.7 copy-start.3
  92.5 4.1 %copy-start.9 = (bf16[512,384]{1,0:T(8,128)(2,1)}, bf16[512,384]{1,0:T(8,128)(2,1)S(1)}, u32[]{:S(2)}) copy-start(bf16[512,384]{1,0:T(8,128)(2,1)S(1)} %collective-permute-done.5.m1_ref) | copy-start | bytes 1179652
  92.5 4.1 %copy-start.10 = (bf16[512,384]{1,0:T(8,128)(2,1)}, bf16[512,384]{1,0:T(8,128)(2,1)S(1)}, u32[]{:S(2)}) copy-start(bf16[512,384]{1,0:T(8,128)(2,1)S(1)} %collective-permute-done.6.m2_ref) | copy-start | bytes 1179652
  96.6 0.8 copy-start.11
  103.6 35.0 %collective-permute-start.10 = (bf16[32,24,768]{2,1,0:T(8,128)(2,1)}, bf16[32,24,768]{2,1,0:T(8,128)(2,1)S(1)}, u32[]{:S(2)}, u32[]{:S(2)}) collective-permute-start(bf16[32,24,768]{2,1,0:T(8,128)(2,1)} %get-tuple-element.61), channel_id=1, source_target_pairs={{0,32},{32,0},{1,33},{33,1},{2,34},{34,2},{3,35},{35,3},{4,36},{36... | collective-permute-start | bytes 3538952 | tf_op jit(solution)/shard_map/ppermute | solution.py:485
  104.3 28.7 %copy-start.1 = (bf16[288,768]{1,0:T(8,128)(2,1)S(1)}, bf16[288,768]{1,0:T(8,128)(2,1)}, u32[]{:S(2)}) copy-start(bf16[288,768]{1,0:T(8,128)(2,1)} %get-tuple-element.57.tt_ref) | copy-start | bytes 1327108
  104.3 28.7 %copy-start.2 = (bf16[288,1536]{1,0:T(8,128)(2,1)S(1)}, bf16[288,1536]{1,0:T(8,128)(2,1)}, u32[]{:S(2)}) copy-start(bf16[288,1536]{1,0:T(8,128)(2,1)} %get-tuple-element.56.taps_ref) | copy-start | bytes 2654212
  104.4 28.7 %copy-start.6 = (f32[2,27,64]{2,0,1:T(2,128)S(1)}, f32[2,27,64]{2,0,1:T(2,128)}, u32[]{:S(2)}) copy-start(f32[2,27,64]{2,0,1:T(2,128)} %param.8) | copy-start | bytes 41476
  123.5 15.1 %copy-start.8 = (bf16[32,24,768]{2,1,0:T(8,128)(2,1)S(1)}, bf16[32,24,768]{2,1,0:T(8,128)(2,1)}, u32[]{:S(2)}) copy-start(bf16[32,24,768]{2,1,0:T(8,128)(2,1)} %get-tuple-element.60) | copy-start | bytes 3538948
  123.5 5.9 %collective-permute-start.9 = (f32[32,1536]{1,0:T(8,128)S(1)}, f32[32,1536]{1,0:T(8,128)S(1)}, u32[]{:S(2)}, u32[]{:S(2)}) collective-permute-start(f32[32,1536]{1,0:T(8,128)S(1)} %get-tuple-element.55.own_ref), channel_id=1, source_target_pairs={{0,1},{1,2},{2,3},{3,4},{4,5},{5,6},{6,7},{7,8},{8,9},{9,10},{10,1... | collective-permute-start | bytes 589832 | tf_op jit(solution)/shard_map/ppermute | solution.py:473
  126.6 6.4 %collective-permute-start.8 = (f32[32,1536]{1,0:T(8,128)S(1)}, f32[32,1536]{1,0:T(8,128)S(1)}, u32[]{:S(2)}, u32[]{:S(2)}) collective-permute-start(f32[32,1536]{1,0:T(8,128)S(1)} %get-tuple-element.55.own_ref), channel_id=1, source_target_pairs={{1,0},{2,1},{3,2},{4,3},{5,4},{6,5},{7,6},{8,7},{9,8},{10,9},{11,1... | collective-permute-start | bytes 589832 | tf_op jit(solution)/shard_map/ppermute | solution.py:477
  135.8 16.3 %copy-start = (bf16[2,288,768]{2,1,0:T(8,128)(2,1)}, bf16[2,288,768]{2,1,0:T(8,128)(2,1)S(1)}, u32[]{:S(2)}) copy-start(bf16[2,288,768]{2,1,0:T(8,128)(2,1)S(1)} %get-tuple-element.59.dv_ref) | copy-start | bytes 2654212
  135.8 16.3 %collective-permute-start.14 = (bf16[32,24,768]{2,1,0:T(8,128)(2,1)}, bf16[32,24,768]{2,1,0:T(8,128)(2,1)}, u32[]{:S(2)}, u32[]{:S(2)}) collective-permute-start(bf16[32,24,768]{2,1,0:T(8,128)(2,1)} %get-tuple-element.62), channel_id=1, source_target_pairs={{0,32},{32,0},{1,33},{33,1},{2,34},{34,2},{3,35},{35,3},{4,36},{36... | collective-permute-start | bytes 3538952 | tf_op jit(solution)/shard_map/ppermute | solution.py:485
  140.0 28.6 %all-to-all-start.2 = ((bf16[32,24,768]{2,1,0:T(8,128)(2,1)}), bf16[32,24,768]{2,1,0:T(8,128)(2,1)S(1)}, u32[]{:S(2)}, u32[]{:S(2)}) async-start(bf16[32,24,768]{2,1,0:T(8,128)(2,1)} %add_convert_fusion), calls=%async_computation.2 | async-start | bytes 2359296 | tf_op jit(solution)/shard_map/all_to_all | solution.py:469
  150.7 1.5 collective-permute-start.15
  168.6 25.4 %all-to-all-start.3 = ((bf16[32,24,1024]{2,1,0:T(8,128)(2,1)}), bf16[32,24,1024]{2,1,0:T(8,128)(2,1)S(1)}, u32[]{:S(2)}, u32[]{:S(2)}) async-start(bf16[32,24,1024]{2,1,0:T(8,128)(2,1)} %pay_b_rows.1), calls=%async_computation.3 | async-start | bytes 3145728 | tf_op jit(solution)/shard_map/all_to_all | solution.py:469
  173.4 29.8 %collective-permute-start.13 = (f32[24,768]{1,0:T(8,128)S(1)}, f32[24,768]{1,0:T(8,128)S(1)}, u32[]{:S(2)}, u32[]{:S(2)}) collective-permute-start(f32[24,768]{1,0:T(8,128)S(1)} %fold.2.refs_0_), channel_id=1, source_target_pairs={{0,96},{32,64},{64,32},{96,0},{1,97},{33,65},{65,33},{97,1},{2,98}... | collective-permute-start | bytes 221192 | tf_op jit(solution)/shard_map/ppermute | solution.py:493
  194.2 16.1 %collective-permute-start.18 = (f32[24,1024]{1,0:T(8,128)S(1)}, f32[24,1024]{1,0:T(8,128)S(1)}, u32[]{:S(2)}, u32[]{:S(2)}) collective-permute-start(f32[24,1024]{1,0:T(8,128)S(1)} %fold.3.refs_4_), channel_id=1, source_target_pairs={{0,96},{32,64},{64,32},{96,0},{1,97},{33,65},{65,33},{97,1},{2,98}... | collective-permute-start | bytes 294920 | tf_op jit(solution)/shard_map/ppermute | solution.py:493
  200.1 10.1 %collective-permute-start.17 = (f32[24,1024]{1,0:T(8,128)S(1)}, f32[24,1024]{1,0:T(8,128)S(1)}, u32[]{:S(2)}, u32[]{:S(2)}) collective-permute-start(f32[24,1024]{1,0:T(8,128)S(1)} %fold.3.refs_4_), channel_id=1, source_target_pairs={{0,64},{32,96},{64,0},{96,32},{1,65},{33,97},{65,1},{97,33},{2,66}... | collective-permute-start | bytes 294920 | tf_op jit(solution)/shard_map/ppermute | solution.py:493
  200.1 10.1 %collective-permute-start.16 = (f32[24,1024]{1,0:T(8,128)S(1)}, f32[24,1024]{1,0:T(8,128)S(1)}, u32[]{:S(2)}, u32[]{:S(2)}) collective-permute-start(f32[24,1024]{1,0:T(8,128)S(1)} %fold.3.refs_4_), channel_id=1, source_target_pairs={{0,32},{32,0},{64,96},{96,64},{1,33},{33,1},{65,97},{97,65},{2,34}... | collective-permute-start | bytes 294920 | tf_op jit(solution)/shard_map/ppermute | solution.py:493
  200.6 9.6 %collective-permute-start.12 = (f32[24,768]{1,0:T(8,128)S(1)}, f32[24,768]{1,0:T(8,128)S(1)}, u32[]{:S(2)}, u32[]{:S(2)}) collective-permute-start(f32[24,768]{1,0:T(8,128)S(1)} %fold.2.refs_0_), channel_id=1, source_target_pairs={{0,64},{32,96},{64,0},{96,32},{1,65},{33,97},{65,1},{97,33},{2,66}... | collective-permute-start | bytes 221192 | tf_op jit(solution)/shard_map/ppermute | solution.py:493
  203.1 7.1 %collective-permute-start.11 = (f32[24,768]{1,0:T(8,128)S(1)}, f32[24,768]{1,0:T(8,128)S(1)}, u32[]{:S(2)}, u32[]{:S(2)}) collective-permute-start(f32[24,768]{1,0:T(8,128)S(1)} %fold.2.refs_0_), channel_id=1, source_target_pairs={{0,32},{32,0},{64,96},{96,64},{1,33},{33,1},{65,97},{97,65},{2,34}... | collective-permute-start | bytes 221192 | tf_op jit(solution)/shard_map/ppermute | solution.py:493
